TPU v7x, 128 devices: a whole 4x4x4 slice. The times are simulated.
128 devices in a mesh: row: 8 (over z, core), col: 16 (over y, x).
Axes of the slice: x: 4, y: 4, z: 4, core: 2. Of those that a mesh axis runs over, the one named last changes fastest.
Arguments:
- right_side: float32 [8, 65536], P(None, ('row', 'col')), may hold values from -30 to 30
- u_factors: bfloat16 [128, 128, 48, 512], P(('row', 'col')), may hold values from -0.078125 to 0.078125
- v_factors: bfloat16 [128, 128, 48, 512], P('row', 'col'), may hold values from -0.25 to 0.25
- ranks: int32 [128, 128], P('row', 'col'), may hold values from 8 to 48
- far_blocks: bfloat16 [16, 512, 65536], P('row', None, 'col'), may hold values from -0.09375 to 0.09375
- block_target: int32 [16, 16], replicated, may hold values from 0 to 127, as said below
- recv_order: int32 [128], replicated, may hold values from 0 to 127, as said below
Outputs:
- densities: float32 [8, 65536], P(None, 'col')
- residual: float32 [8, 65536], P(None, ('row', 'col'))
- far_field: float32 [128, 4096], P(('row', 'col'))
Inputs may be any that keep to these rules, and one draw needn't show every extreme that they name: `recv_order`: a permutation of the receiver patches. `block_target`: block (b, c) with b % 2 == 0 lies on device g = (b // 2) * 16 + c; its receiver patch is stored in output rows owned by device (g + 128 / 2) mod 128 if g is even and by device g - 1 if g is odd; the other blocks may name any receiver patch.
All inputs are finite; a program needn't handle non-finite values.
Results may differ from a plain program's by a relative error of at most 0.008.
Values may be sent and summed in bfloat16 or wider, within the bound.
No kernel may reach another device: no remote copies, remote signals or barrier semaphores. Data moves between devices by JAX's collectives and lax.ppermute only.
A program may use at most 128 MiB of HBM per device.

v0:
```python
import jax
import jax.numpy as jnp
from jax import lax
from jax.sharding import PartitionSpec as P

ITERS = 2


def per_device(right_side, u_factors, v_factors, ranks, far_blocks, block_target, recv_order):
    dens_count = right_side.shape[0]
    own_rows = u_factors.shape[0]
    all_cols = u_factors.shape[1]
    slot_count = u_factors.shape[2]
    patch_len = u_factors.shape[3]
    group_rows = v_factors.shape[0]
    own_cols = v_factors.shape[1]
    slot_index = lax.broadcasted_iota(jnp.int32, (group_rows, own_cols, slot_count, 1), 2)
    kept = (slot_index < ranks[:, :, None, None]).astype(jnp.float32)
    kept_half = kept.astype(jnp.bfloat16)
    residual = right_side
    densities = jnp.zeros((dens_count, own_cols * patch_len), jnp.float32)
    for iteration in range(ITERS):
        res_bf = residual.astype(jnp.bfloat16).reshape(dens_count, own_rows, patch_len)
        back_coef = jnp.einsum(
            "ijsp,dip->ijsd", u_factors, res_bf, preferred_element_type=jnp.float32
        )
        back_coef = back_coef.astype(jnp.bfloat16).reshape(
            own_rows, all_cols, slot_count * dens_count
        )
        arrived = lax.all_to_all(back_coef, "col", split_axis=1, concat_axis=0, tiled=True)
        arrived = arrived.reshape(group_rows, own_cols, slot_count, dens_count) * kept_half
        partial_grad = jnp.einsum(
            "ijsp,ijsd->djp", v_factors, arrived, preferred_element_type=jnp.float32
        )
        grad = lax.psum(partial_grad.reshape(dens_count, own_cols * patch_len), "row")
        grad_local = jnp.sum(grad * grad, axis=1)
        grad_sq = lax.psum(grad_local, "col")
        grad_bf = grad.astype(jnp.bfloat16).reshape(dens_count, own_cols, patch_len)
        coefficients = (
            jnp.einsum("ijsp,djp->ijsd", v_factors, grad_bf, preferred_element_type=jnp.float32)
            * kept
        )
        coefficients = coefficients.astype(jnp.bfloat16).reshape(
            group_rows, own_cols, slot_count * dens_count
        )
        landed = lax.all_to_all(coefficients, "col", split_axis=0, concat_axis=1, tiled=True)
        landed = landed.reshape(own_rows, all_cols, slot_count, dens_count)
        image = jnp.einsum("ijsp,ijsd->dip", u_factors, landed, preferred_element_type=jnp.float32)
        image = image.reshape(dens_count, own_rows * patch_len)
        image_local = jnp.sum(image * image, axis=1)
        image_sq = lax.psum(image_local, ("row", "col"))
        step_size = grad_sq / (image_sq + 1e-06)
        densities = densities + step_size[:, None] * grad
        residual = residual - step_size[:, None] * image
    block_count = far_blocks.shape[0]
    x_half = densities.astype(jnp.bfloat16)
    block_field = jnp.einsum("bpn,dn->bdp", far_blocks, x_half, preferred_element_type=jnp.float32)
    block_field = block_field.reshape(block_count, dens_count * patch_len)
    local_target = lax.dynamic_slice(
        block_target, (lax.axis_index("row") * block_count, lax.axis_index("col")), (block_count, 1)
    ).reshape(block_count)
    onehot = (local_target[:, None] == recv_order[None, :]).astype(jnp.float32)
    far_field = lax.psum_scatter(
        jnp.dot(
            onehot.T,
            block_field,
            preferred_element_type=jnp.float32,
            precision=lax.Precision.HIGHEST,
        ),
        ("row", "col"),
        scatter_dimension=0,
        tiled=True,
    )
    return (densities, residual, far_field)


def solution(mesh):
    return jax.shard_map(
        per_device,
        mesh=mesh,
        in_specs=(
            P(None, ("row", "col")),
            P(("row", "col"), None, None, None),
            P("row", "col", None, None),
            P("row", "col"),
            P("row", None, "col"),
            P(),
            P(),
        ),
        out_specs=(P(None, "col"), P(None, ("row", "col")), P(("row", "col"), None)),
        check_vma=False,
    )
```

profile of v0, /device:TPU:1, one launch (start us, length us, event | category | flops | bytes accessed | tf_op | source)
XLA Modules:
  0.0 595.4 jit_solution(9957855549774173676)
XLA Ops:
  7.2 5.9 convolution_convert_fusion
  15.9 7.6 %all-to-all-start = ((bf16[16,2,1536]{2,1,0:T(2,128)(2,1)}), bf16[16,2,1536]{2,1,0:T(2,128)(2,1)S(1)}, u32[]{:S(2)}, u32[]{:S(2)}) async-start(bf16[16,2,1536]{2,1,0:T(2,128)(2,1)} %reshape.129), calls=%async_computation | async-start | bytes 196608 | tf_op jit(solution)/shard_map/all_to_all | solution.py:30
  23.7 6.6 %all-to-all-done = bf16[16,2,1536]{2,1,0:T(2,128)(2,1)S(1)} async-done(((bf16[16,2,1536]{2,1,0:T(2,128)(2,1)}), bf16[16,2,1536]{2,1,0:T(2,128)(2,1)S(1)}, u32[]{:S(2)}, u32[]{:S(2)}) %all-to-all-start) | async-done | bytes 98336 | tf_op jit(solution)/shard_map/all_to_all | solution.py:30
  32.6 4.8 fusion.8
  37.4 58.2 %all-reduce.5.cloned.1.call-done = f32[8,4096]{1,0:T(8,128)} async-done(((f32[8,4096]{1,0:T(8,128)}), f32[8,4096]{1,0:T(8,128)}) %all-reduce.5.cloned.1.call-update) | async-done | bytes 131088 | tf_op jit(solution)/shard_map/psum | solution.py:35
  96.7 5.9 fusion.22
  104.1 6.5 %all-to-all-start.1 = ((bf16[16,8,384]{2,1,0:T(8,128)(2,1)}), bf16[16,8,384]{2,1,0:T(8,128)(2,1)S(1)}, u32[]{:S(2)}, u32[]{:S(2)}) async-start(bf16[16,8,384]{2,1,0:T(8,128)(2,1)} %copy.56), calls=%async_computation.1 | async-start | bytes 196608 | tf_op jit(solution)/shard_map/all_to_all | solution.py:46
  110.6 33.3 %psum.43 = f32[8]{0:T(128)S(1)} all-reduce(f32[8]{0:T(128)S(1)} %get-tuple-element.5), channel_id=1, replica_groups=mesh['row'=8,'col'=16] {'col'}, use_global_device_ids=true, to_apply=%region_2.0 | all-reduce | flops 8 | bytes 64 | tf_op jit(solution)/shard_map/psum | solution.py:37
  144.0 1.8 reshape.109
  145.8 3.8 multiply_reduce_fusion.3
  149.6 72.1 %psum.44 = f32[8]{0:T(128)S(1)} all-reduce(f32[8]{0:T(128)S(1)} %get-tuple-element.9), channel_id=1, replica_groups=mesh['row'=8,'col'=16] {'row','col'}, use_global_device_ids=true, to_apply=%region_4.0 | all-reduce | flops 8 | bytes 64 | tf_op jit(solution)/shard_map/psum | solution.py:51
  221.7 9.4 %fusion.31 = bf16[1,128,384]{1,2,0:T(8,128)(2,1)S(1)} fusion(bf16[128,48,512]{2,1,0:T(8,128)(2,1)} %bitcast.81, f32[8,512]{1,0:T(8,128)S(1)} %copy-done.4, f32[8,512]{1,0:T(8,128)S(1)} %get-tuple-element.10, f32[8]{0:T(128)S(1)} %add_divide_fusion.1), kind=kOutput, calls=%fused_computation.18 | convolution fusion | flops 50393088 | bytes 6422560 | tf_op jit(solution)/shard_map/ijsp,dip->ijsd/dot_general | solution.py:24
  232.6 10.2 %all_to_all.16 = bf16[16,2,1536]{2,1,0:T(2,128)(2,1)S(1)} all-to-all(bf16[16,2,1536]{2,1,0:T(2,128)(2,1)S(1)} %reshape.131), channel_id=1, replica_groups=mesh['row'=8,'col'=16] {'col'}, dimensions={0} | all-to-all | bytes 196608 | tf_op jit(solution)/shard_map/all_to_all | solution.py:30
  245.2 4.8 fusion.6
  250.1 55.2 %all-reduce.7.cloned.1.call-done = f32[8,4096]{1,0:T(8,128)} async-done(((f32[8,4096]{1,0:T(8,128)}), f32[8,4096]{1,0:T(8,128)}) %all-reduce.7.cloned.1.call-update) | async-done | bytes 131088 | tf_op jit(solution)/shard_map/psum | solution.py:35
  306.4 5.9 fusion.25
  313.7 6.5 %all-to-all-start.3 = ((bf16[16,8,384]{2,1,0:T(8,128)(2,1)}), bf16[16,8,384]{2,1,0:T(8,128)(2,1)S(1)}, u32[]{:S(2)}, u32[]{:S(2)}) async-start(bf16[16,8,384]{2,1,0:T(8,128)(2,1)} %copy.63), calls=%async_computation.3 | async-start | bytes 196608 | tf_op jit(solution)/shard_map/all_to_all | solution.py:46
  320.5 33.2 %psum.46 = f32[8]{0:T(128)S(1)} all-reduce(f32[8]{0:T(128)S(1)} %get-tuple-element.4), channel_id=1, replica_groups=mesh['row'=8,'col'=16] {'col'}, use_global_device_ids=true, to_apply=%region_7.0 | all-reduce | flops 8 | bytes 64 | tf_op jit(solution)/shard_map/psum | solution.py:37
  353.8 1.8 reshape.115
  355.5 3.8 multiply_reduce_fusion.2
  359.4 72.0 %psum.47 = f32[8]{0:T(128)S(1)} all-reduce(f32[8]{0:T(128)S(1)} %get-tuple-element.11), channel_id=1, replica_groups=mesh['row'=8,'col'=16] {'row','col'}, use_global_device_ids=true, to_apply=%region_9.0 | all-reduce | flops 8 | bytes 64 | tf_op jit(solution)/shard_map/psum | solution.py:51
  431.5 5.7 convolution_bitcast_fusion
  437.3 2.4 fusion.44
  440.4 146.9 %all-reduce.9.cloned.1.call-done = f32[128,4096]{1,0:T(8,128)} async-done(((f32[128,4096]{1,0:T(8,128)}), f32[128,4096]{1,0:T(8,128)}) %all-reduce.9.cloned.1.call-update) | async-done | bytes 2097168
  (51 shorter events, 17.1 us)
Async XLA Ops:
  7.2 313.2 %copy-start = (s32[16,16]{1,0:T(8,128)S(1)}, s32[16,16]{1,0:T(8,128)}, u32[]{:S(2)}) copy-start(s32[16,16]{1,0:T(8,128)} %param.12) | copy-start | bytes 3076
  7.2 16.4 %copy-start.5 = (s32[16,8]{0,1:T(8,128)S(1)}, s32[16,8]{0,1:T(8,128)}, u32[]{:S(2)}) copy-start(s32[16,8]{0,1:T(8,128)} %param.10) | copy-start | bytes 1540
  15.9 14.3 %all-to-all-start = ((bf16[16,2,1536]{2,1,0:T(2,128)(2,1)}), bf16[16,2,1536]{2,1,0:T(2,128)(2,1)S(1)}, u32[]{:S(2)}, u32[]{:S(2)}) async-start(bf16[16,2,1536]{2,1,0:T(2,128)(2,1)} %reshape.129), calls=%async_computation | async-start | bytes 196608 | tf_op jit(solution)/shard_map/all_to_all | solution.py:30
  23.5 72.1 %all-reduce.5.cloned.1.call-start = ((), (), s32[]{:S(2)}) async-start(), calls=%async_computation.4 | async-start | bytes 262144 | tf_op jit(solution)/shard_map/psum | solution.py:35
  102.6 119.1 %copy-start.4 = (f32[8,512]{1,0:T(8,128)S(1)}, f32[8,512]{1,0:T(8,128)}, u32[]{:S(2)}) copy-start(f32[8,512]{1,0:T(8,128)} %param.7) | copy-start | bytes 49156
  104.1 39.9 %all-to-all-start.1 = ((bf16[16,8,384]{2,1,0:T(8,128)(2,1)}), bf16[16,8,384]{2,1,0:T(8,128)(2,1)S(1)}, u32[]{:S(2)}, u32[]{:S(2)}) async-start(bf16[16,8,384]{2,1,0:T(8,128)(2,1)} %copy.56), calls=%async_computation.1 | async-start | bytes 196608 | tf_op jit(solution)/shard_map/all_to_all | solution.py:46
  110.6 194.7 %all-reduce.7.cloned.1.call-start = ((), (), s32[]{:S(2)}) async-start(), calls=%async_computation.5 | async-start | bytes 262144 | tf_op jit(solution)/shard_map/psum | solution.py:35
  312.3 119.2 %copy-start.2 = (f32[8,4096]{1,0:T(8,128)S(1)}, f32[8,4096]{1,0:T(8,128)}, u32[]{:S(2)}) copy-start(f32[8,4096]{1,0:T(8,128)} %all-reduce.5.cloned.1.call-done) | copy-start | bytes 393220
  312.3 119.2 %copy-start.3 = (f32[8,4096]{1,0:T(8,128)S(1)}, f32[8,4096]{1,0:T(8,128)}, u32[]{:S(2)}) copy-start(f32[8,4096]{1,0:T(8,128)} %all-reduce.7.cloned.1.call-done) | copy-start | bytes 393220
  313.7 40.0 %all-to-all-start.3 = ((bf16[16,8,384]{2,1,0:T(8,128)(2,1)}), bf16[16,8,384]{2,1,0:T(8,128)(2,1)S(1)}, u32[]{:S(2)}, u32[]{:S(2)}) async-start(bf16[16,8,384]{2,1,0:T(8,128)(2,1)} %copy.63), calls=%async_computation.3 | async-start | bytes 196608 | tf_op jit(solution)/shard_map/all_to_all | solution.py:46
  320.3 267.1 %all-reduce.9.cloned.1.call-start = ((), (), s32[]{:S(2)}) async-start(), calls=%async_computation.6 | async-start | bytes 4194304
  359.4 77.9 %copy-start.6 = (s32[128]{0:T(128)S(1)}, s32[128]{0:T(128)}, u32[]{:S(2)}) copy-start(s32[128]{0:T(128)} %param.13) | copy-start | bytes 1540
  431.5 8.2 %copy-start.1 = (f32[8,4096]{1,0:T(8,128)}, f32[8,4096]{1,0:T(8,128)S(1)}, u32[]{:S(2)}) copy-start(f32[8,4096]{1,0:T(8,128)S(1)} %multiply_add_fusion) | copy-start | bytes 393220
Sparse Core Ops, SparseCore 0:
  37.6 58.0 all-reduce.4
  250.2 55.0 all-reduce.6
  439.8 147.4 all-reduce.8
where the time goes:
time: 596 us; the launch traced here: 595 us
  waiting for transfers between devices  267 us (45%)
  blocking collectives  221 us (37%)
  matrix products  52.3 us (9%)
  starting transfers between devices  20.8 us (3%)
  local copies, waits for them, and re-layouts  15 us (3%)
  between operations  14 us (2%)
    unnamed x4, waiting for transfers between devices  147 us
    psum x2, blocking collectives, per_device(): image_sq = lax.psum(image_local, ('row', 'col'))  144 us
    psum x2, waiting for transfers between devices, per_device(): lax.psum(partial_grad.reshape(dens_count, own_cols * patch_len), 'row')  113 us
    psum x2, blocking collectives, per_device(): grad_sq = lax.psum(grad_local, 'col')  66.6 us
    dot_general x2, matrix products, per_device(): jnp.einsum('ijsp,dip->ijsd', u_factors, res_bf, preferred_element_type=jn...  15.3 us
    all_to_all x2, starting transfers between devices, per_device(): lax.all_to_all(coefficients, 'col', split_axis=0, concat_axis=1, tiled=True)  13.1 us
  transfers between devices with their start and end apart: 6, of which 4 were waited for; matrix products, arithmetic and copies ran while one was open for 0% of the time, Pallas kernels for 0%

commit v1 on v0

v1 whole, which is shorter than its diff:
```python
import jax
import jax.numpy as jnp
from jax import lax
from jax.experimental import pallas as pl
from jax.experimental.pallas import tpu as pltpu
from jax.sharding import PartitionSpec as P

F32, BF16 = jnp.float32, jnp.bfloat16
MIB = 1 << 20


def dot_nt(a, b):
    return lax.dot_general(a, b, (((1,), (1,)), ((), ())), preferred_element_type=F32)


def dot_nn(a, b):
    return lax.dot_general(a, b, (((1,), (0,)), ((), ())), preferred_element_type=F32)


def spread(value):
    high = value.astype(BF16).astype(F32)
    rest = value - high
    mid = rest.astype(BF16).astype(F32)
    low = rest - mid
    lane = lax.broadcasted_iota(jnp.int32, (value.shape[0], 128), 1)
    zero = jnp.zeros((value.shape[0], 128), F32)
    return jnp.where(
        lane == 0, high, jnp.where(lane == 1, mid, jnp.where(lane == 2, low, zero))
    ).astype(BF16)


def gather_sum(ref, low, width):
    total = ref[0, :, low : low + width].astype(F32)
    for source in range(1, ref.shape[0]):
        total = total + ref[source, :, low : low + width].astype(F32)
    return total


def call(kernel, outs, args, smem=(), scratch=(), limit=8):
    vm = pl.BlockSpec(memory_space=pltpu.VMEM)
    sm = pl.BlockSpec(memory_space=pltpu.SMEM)
    return pl.pallas_call(
        kernel,
        out_shape=tuple(jax.ShapeDtypeStruct(s, d) for s, d in outs),
        in_specs=[sm if at in smem else vm for at in range(len(args))],
        out_specs=tuple(vm for _ in outs),
        scratch_shapes=list(scratch),
        compiler_params=pltpu.CompilerParams(vmem_limit_bytes=limit * MIB),
        name=kernel.__name__,
    )(*args)


def per_device(right_side, u_factors, v_factors, ranks, far_blocks, block_target, recv_order):
    dens = right_side.shape[0]
    all_cols, slots, patch = u_factors.shape[1:]
    rows, cols = v_factors.shape[:2]
    peers = all_cols // cols
    wide = cols * slots
    n_row = lax.axis_size("row")
    tall = cols * dens
    blocks = far_blocks.shape[0]

    def in_vmem(x):
        return pltpu.with_memory_space_constraint(x, pltpu.VMEM)

    u_all = in_vmem(u_factors.reshape(all_cols * slots, patch))
    v_all = in_vmem(v_factors.reshape(rows * wide, patch))
    far_all = in_vmem(far_blocks)
    bound = jnp.repeat(
        (ranks + slots * jnp.arange(cols, dtype=jnp.int32)[None, :]).T, dens, axis=0
    )

    def kept_lanes(bound_ref, row_patch):
        lane = lax.broadcasted_iota(jnp.int32, (tall, wide), 1)
        first = lax.broadcasted_iota(jnp.int32, (tall, wide), 0) // dens * slots
        return (lane >= first) & (lane < bound_ref[:, row_patch : row_patch + 1])

    def back_kernel(res_ref, u_ref, out_ref):
        back = dot_nt(res_ref[...].astype(BF16), u_ref[...])
        for peer in range(peers):
            out_ref[peer] = back[:, peer * wide : (peer + 1) * wide].astype(BF16)

    def fill_left(in_ref, bound_ref, left_ref):
        for i in range(rows):
            piece = in_ref[i, :, 0:wide].astype(F32)
            stacked = jnp.concatenate([piece] * cols, axis=0)
            left_ref[:, i * wide : (i + 1) * wide] = jnp.where(
                kept_lanes(bound_ref, i), stacked, 0.0
            ).astype(BF16)

    def grad_kernel(in_ref, bound_ref, v_ref, out_ref, left_ref):
        fill_left(in_ref, bound_ref, left_ref)
        out_ref[...] = dot_nn(left_ref[...], v_ref[...])

    def grad_norm_kernel(in_ref, bound_ref, v_ref, out_ref, left_ref):
        fill_left(in_ref, bound_ref, left_ref)
        out_ref[0:tall, :] = dot_nn(left_ref[...], v_ref[...])
        norm = jnp.sum(gather_sum(in_ref, wide, 128), axis=1, keepdims=True)
        out_ref[tall : tall + dens, :] = jnp.broadcast_to(norm, (dens, patch))

    def coefficients(grad, bound_ref, v_ref, out_ref):
        half = grad.astype(BF16)
        for i in range(0, rows, 2):
            both = dot_nt(half, v_ref[i * wide : (i + 2) * wide, :])
            for k in range(2):
                part = jnp.where(
                    kept_lanes(bound_ref, i + k), both[:, k * wide : (k + 1) * wide], 0.0
                )
                total = part[0:dens]
                for j in range(1, cols):
                    total = total + part[j * dens : (j + 1) * dens]
                out_ref[i + k, :, 0:wide] = total.astype(BF16)

    def norm_of(grad):
        line = jnp.sum(grad * grad, axis=1, keepdims=True)
        total = line[0:dens]
        for j in range(1, line.shape[0] // dens):
            total = total + line[j * dens : (j + 1) * dens]
        return total

    def coef_kernel(p0_ref, p2_ref, p4_ref, p6_ref, bound_ref, v_ref, out_ref, grad_ref):
        grad = (p0_ref[...].astype(F32) + p2_ref[...].astype(F32)) + (
            p4_ref[...].astype(F32) + p6_ref[...].astype(F32)
        )
        grad_ref[...] = grad
        coefficients(grad, bound_ref, v_ref, out_ref)
        mine = spread(norm_of(grad))
        for i in range(rows):
            out_ref[i, :, wide : wide + 128] = mine

    def image_of(in_ref, u_ref):
        left = jnp.concatenate([in_ref[c, :, 0:wide] for c in range(peers)], axis=1)
        return dot_nn(left, u_ref[...])

    def image_back_kernel(in_ref, u_ref, image_ref, gsq_ref, out_ref):
        image = image_of(in_ref, u_ref)
        image_ref[...] = image
        gsq_ref[...] = jnp.broadcast_to(
            jnp.sum(gather_sum(in_ref, wide, 128), axis=1, keepdims=True), (dens, 128)
        )
        high = image.astype(BF16)
        low = (image - high.astype(F32)).astype(BF16)
        both = dot_nt(jnp.concatenate([high, low], axis=0), u_ref[...])
        back = both[0:dens] + both[dens : 2 * dens]
        mine = spread(norm_of(image))
        for peer in range(peers):
            out_ref[peer, :, 0:wide] = back[:, peer * wide : (peer + 1) * wide].astype(BF16)
            out_ref[peer, :, wide : wide + 128] = mine

    far_low = wide + 128

    def coef_far_kernel(
        p0_ref, p2_ref, p4_ref, p6_ref, grad_ref, gsq_ref, bound_ref, v_ref, far_ref,
        out_ref, first_ref, second_ref, step_ref, even_ref,
    ):
        wave = (p0_ref[...].astype(F32) + p2_ref[...].astype(F32)) + (
            p4_ref[...].astype(F32) + p6_ref[...].astype(F32)
        )
        isq = jnp.sum(wave[tall : tall + dens, 0:128], axis=1, keepdims=True)
        step = gsq_ref[:, 0:1] / (isq + 1e-6)
        step_ref[...] = jnp.broadcast_to(step, (dens, 128))
        steps = jnp.concatenate([step] * cols, axis=0)
        first = steps * grad_ref[...]
        second = grad_ref[...] - steps * wave[0:tall]
        first_ref[...] = first
        second_ref[...] = second
        coefficients(second, bound_ref, v_ref, out_ref)
        mine = spread(norm_of(second))
        first_row = jnp.concatenate([first[j * dens : (j + 1) * dens] for j in range(cols)], axis=1)
        second_row = jnp.concatenate(
            [second[j * dens : (j + 1) * dens] for j in range(cols)], axis=1
        )
        left = jnp.concatenate([first_row, second_row], axis=0).astype(BF16)
        even = dot_nt(left, far_ref[0])
        odd = dot_nt(left, far_ref[1])
        even_ref[...] = jnp.concatenate([even[0:dens], even[dens : 2 * dens]], axis=1).astype(BF16)
        send = jnp.concatenate([odd[0:dens], odd[dens : 2 * dens]], axis=1).astype(BF16)
        for i in range(rows):
            out_ref[i, :, wide : wide + 128] = mine
            out_ref[i, :, far_low : far_low + 2 * patch] = send

    def image_far_kernel(route_ref, even_ref, in_ref, u_ref, image_ref, gsq_ref, out_ref):
        image = image_of(in_ref, u_ref)
        image_ref[...] = image
        gsq_ref[...] = jnp.broadcast_to(
            jnp.sum(gather_sum(in_ref, wide, 128), axis=1, keepdims=True), (dens, 128)
        )
        mine = spread(norm_of(image))
        for target in range(n_row):
            total = even_ref[...].astype(F32) * route_ref[target, peers]
            for source in range(peers):
                total = total + in_ref[source, :, far_low : far_low + 2 * patch].astype(
                    F32
                ) * route_ref[target, source]
            out_ref[target, :, 0 : 2 * patch] = total.astype(BF16)
            out_ref[target, :, 2 * patch : 2 * patch + 128] = mine

    def relay_kernel(in_ref, out_ref):
        mine = spread(jnp.sum(gather_sum(in_ref, 2 * patch, 128), axis=1, keepdims=True))
        for peer in range(peers):
            out_ref[peer] = mine

    def finish_kernel(
        norm_ref, gsq_ref, first_ref, second_ref, res_ref, image1_ref, image2_ref, step_ref,
        far_ref, side_ref, dens_ref, out_res_ref, out_far_ref,
    ):
        isq = jnp.sum(gather_sum(norm_ref, 0, 128), axis=1, keepdims=True)
        step = gsq_ref[:, 0:1] / (isq + 1e-6)
        for j in range(cols):
            at = slice(j * dens, (j + 1) * dens)
            dens_ref[:, j * patch : (j + 1) * patch] = first_ref[at] + step * second_ref[at]
        out_res_ref[...] = (
            res_ref[...] - step_ref[:, 0:1] * image1_ref[...] - step * image2_ref[...]
        )
        both = gather_sum(far_ref, 0, 2 * patch) + side_ref[...].astype(F32)
        field = both[:, 0:patch] + step * both[:, patch : 2 * patch]
        for d in range(dens):
            out_far_ref[:, d * patch : (d + 1) * patch] = field[d : d + 1]

    def over_rows(part):
        pair = part + lax.ppermute(part, "row", [(i, i ^ 1) for i in range(n_row)])
        if pair.shape[0] > tall:
            high = lax.reduce_precision(pair, 8, 7)
            rest = pair - high
            mid = lax.reduce_precision(rest, 8, 7)
            row = lax.broadcasted_iota(jnp.int32, pair.shape, 0)
            lane = lax.broadcasted_iota(jnp.int32, pair.shape, 1)
            terms = jnp.where(
                lane == 0, high, jnp.where(lane == 1, mid, jnp.where(lane == 2, rest - mid, 0.0))
            )
            pair = jnp.where(row < tall, pair, terms)
        half = lax.optimization_barrier(pair.astype(BF16))
        return [half] + [
            lax.ppermute(half, "row", [(i, i ^ k) for i in range(n_row)]) for k in (2, 4, 6)
        ]

    def over_col(x):
        return lax.all_to_all(x, "col", split_axis=0, concat_axis=0, tiled=True)

    me_row, me_col = lax.axis_index("row"), lax.axis_index("col")
    odd_targets = lax.dynamic_slice(block_target, (me_row * blocks + 1, 0), (1, peers))
    my_order = lax.dynamic_slice(recv_order.reshape(n_row, peers), (0, me_col), (n_row, 1))
    partner = (jnp.arange(n_row) == (me_row + n_row // 2) % n_row) & (me_col % 2 == 0)
    route = jnp.concatenate([my_order == odd_targets, partner[:, None]], axis=1).astype(F32)

    left_scratch = (pltpu.VMEM((tall, rows * wide), BF16),)
    (sent,) = call(back_kernel, [((peers, dens, wide), BF16)], [right_side, u_all])
    (part,) = call(
        grad_kernel, [((tall, patch), F32)], [over_col(sent), bound, v_all], scratch=left_scratch
    )
    sent, grad = call(
        coef_kernel,
        [((rows, dens, wide + 128), BF16), ((tall, patch), F32)],
        over_rows(part) + [bound, v_all],
    )
    image1, gsq1, sent = call(
        image_back_kernel,
        [((dens, patch), F32), ((dens, 128), F32), ((peers, dens, wide + 128), BF16)],
        [over_col(sent), u_all],
    )
    (part,) = call(
        grad_norm_kernel,
        [((tall + dens, patch), F32)],
        [over_col(sent), bound, v_all],
        scratch=left_scratch,
    )
    sent, first, second, step1, even = call(
        coef_far_kernel,
        [
            ((rows, dens, far_low + 2 * patch), BF16),
            ((tall, patch), F32),
            ((tall, patch), F32),
            ((dens, 128), F32),
            ((dens, 2 * patch), BF16),
        ],
        over_rows(part) + [grad, gsq1, bound, v_all, far_all],
    )
    side = lax.ppermute(even, "col", [(c, c - 1) for c in range(1, peers, 2)])
    image2, gsq2, sent = call(
        image_far_kernel,
        [((dens, patch), F32), ((dens, 128), F32), ((n_row, dens, 2 * patch + 128), BF16)],
        [route, even, over_col(sent), u_all],
        smem=(0,),
    )
    far_in = lax.all_to_all(sent, "row", split_axis=0, concat_axis=0, tiled=True)
    (relayed,) = call(relay_kernel, [((peers, dens, 128), BF16)], [far_in])
    densities, residual, far_field = call(
        finish_kernel,
        [((dens, cols * patch), F32), ((dens, patch), F32), ((1, dens * patch), F32)],
        [over_col(relayed), gsq2, first, second, right_side, image1, image2, step1, far_in, side],
    )
    return densities, residual, far_field


def solution(mesh):
    return jax.shard_map(
        per_device,
        mesh=mesh,
        in_specs=(
            P(None, ("row", "col")),
            P(("row", "col"), None, None, None),
            P("row", "col", None, None),
            P("row", "col"),
            P("row", None, "col"),
            P(),
            P(),
        ),
        out_specs=(P(None, "col"), P(None, ("row", "col")), P(("row", "col"), None)),
        check_vma=False,
    )
```

time: 596 us -> 132 us (0.22)
  waiting for transfers between devices: 267 us -> 36.7 us
  blocking collectives: 221 us -> 20.2 us
  matrix products: 52.3 us -> 0 us
  Pallas kernels: 0 us -> 18.8 us
  starting transfers between devices: 20.8 us -> 35.2 us
  between operations: 14 us -> 0.8 us
    psum x4 -> x0, blocking collectives: 211 us -> none  [the longest x2 144 us: per_device(): image_sq = lax.psum(image_local, ('row', 'col'))]
    unnamed x4 -> x0, waiting for transfers between devices: 147 us -> none
    psum x2 -> x0, waiting for transfers between devices: 113 us -> none  [per_device(): lax.psum(partial_grad.reshape(dens_count, own_cols * patch_len), 'row')]
    dot_general x10 -> x0, matrix products: 52.3 us -> none  [the longest x2 15.3 us: per_device(): jnp.einsum('ijsp,dip->ijsd', u_factors, res_bf, preferred_element_type=jn...]
    pallas_call x0 -> x9, Pallas kernels: none -> 18.8 us  [call(): pl.pallas_call(kernel, out_shape=tuple((jax.ShapeDtypeStruct(s, d) for s,...]
    all_to_all x3 -> x4, waiting for transfers between devices: 6.56 us -> 23.7 us  [over_col(): return lax.all_to_all(x, 'col', split_axis=0, concat_axis=0, tiled=True)]
    ppermute x0 -> x9, starting transfers between devices: none -> 16.9 us  [the longest x6 8.96 us: over_rows(): lax.ppermute(half, 'row', [(i, i ^ k) for i in range(n_row)])]
    unnamed x21 -> x26, local copies, waits for them, and re-layouts: 2.99 us -> 18 us
  transfers between devices with their start and end apart: 6 -> 13, of which waited for: 4 -> 11; matrix products, arithmetic and copies ran while one was open for 0% -> 0% of each run, Pallas kernels for 0% -> 0%
where the time goes in v1:
time: 132 us; the launch traced here: 130 us
  waiting for transfers between devices  36.7 us (28%)
  starting transfers between devices  35.2 us (27%)
  blocking collectives  20.2 us (15%)
  Pallas kernels  18.8 us (14%)
  local copies, waits for them, and re-layouts  18.3 us (14%)
    all_to_all x4, waiting for transfers between devices, over_col(): return lax.all_to_all(x, 'col', split_axis=0, concat_axis=0, tiled=True)  23.7 us
    pallas_call x9, Pallas kernels, call(): pl.pallas_call(kernel, out_shape=tuple((jax.ShapeDtypeStruct(s, d) for s,...  18.8 us
    all_to_all x4, starting transfers between devices, over_col(): return lax.all_to_all(x, 'col', split_axis=0, concat_axis=0, tiled=True)  18.3 us
    unnamed x26, local copies, waits for them, and re-layouts  18 us
    all_to_all x1, blocking collectives, per_device(): lax.all_to_all(sent, 'row', split_axis=0, concat_axis=0, tiled=True)  10.5 us
    all_to_all x1, blocking collectives, over_col(): return lax.all_to_all(x, 'col', split_axis=0, concat_axis=0, tiled=True)  9.73 us
    ppermute x6, starting transfers between devices, over_rows(): lax.ppermute(half, 'row', [(i, i ^ k) for i in range(n_row)])  8.96 us
    ppermute x6, waiting for transfers between devices, over_rows(): lax.ppermute(half, 'row', [(i, i ^ k) for i in range(n_row)])  7.48 us
  transfers between devices with their start and end apart: 13, of which 11 were waited for; matrix products, arithmetic and copies ran while one was open for 0% of the time, Pallas kernels for 0%

profile of v1, /device:TPU:1, one launch (start us, length us, event | category | flops | bytes accessed | tf_op | source)
XLA Modules:
  0.0 130.3 jit_solution(15043000108524408825)
XLA Ops:
  0.7 2.8 %copy-done.5 = bf16[1,128,48,512]{3,2,1,0:T(8,128)(2,1)S(1)} copy-done((bf16[1,128,48,512]{3,2,1,0:T(8,128)(2,1)S(1)}, bf16[1,128,48,512]{3,2,1,0:T(8,128)(2,1)}, u32[]{:S(2)}) %copy-start.5) | copy-done | bytes 6291480
  4.2 2.4 %back_kernel.1 = bf16[16,8,384]{2,1,0:T(8,128)(2,1)} custom-call(f32[8,512]{1,0:T(8,128)S(1)} %copy-done.9, bf16[6144,512]{1,0:T(8,128)(2,1)S(1)} %bitcast.12), custom_call_target="tpu_custom_call" | custom-call | tf_op jit(solution)/shard_map/back_kernel/pallas_call | solution.py:42
  6.5 7.6 %all-to-all-start = ((bf16[16,8,384]{2,1,0:T(8,128)(2,1)}), bf16[16,8,384]{2,1,0:T(8,128)(2,1)S(1)}, u32[]{:S(2)}, u32[]{:S(2)}) async-start(bf16[16,8,384]{2,1,0:T(8,128)(2,1)} %back_kernel.1), calls=%async_computation | async-start | bytes 196608 | tf_op jit(solution)/shard_map/all_to_all | solution.py:238
  14.2 6.6 %all-to-all-done.in_ref = bf16[16,8,384]{2,1,0:T(8,128)(2,1)S(1)} async-done(((bf16[16,8,384]{2,1,0:T(8,128)(2,1)}), bf16[16,8,384]{2,1,0:T(8,128)(2,1)S(1)}, u32[]{:S(2)}, u32[]{:S(2)}) %all-to-all-start) | async-done | bytes 98336 | tf_op jit(solution)/shard_map/all_to_all | solution.py:238
  20.9 2.8 %copy-done.1 = bf16[16,8,48,512]{3,2,1,0:T(8,128)(2,1)S(1)} copy-done((bf16[16,8,48,512]{3,2,1,0:T(8,128)(2,1)S(1)}, bf16[16,8,48,512]{3,2,1,0:T(8,128)(2,1)}, u32[]{:S(2)}) %copy-start.1) | copy-done | bytes 6291480
  24.9 2.1 %collective-permute-start = (f32[64,512]{1,0:T(8,128)S(1)}, f32[64,512]{1,0:T(8,128)S(1)}, u32[]{:S(2)}, u32[]{:S(2)}) collective-permute-start(f32[64,512]{1,0:T(8,128)S(1)} %grad_kernel.1), channel_id=1, source_target_pairs={{0,16},{16,0},{32,48},{48,32},{64,80},{80,64},{96,112},{112,96},{1... | collective-permute-start | bytes 393224 | tf_op jit(solution)/shard_map/ppermute | solution.py:221
  29.8 3.3 %collective-permute-start.2 = (bf16[64,512]{1,0:T(8,128)(2,1)S(1)}, bf16[64,512]{1,0:T(8,128)(2,1)S(1)}, u32[]{:S(2)}, u32[]{:S(2)}) collective-permute-start(bf16[64,512]{1,0:T(8,128)(2,1)S(1)} %add_convert_fusion.p0_ref), channel_id=1, source_target_pairs={{0,64},{16,80},{32,96},{48,112},{64,0},{80,16},{96,32},{112,48},{1... | collective-permute-start | bytes 196616 | tf_op jit(solution)/shard_map/ppermute | solution.py:234
  33.1 2.9 %collective-permute-done.2.p4_ref = bf16[64,512]{1,0:T(8,128)(2,1)S(1)} collective-permute-done((bf16[64,512]{1,0:T(8,128)(2,1)S(1)}, bf16[64,512]{1,0:T(8,128)(2,1)S(1)}, u32[]{:S(2)}, u32[]{:S(2)}) %collective-permute-start.2) | collective-permute-done | bytes 65568 | tf_op jit(solution)/shard_map/ppermute | solution.py:234
  39.6 9.7 %all_to_all.30.in_ref = bf16[16,8,512]{2,1,0:T(8,128)(2,1)S(1)} all-to-all(bf16[16,8,512]{2,1,0:T(8,128)(2,1)S(1)} %get-tuple-element.16), channel_id=1, replica_groups=mesh['row'=8,'col'=16] {'col'}, dimensions={0} | all-to-all | bytes 262144 | tf_op jit(solution)/shard_map/all_to_all | solution.py:238
  49.3 3.3 %image_back_kernel.1 = (f32[8,512]{1,0:T(8,128)S(1)}, f32[8,128]{1,0:T(8,128)S(1)}, bf16[16,8,512]{2,1,0:T(8,128)(2,1)}) custom-call(bf16[16,8,512]{2,1,0:T(8,128)(2,1)S(1)} %all_to_all.30.in_ref, bf16[6144,512]{1,0:T(8,128)(2,1)S(1)} %bitcast.13), custom_call_target="tpu_custom_call" | custom-call | tf_op jit(solution)/shard_map/image_back_kernel/pallas_call | solution.py:42
  52.6 3.5 %all-to-all-start.2 = ((bf16[16,8,512]{2,1,0:T(8,128)(2,1)}), bf16[16,8,512]{2,1,0:T(8,128)(2,1)S(1)}, u32[]{:S(2)}, u32[]{:S(2)}) async-start(bf16[16,8,512]{2,1,0:T(8,128)(2,1)} %get-tuple-element.17), calls=%async_computation.2 | async-start | bytes 262144 | tf_op jit(solution)/shard_map/all_to_all | solution.py:238
  56.1 6.8 %all-to-all-done.2.in_ref = bf16[16,8,512]{2,1,0:T(8,128)(2,1)S(1)} async-done(((bf16[16,8,512]{2,1,0:T(8,128)(2,1)}), bf16[16,8,512]{2,1,0:T(8,128)(2,1)S(1)}, u32[]{:S(2)}, u32[]{:S(2)}) %all-to-all-start.2) | async-done | bytes 131104 | tf_op jit(solution)/shard_map/all_to_all | solution.py:238
  62.9 2.8 %copy-done.3 = bf16[16,8,48,512]{3,2,1,0:T(8,128)(2,1)S(1)} copy-done((bf16[16,8,48,512]{3,2,1,0:T(8,128)(2,1)S(1)}, bf16[16,8,48,512]{3,2,1,0:T(8,128)(2,1)}, u32[]{:S(2)}) %copy-start.3) | copy-done | bytes 6291480
  67.0 4.5 %collective-permute-start.4 = (f32[72,512]{1,0:T(8,128)S(1)}, f32[72,512]{1,0:T(8,128)S(1)}, u32[]{:S(2)}, u32[]{:S(2)}) collective-permute-start(f32[72,512]{1,0:T(8,128)S(1)} %grad_norm_kernel.1), channel_id=1, source_target_pairs={{0,16},{16,0},{32,48},{48,32},{64,80},{80,64},{96,112},{112,96},{1... | collective-permute-start | bytes 442376 | tf_op jit(solution)/shard_map/ppermute | solution.py:221
  73.9 2.7 %collective-permute-start.7 = (bf16[72,512]{1,0:T(8,128)(2,1)S(1)}, bf16[72,512]{1,0:T(8,128)(2,1)S(1)}, u32[]{:S(2)}, u32[]{:S(2)}) collective-permute-start(bf16[72,512]{1,0:T(8,128)(2,1)S(1)} %fusion.1.p0_ref), channel_id=1, source_target_pairs={{0,96},{16,112},{32,64},{48,80},{64,32},{80,48},{96,0},{112,16},{1... | collective-permute-start | bytes 221192 | tf_op jit(solution)/shard_map/ppermute | solution.py:234
  79.6 2.8 %copy-done.4 = bf16[16,8,48,512]{3,2,1,0:T(8,128)(2,1)S(1)} copy-done((bf16[16,8,48,512]{3,2,1,0:T(8,128)(2,1)S(1)}, bf16[16,8,48,512]{3,2,1,0:T(8,128)(2,1)}, u32[]{:S(2)}) %copy-start.4) | copy-done | bytes 6291480
  82.4 3.4 %copy-done.8 = bf16[2,512,4096]{2,1,0:T(8,128)(2,1)S(1)} copy-done((bf16[2,512,4096]{2,1,0:T(8,128)(2,1)S(1)}, bf16[2,512,4096]{2,1,0:T(8,128)(2,1)}, u32[]{:S(2)}) %copy-start.8) | copy-done | bytes 8388632
  85.8 5.1 %coef_far_kernel.1 = (bf16[16,8,1536]{2,1,0:T(8,128)(2,1)}, f32[64,512]{1,0:T(8,128)S(1)}, f32[64,512]{1,0:T(8,128)S(1)}, f32[8,128]{1,0:T(8,128)S(1)}, bf16[8,1024]{1,0:T(8,128)(2,1)S(1)}) custom-call(bf16[72,512]{1,0:T(8,128)(2,1)S(1)} %fusion.1.p0_ref, bf16[72,512]{1,0:T(8,128)(2,1)S(1)} %collective-permute-done.5.p2_ref, ...), custom_call_target="tpu_custom_call" | custom-call | tf_op jit(solution)/shard_map/coef_far_kernel/pallas_call | solution.py:42
  90.8 3.7 %all-to-all-start.3 = ((bf16[16,8,1536]{2,1,0:T(8,128)(2,1)}), bf16[16,8,1536]{2,1,0:T(8,128)(2,1)S(1)}, u32[]{:S(2)}, u32[]{:S(2)}) async-start(bf16[16,8,1536]{2,1,0:T(8,128)(2,1)} %get-tuple-element.21), calls=%async_computation.3 | async-start | bytes 786432 | tf_op jit(solution)/shard_map/all_to_all | solution.py:238
  95.0 8.7 %all-to-all-done.3.in_ref = bf16[16,8,1536]{2,1,0:T(8,128)(2,1)S(1)} async-done(((bf16[16,8,1536]{2,1,0:T(8,128)(2,1)}), bf16[16,8,1536]{2,1,0:T(8,128)(2,1)S(1)}, u32[]{:S(2)}, u32[]{:S(2)}) %all-to-all-start.3) | async-done | bytes 393248 | tf_op jit(solution)/shard_map/all_to_all | solution.py:238
  103.7 2.8 %copy-done.7 = bf16[1,128,48,512]{3,2,1,0:T(8,128)(2,1)S(1)} copy-done((bf16[1,128,48,512]{3,2,1,0:T(8,128)(2,1)S(1)}, bf16[1,128,48,512]{3,2,1,0:T(8,128)(2,1)}, u32[]{:S(2)}) %copy-start.7) | copy-done | bytes 6291480
  108.4 10.5 %all_to_all.31.in_ref.far_ref = bf16[8,8,1152]{2,1,0:T(8,128)(2,1)S(1)} all-to-all(bf16[8,8,1152]{2,1,0:T(8,128)(2,1)S(1)} %get-tuple-element.22), channel_id=1, replica_groups=mesh['row'=8,'col'=16] {'row'}, dimensions={0} | all-to-all | bytes 294912 | tf_op jit(solution)/shard_map/all_to_all | solution.py:285
  119.6 3.5 %all-to-all-start.5 = ((bf16[16,8,128]{2,1,0:T(8,128)(2,1)}), bf16[16,8,128]{2,1,0:T(8,128)(2,1)S(1)}, u32[]{:S(2)}, u32[]{:S(2)}) async-start(bf16[16,8,128]{2,1,0:T(8,128)(2,1)} %relay_kernel.1), calls=%async_computation.5 | async-start | bytes 65536 | tf_op jit(solution)/shard_map/all_to_all | solution.py:238
  124.4 3.5 %collective-permute-done.8.side_ref = bf16[8,1024]{1,0:T(8,128)(2,1)S(1)} collective-permute-done((bf16[8,1024]{1,0:T(8,128)(2,1)S(1)}, bf16[8,1024]{1,0:T(8,128)(2,1)S(1)}, u32[]{:S(2)}, u32[]{:S(2)}) %collective-permute-start.8) | collective-permute-done | bytes 16416 | tf_op jit(solution)/shard_map/ppermute | solution.py:278
  (53 shorter events, 21.9 us)
Async XLA Ops:
  0.6 93.9 %copy-start = (s32[16,16]{1,0:T(8,128)S(1)}, s32[16,16]{1,0:T(8,128)}, u32[]{:S(2)}) copy-start(s32[16,16]{1,0:T(8,128)} %param.12) | copy-start | bytes 3076
  0.6 2.8 %copy-start.5 = (bf16[1,128,48,512]{3,2,1,0:T(8,128)(2,1)S(1)}, bf16[1,128,48,512]{3,2,1,0:T(8,128)(2,1)}, u32[]{:S(2)}) copy-start(bf16[1,128,48,512]{3,2,1,0:T(8,128)(2,1)} %param.8) | copy-start | bytes 18874372
  4.2 10.0 %copy-start.11 = (s32[16,8]{0,1:T(8,128)S(1)}, s32[16,8]{0,1:T(8,128)}, u32[]{:S(2)}) copy-start(s32[16,8]{0,1:T(8,128)} %param.10) | copy-start | bytes 1540
  6.5 14.3 %all-to-all-start = ((bf16[16,8,384]{2,1,0:T(8,128)(2,1)}), bf16[16,8,384]{2,1,0:T(8,128)(2,1)S(1)}, u32[]{:S(2)}, u32[]{:S(2)}) async-start(bf16[16,8,384]{2,1,0:T(8,128)(2,1)} %back_kernel.1), calls=%async_computation | async-start | bytes 196608 | tf_op jit(solution)/shard_map/all_to_all | solution.py:238
  20.9 2.8 %copy-start.1 = (bf16[16,8,48,512]{3,2,1,0:T(8,128)(2,1)S(1)}, bf16[16,8,48,512]{3,2,1,0:T(8,128)(2,1)}, u32[]{:S(2)}) copy-start(bf16[16,8,48,512]{3,2,1,0:T(8,128)(2,1)} %param.9) | copy-start | bytes 18874372
  23.6 13.9 %copy-start.2 = (bf16[16,8,48,512]{3,2,1,0:T(8,128)(2,1)S(1)}, bf16[16,8,48,512]{3,2,1,0:T(8,128)(2,1)}, u32[]{:S(2)}) copy-start(bf16[16,8,48,512]{3,2,1,0:T(8,128)(2,1)} %param.9) | copy-start | bytes 18874372
  23.6 25.7 %copy-start.6 = (bf16[1,128,48,512]{3,2,1,0:T(8,128)(2,1)S(1)}, bf16[1,128,48,512]{3,2,1,0:T(8,128)(2,1)}, u32[]{:S(2)}) copy-start(bf16[1,128,48,512]{3,2,1,0:T(8,128)(2,1)} %param.8) | copy-start | bytes 18874372
  24.9 3.1 %collective-permute-start = (f32[64,512]{1,0:T(8,128)S(1)}, f32[64,512]{1,0:T(8,128)S(1)}, u32[]{:S(2)}, u32[]{:S(2)}) collective-permute-start(f32[64,512]{1,0:T(8,128)S(1)} %grad_kernel.1), channel_id=1, source_target_pairs={{0,16},{16,0},{32,48},{48,32},{64,80},{80,64},{96,112},{112,96},{1... | collective-permute-start | bytes 393224 | tf_op jit(solution)/shard_map/ppermute | solution.py:221
  28.0 5.0 %collective-permute-start.1 = (bf16[64,512]{1,0:T(8,128)(2,1)S(1)}, bf16[64,512]{1,0:T(8,128)(2,1)S(1)}, u32[]{:S(2)}, u32[]{:S(2)}) collective-permute-start(bf16[64,512]{1,0:T(8,128)(2,1)S(1)} %add_convert_fusion.p0_ref), channel_id=1, source_target_pairs={{0,32},{16,48},{32,0},{48,16},{64,96},{80,112},{96,64},{112,80},{1... | collective-permute-start | bytes 196616 | tf_op jit(solution)/shard_map/ppermute | solution.py:234
  29.8 6.2 %collective-permute-start.2 = (bf16[64,512]{1,0:T(8,128)(2,1)S(1)}, bf16[64,512]{1,0:T(8,128)(2,1)S(1)}, u32[]{:S(2)}, u32[]{:S(2)}) collective-permute-start(bf16[64,512]{1,0:T(8,128)(2,1)S(1)} %add_convert_fusion.p0_ref), channel_id=1, source_target_pairs={{0,64},{16,80},{32,96},{48,112},{64,0},{80,16},{96,32},{112,48},{1... | collective-permute-start | bytes 196616 | tf_op jit(solution)/shard_map/ppermute | solution.py:234
  33.1 4.5 %collective-permute-start.3 = (bf16[64,512]{1,0:T(8,128)(2,1)S(1)}, bf16[64,512]{1,0:T(8,128)(2,1)S(1)}, u32[]{:S(2)}, u32[]{:S(2)}) collective-permute-start(bf16[64,512]{1,0:T(8,128)(2,1)S(1)} %add_convert_fusion.p0_ref), channel_id=1, source_target_pairs={{0,96},{16,112},{32,64},{48,80},{64,32},{80,48},{96,0},{112,16},{1... | collective-permute-start | bytes 196616 | tf_op jit(solution)/shard_map/ppermute | solution.py:234
  52.6 10.3 %all-to-all-start.2 = ((bf16[16,8,512]{2,1,0:T(8,128)(2,1)}), bf16[16,8,512]{2,1,0:T(8,128)(2,1)S(1)}, u32[]{:S(2)}, u32[]{:S(2)}) async-start(bf16[16,8,512]{2,1,0:T(8,128)(2,1)} %get-tuple-element.17), calls=%async_computation.2 | async-start | bytes 262144 | tf_op jit(solution)/shard_map/all_to_all | solution.py:238
  62.9 2.8 %copy-start.3 = (bf16[16,8,48,512]{3,2,1,0:T(8,128)(2,1)S(1)}, bf16[16,8,48,512]{3,2,1,0:T(8,128)(2,1)}, u32[]{:S(2)}) copy-start(bf16[16,8,48,512]{3,2,1,0:T(8,128)(2,1)} %param.9) | copy-start | bytes 18874372
  67.0 5.6 %collective-permute-start.4 = (f32[72,512]{1,0:T(8,128)S(1)}, f32[72,512]{1,0:T(8,128)S(1)}, u32[]{:S(2)}, u32[]{:S(2)}) collective-permute-start(f32[72,512]{1,0:T(8,128)S(1)} %grad_norm_kernel.1), channel_id=1, source_target_pairs={{0,16},{16,0},{32,48},{48,32},{64,80},{80,64},{96,112},{112,96},{1... | collective-permute-start | bytes 442376 | tf_op jit(solution)/shard_map/ppermute | solution.py:221
  72.6 4.0 %collective-permute-start.5 = (bf16[72,512]{1,0:T(8,128)(2,1)S(1)}, bf16[72,512]{1,0:T(8,128)(2,1)S(1)}, u32[]{:S(2)}, u32[]{:S(2)}) collective-permute-start(bf16[72,512]{1,0:T(8,128)(2,1)S(1)} %fusion.1.p0_ref), channel_id=1, source_target_pairs={{0,32},{16,48},{32,0},{48,16},{64,96},{80,112},{96,64},{112,80},{1... | collective-permute-start | bytes 221192 | tf_op jit(solution)/shard_map/ppermute | solution.py:234
  72.7 4.8 %collective-permute-start.6 = (bf16[72,512]{1,0:T(8,128)(2,1)S(1)}, bf16[72,512]{1,0:T(8,128)(2,1)S(1)}, u32[]{:S(2)}, u32[]{:S(2)}) collective-permute-start(bf16[72,512]{1,0:T(8,128)(2,1)S(1)} %fusion.1.p0_ref), channel_id=1, source_target_pairs={{0,64},{16,80},{32,96},{48,112},{64,0},{80,16},{96,32},{112,48},{1... | collective-permute-start | bytes 221192 | tf_op jit(solution)/shard_map/ppermute | solution.py:234
  73.9 5.7 %collective-permute-start.7 = (bf16[72,512]{1,0:T(8,128)(2,1)S(1)}, bf16[72,512]{1,0:T(8,128)(2,1)S(1)}, u32[]{:S(2)}, u32[]{:S(2)}) collective-permute-start(bf16[72,512]{1,0:T(8,128)(2,1)S(1)} %fusion.1.p0_ref), channel_id=1, source_target_pairs={{0,96},{16,112},{32,64},{48,80},{64,32},{80,48},{96,0},{112,16},{1... | collective-permute-start | bytes 221192 | tf_op jit(solution)/shard_map/ppermute | solution.py:234
  79.6 2.8 %copy-start.4 = (bf16[16,8,48,512]{3,2,1,0:T(8,128)(2,1)S(1)}, bf16[16,8,48,512]{3,2,1,0:T(8,128)(2,1)}, u32[]{:S(2)}) copy-start(bf16[16,8,48,512]{3,2,1,0:T(8,128)(2,1)} %param.9) | copy-start | bytes 18874372
  82.4 3.4 %copy-start.8 = (bf16[2,512,4096]{2,1,0:T(8,128)(2,1)S(1)}, bf16[2,512,4096]{2,1,0:T(8,128)(2,1)}, u32[]{:S(2)}) copy-start(bf16[2,512,4096]{2,1,0:T(8,128)(2,1)} %far_ref.1) | copy-start | bytes 25165828
  85.8 8.8 %copy-start.12 = (s32[128]{0:T(128)S(1)}, s32[128]{0:T(128)}, u32[]{:S(2)}) copy-start(s32[128]{0:T(128)} %param.13) | copy-start | bytes 1540
  90.8 38.7 %copy-start.10 = (f32[8,512]{1,0:T(8,128)S(1)}, f32[8,512]{1,0:T(8,128)}, u32[]{:S(2)}) copy-start(f32[8,512]{1,0:T(8,128)} %res_ref.3) | copy-start | bytes 49156
  90.8 12.8 %all-to-all-start.3 = ((bf16[16,8,1536]{2,1,0:T(8,128)(2,1)}), bf16[16,8,1536]{2,1,0:T(8,128)(2,1)S(1)}, u32[]{:S(2)}, u32[]{:S(2)}) async-start(bf16[16,8,1536]{2,1,0:T(8,128)(2,1)} %get-tuple-element.21), calls=%async_computation.3 | async-start | bytes 786432 | tf_op jit(solution)/shard_map/all_to_all | solution.py:238
  119.6 9.9 %all-to-all-start.5 = ((bf16[16,8,128]{2,1,0:T(8,128)(2,1)}), bf16[16,8,128]{2,1,0:T(8,128)(2,1)S(1)}, u32[]{:S(2)}, u32[]{:S(2)}) async-start(bf16[16,8,128]{2,1,0:T(8,128)(2,1)} %relay_kernel.1), calls=%async_computation.5 | async-start | bytes 65536 | tf_op jit(solution)/shard_map/all_to_all | solution.py:238
  123.1 4.8 %collective-permute-start.8 = (bf16[8,1024]{1,0:T(8,128)(2,1)S(1)}, bf16[8,1024]{1,0:T(8,128)(2,1)S(1)}, u32[]{:S(2)}, u32[]{:S(2)}) collective-permute-start(bf16[8,1024]{1,0:T(8,128)(2,1)S(1)} %get-tuple-element.20.even_ref), channel_id=1, source_target_pairs={{1,0},{3,2},{5,4},{7,6},{9,8},{11,10},{13,12},{15,14},{17,16},{19,... | collective-permute-start | bytes 49160 | tf_op jit(solution)/shard_map/ppermute | solution.py:278
  (2 other events, 3.5 us)

commit v2 on v1

--- a/solution.py
+++ b/solution.py
@@ -36,13 +36,19 @@
     return total
 
 
-def call(kernel, outs, args, smem=(), scratch=(), limit=8):
+def call(kernel, outs, args, smem=(), hbm=(), keep=(), scratch=(), limit=8):
     vm = pl.BlockSpec(memory_space=pltpu.VMEM)
     sm = pl.BlockSpec(memory_space=pltpu.SMEM)
+    far_away = pl.BlockSpec(memory_space=pltpu.HBM)
     return pl.pallas_call(
         kernel,
-        out_shape=tuple(jax.ShapeDtypeStruct(s, d) for s, d in outs),
-        in_specs=[sm if at in smem else vm for at in range(len(args))],
+        out_shape=tuple(
+            pltpu.VMEM(s, d) if at in keep else jax.ShapeDtypeStruct(s, d)
+            for at, (s, d) in enumerate(outs)
+        ),
+        in_specs=[
+            sm if at in smem else far_away if at in hbm else vm for at in range(len(args))
+        ],
         out_specs=tuple(vm for _ in outs),
         scratch_shapes=list(scratch),
         compiler_params=pltpu.CompilerParams(vmem_limit_bytes=limit * MIB),
@@ -57,28 +63,38 @@
     peers = all_cols // cols
     wide = cols * slots
     n_row = lax.axis_size("row")
+    devices = n_row * peers
     tall = cols * dens
     blocks = far_blocks.shape[0]
 
-    def in_vmem(x):
-        return pltpu.with_memory_space_constraint(x, pltpu.VMEM)
-
-    u_all = in_vmem(u_factors.reshape(all_cols * slots, patch))
-    v_all = in_vmem(v_factors.reshape(rows * wide, patch))
-    far_all = in_vmem(far_blocks)
-    bound = jnp.repeat(
-        (ranks + slots * jnp.arange(cols, dtype=jnp.int32)[None, :]).T, dens, axis=0
-    )
-
+    u_flat = pltpu.with_memory_space_constraint(
+        u_factors.reshape(all_cols * slots, patch), pltpu.HBM
+    )
+    v_all = pltpu.with_memory_space_constraint(v_factors.reshape(rows * wide, patch), pltpu.VMEM)
+    far_all = pltpu.with_memory_space_constraint(far_blocks, pltpu.VMEM)
+    parts = 8
     def kept_lanes(bound_ref, row_patch):
         lane = lax.broadcasted_iota(jnp.int32, (tall, wide), 1)
         first = lax.broadcasted_iota(jnp.int32, (tall, wide), 0) // dens * slots
-        return (lane >= first) & (lane < bound_ref[:, row_patch : row_patch + 1])
-
-    def back_kernel(res_ref, u_ref, out_ref):
-        back = dot_nt(res_ref[...].astype(BF16), u_ref[...])
-        for peer in range(peers):
-            out_ref[peer] = back[:, peer * wide : (peer + 1) * wide].astype(BF16)
+        at = lane - first
+        return (at >= 0) & (at < bound_ref[:, row_patch : row_patch + 1])
+
+    def back_kernel(res_hbm, u_hbm, out_ref, u_ref, res_ref, sems):
+        share = u_flat.shape[0] // parts
+        each = peers // parts
+        copies = [pltpu.make_async_copy(res_hbm, res_ref, sems.at[parts])]
+        for part in range(parts):
+            at = pl.ds(part * share, share)
+            copies.append(pltpu.make_async_copy(u_hbm.at[at], u_ref.at[at], sems.at[part]))
+        for copy in copies:
+            copy.start()
+        copies[0].wait()
+        half = res_ref[...].astype(BF16)
+        for part in range(parts):
+            copies[part + 1].wait()
+            back = dot_nt(half, u_ref[part * share : (part + 1) * share, :])
+            for k in range(each):
+                out_ref[part * each + k] = back[:, k * wide : (k + 1) * wide].astype(BF16)
 
     def fill_left(in_ref, bound_ref, left_ref):
         for i in range(rows):
@@ -166,11 +182,11 @@
         second_ref[...] = second
         coefficients(second, bound_ref, v_ref, out_ref)
         mine = spread(norm_of(second))
-        first_row = jnp.concatenate([first[j * dens : (j + 1) * dens] for j in range(cols)], axis=1)
-        second_row = jnp.concatenate(
-            [second[j * dens : (j + 1) * dens] for j in range(cols)], axis=1
-        )
-        left = jnp.concatenate([first_row, second_row], axis=0).astype(BF16)
+        lines = [
+            jnp.concatenate([x[j * dens : (j + 1) * dens] for j in range(cols)], axis=1)
+            for x in (first, second)
+        ]
+        left = jnp.concatenate(lines, axis=0).astype(BF16)
         even = dot_nt(left, far_ref[0])
         odd = dot_nt(left, far_ref[1])
         even_ref[...] = jnp.concatenate([even[0:dens], even[dens : 2 * dens]], axis=1).astype(BF16)
@@ -179,32 +195,50 @@
             out_ref[i, :, wide : wide + 128] = mine
             out_ref[i, :, far_low : far_low + 2 * patch] = send
 
-    def image_far_kernel(route_ref, even_ref, in_ref, u_ref, image_ref, gsq_ref, out_ref):
+    def image_last_kernel(in_ref, u_ref, image_ref, gsq_ref, out_ref):
         image = image_of(in_ref, u_ref)
         image_ref[...] = image
         gsq_ref[...] = jnp.broadcast_to(
             jnp.sum(gather_sum(in_ref, wide, 128), axis=1, keepdims=True), (dens, 128)
         )
-        mine = spread(norm_of(image))
-        for target in range(n_row):
-            total = even_ref[...].astype(F32) * route_ref[target, peers]
+        here = lax.broadcasted_iota(jnp.int32, (dens, 128), 0) == lax.broadcasted_iota(
+            jnp.int32, (dens, 128), 1
+        )
+        line = jnp.sum(jnp.where(here, norm_of(image), 0.0), axis=0, keepdims=True)
+        for peer in range(devices):
+            out_ref[peer] = line
+
+    def route_kernel(target_ref, order_ref, even_ref, in_ref, keep_ref, give_ref):
+        row, col = lax.axis_index("row"), lax.axis_index("col")
+        for m in range(n_row):
+            mine = order_ref[lax.bitwise_xor(row, m) * peers + col]
+            total = jnp.zeros((dens, 2 * patch), F32)
+            if m == n_row // 2:
+                total = even_ref[...].astype(F32) * jnp.where(col % 2 == 0, 1.0, 0.0)
             for source in range(peers):
-                total = total + in_ref[source, :, far_low : far_low + 2 * patch].astype(
-                    F32
-                ) * route_ref[target, source]
-            out_ref[target, :, 0 : 2 * patch] = total.astype(BF16)
-            out_ref[target, :, 2 * patch : 2 * patch + 128] = mine
-
-    def relay_kernel(in_ref, out_ref):
-        mine = spread(jnp.sum(gather_sum(in_ref, 2 * patch, 128), axis=1, keepdims=True))
-        for peer in range(peers):
-            out_ref[peer] = mine
+                hit = jnp.where(target_ref[row * blocks + 1, source] == mine, 1.0, 0.0)
+                piece = in_ref[source, :, far_low : far_low + 2 * patch].astype(F32)
+                total = total + piece * hit
+            out_ref = keep_ref if m % 2 == 0 else give_ref
+            out_ref[m // 2] = total.astype(BF16)
+
+    def pair_kernel(own_ref, other_ref, out_ref):
+        out_ref[0:tall, :] = (own_ref[0:tall] + other_ref[0:tall]).astype(BF16)
+        low = slice(tall, tall + dens)
+        out_ref[low, 0:128] = spread(own_ref[low, 0:1] + other_ref[low, 0:1])
+        out_ref[low, 128:patch] = jnp.zeros((dens, patch - 128), BF16)
 
     def finish_kernel(
         norm_ref, gsq_ref, first_ref, second_ref, res_ref, image1_ref, image2_ref, step_ref,
-        far_ref, side_ref, dens_ref, out_res_ref, out_far_ref,
+        f0_ref, f2_ref, f4_ref, f6_ref, side_ref, dens_ref, out_res_ref, out_far_ref,
     ):
-        isq = jnp.sum(gather_sum(norm_ref, 0, 128), axis=1, keepdims=True)
+        line = norm_ref[0]
+        for source in range(1, devices):
+            line = line + norm_ref[source]
+        here = lax.broadcasted_iota(jnp.int32, (dens, 128), 0) == lax.broadcasted_iota(
+            jnp.int32, (dens, 128), 1
+        )
+        isq = jnp.sum(jnp.where(here, line, 0.0), axis=1, keepdims=True)
         step = gsq_ref[:, 0:1] / (isq + 1e-6)
         for j in range(cols):
             at = slice(j * dens, (j + 1) * dens)
@@ -212,41 +246,42 @@
         out_res_ref[...] = (
             res_ref[...] - step_ref[:, 0:1] * image1_ref[...] - step * image2_ref[...]
         )
-        both = gather_sum(far_ref, 0, 2 * patch) + side_ref[...].astype(F32)
+        both = side_ref[...].astype(F32)
+        for ref in (f0_ref, f2_ref, f4_ref, f6_ref):
+            both = both + ref[...].astype(F32)
         field = both[:, 0:patch] + step * both[:, patch : 2 * patch]
         for d in range(dens):
             out_far_ref[:, d * patch : (d + 1) * patch] = field[d : d + 1]
 
+    def row_shift(x, k):
+        return lax.ppermute(x, "row", [(i, i ^ k) for i in range(n_row)])
+
     def over_rows(part):
-        pair = part + lax.ppermute(part, "row", [(i, i ^ 1) for i in range(n_row)])
-        if pair.shape[0] > tall:
-            high = lax.reduce_precision(pair, 8, 7)
-            rest = pair - high
-            mid = lax.reduce_precision(rest, 8, 7)
-            row = lax.broadcasted_iota(jnp.int32, pair.shape, 0)
-            lane = lax.broadcasted_iota(jnp.int32, pair.shape, 1)
-            terms = jnp.where(
-                lane == 0, high, jnp.where(lane == 1, mid, jnp.where(lane == 2, rest - mid, 0.0))
-            )
-            pair = jnp.where(row < tall, pair, terms)
-        half = lax.optimization_barrier(pair.astype(BF16))
-        return [half] + [
-            lax.ppermute(half, "row", [(i, i ^ k) for i in range(n_row)]) for k in (2, 4, 6)
-        ]
+        other = row_shift(part, 1)
+        if part.shape[0] > tall:
+            (half,) = call(pair_kernel, [(part.shape, BF16)], [part, other])
+        else:
+            half = (part + other).astype(BF16)
+        half = lax.optimization_barrier(half)
+        return [half] + [row_shift(half, k) for k in (2, 4, 6)]
 
     def over_col(x):
         return lax.all_to_all(x, "col", split_axis=0, concat_axis=0, tiled=True)
 
-    me_row, me_col = lax.axis_index("row"), lax.axis_index("col")
-    odd_targets = lax.dynamic_slice(block_target, (me_row * blocks + 1, 0), (1, peers))
-    my_order = lax.dynamic_slice(recv_order.reshape(n_row, peers), (0, me_col), (n_row, 1))
-    partner = (jnp.arange(n_row) == (me_row + n_row // 2) % n_row) & (me_col % 2 == 0)
-    route = jnp.concatenate([my_order == odd_targets, partner[:, None]], axis=1).astype(F32)
-
     left_scratch = (pltpu.VMEM((tall, rows * wide), BF16),)
-    (sent,) = call(back_kernel, [((peers, dens, wide), BF16)], [right_side, u_all])
+    dma = pltpu.SemaphoreType.DMA
+    sent, u_all = call(
+        back_kernel,
+        [((peers, dens, wide), BF16), (u_flat.shape, BF16)],
+        [pltpu.with_memory_space_constraint(right_side, pltpu.HBM), u_flat],
+        hbm=(0, 1),
+        keep=(1,),
+        scratch=(pltpu.VMEM((dens, patch), F32), dma((parts + 1,))),
+    )
+    landed, known = lax.optimization_barrier((over_col(sent), ranks))
+    bound = jnp.repeat(known.T, dens, axis=0)
     (part,) = call(
-        grad_kernel, [((tall, patch), F32)], [over_col(sent), bound, v_all], scratch=left_scratch
+        grad_kernel, [((tall, patch), F32)], [landed, bound, v_all], scratch=left_scratch
     )
     sent, grad = call(
         coef_kernel,
@@ -275,19 +310,26 @@
         ],
         over_rows(part) + [grad, gsq1, bound, v_all, far_all],
     )
+    landed = over_col(sent)
+    image2, gsq2, sent = call(
+        image_last_kernel,
+        [((dens, patch), F32), ((dens, 128), F32), ((devices, 1, 128), F32)],
+        [landed, u_all],
+    )
+    norms = lax.all_to_all(sent, ("row", "col"), split_axis=0, concat_axis=0, tiled=True)
+    keep, give = call(
+        route_kernel,
+        [((n_row // 2, dens, 2 * patch), BF16)] * 2,
+        [block_target, recv_order, even, landed],
+        smem=(0, 1),
+    )
+    near = keep + row_shift(give, 1)
+    pieces = [near[0]] + [row_shift(near[k], 2 * k) for k in range(1, n_row // 2)]
     side = lax.ppermute(even, "col", [(c, c - 1) for c in range(1, peers, 2)])
-    image2, gsq2, sent = call(
-        image_far_kernel,
-        [((dens, patch), F32), ((dens, 128), F32), ((n_row, dens, 2 * patch + 128), BF16)],
-        [route, even, over_col(sent), u_all],
-        smem=(0,),
-    )
-    far_in = lax.all_to_all(sent, "row", split_axis=0, concat_axis=0, tiled=True)
-    (relayed,) = call(relay_kernel, [((peers, dens, 128), BF16)], [far_in])
     densities, residual, far_field = call(
         finish_kernel,
         [((dens, cols * patch), F32), ((dens, patch), F32), ((1, dens * patch), F32)],
-        [over_col(relayed), gsq2, first, second, right_side, image1, image2, step1, far_in, side],
+        [norms, gsq2, first, second, right_side, image1, image2, step1] + pieces + [side],
     )
     return densities, residual, far_field
 

time: 132 us -> 109 us (0.83)
  blocking collectives: 20.2 us -> 44.8 us
  waiting for transfers between devices: 36.7 us -> 14.7 us
  local copies, waits for them, and re-layouts: 18.3 us -> 0.05 us
  starting transfers between devices: 35.2 us -> 28 us
    all_to_all x1 -> x4, blocking collectives: 9.73 us -> 44.8 us  [over_col(): return lax.all_to_all(x, 'col', split_axis=0, concat_axis=0, tiled=True)]
    all_to_all x4 -> x1, waiting for transfers between devices: 23.7 us -> 5.5 us  [per_device(): lax.all_to_all(sent, ('row', 'col'), split_axis=0, concat_axis=0, tiled=T...]
    unnamed x26 -> x14, local copies, waits for them, and re-layouts: 18 us -> 0.04 us
    all_to_all x4 -> x1, starting transfers between devices: 18.3 us -> 5.16 us  [per_device(): lax.all_to_all(sent, ('row', 'col'), split_axis=0, concat_axis=0, tiled=T...]
    all_to_all x1 -> x0, blocking collectives: 10.5 us -> none  [per_device(): lax.all_to_all(sent, 'row', split_axis=0, concat_axis=0, tiled=True)]
    ppermute x8 -> x12, starting transfers between devices: 15.6 us -> 21.6 us  [row_shift(): return lax.ppermute(x, 'row', [(i, i ^ k) for i in range(n_row)])]
    ppermute x1, waiting for transfers between devices: 3.48 us -> 0.01 us  [per_device(): side = lax.ppermute(even, 'col', [(c, c - 1) for c in range(1, peers, 2)])]
    pallas_call x9 -> x10, Pallas kernels: 18.8 us -> 19.8 us  [call(): pl.pallas_call(kernel, out_shape=tuple((pltpu.VMEM(s, d) if at in keep el...]
  transfers between devices with their start and end apart: 13 -> 14, of which waited for: 11 -> 8; matrix products, arithmetic and copies ran while one was open for 0% -> 0% of each run, Pallas kernels for 0% -> 2%
where the time goes in v2:
time: 109 us; the launch traced here: 108 us
  blocking collectives  44.8 us (41%)
  starting transfers between devices  28 us (26%)
  Pallas kernels  19.8 us (18%)
  waiting for transfers between devices  14.7 us (13%)
    all_to_all x4, blocking collectives, over_col(): return lax.all_to_all(x, 'col', split_axis=0, concat_axis=0, tiled=True)  44.8 us
    ppermute x12, starting transfers between devices, row_shift(): return lax.ppermute(x, 'row', [(i, i ^ k) for i in range(n_row)])  21.6 us
    pallas_call x10, Pallas kernels, call(): pl.pallas_call(kernel, out_shape=tuple((pltpu.VMEM(s, d) if at in keep el...  19.8 us
    ppermute x12, waiting for transfers between devices, row_shift(): return lax.ppermute(x, 'row', [(i, i ^ k) for i in range(n_row)])  9.25 us
    all_to_all x1, waiting for transfers between devices, per_device(): lax.all_to_all(sent, ('row', 'col'), split_axis=0, concat_axis=0, tiled=T...  5.5 us
    all_to_all x1, starting transfers between devices, per_device(): lax.all_to_all(sent, ('row', 'col'), split_axis=0, concat_axis=0, tiled=T...  5.16 us
  transfers between devices with their start and end apart: 14, of which 8 were waited for; matrix products, arithmetic and copies ran while one was open for 0% of the time, Pallas kernels for 2%

profile of v2, /device:TPU:1, one launch (start us, length us, event | category | flops | bytes accessed | tf_op | source)
XLA Modules:
  0.0 108.2 jit_solution(14492581867334420619)
XLA Ops:
  0.7 4.5 %back_kernel.1 = (bf16[16,8,384]{2,1,0:T(8,128)(2,1)S(1)}, bf16[6144,512]{1,0:T(8,128)(2,1)S(1)}) custom-call(f32[8,512]{1,0:T(8,128)} %res_ref.1, bf16[6144,512]{1,0:T(8,128)(2,1)} %bitcast.20), custom_call_target="tpu_custom_call" | custom-call | tf_op jit(solution)/shard_map/back_kernel/pallas_call | solution.py:43
  5.1 14.1 %all_to_all.25.in_ref = bf16[16,8,384]{2,1,0:T(8,128)(2,1)S(1)} all-to-all(bf16[16,8,384]{2,1,0:T(8,128)(2,1)S(1)} %get-tuple-element.22), channel_id=1, replica_groups=mesh['row'=8,'col'=16] {'col'}, dimensions={0} | all-to-all | bytes 196608 | tf_op jit(solution)/shard_map/all_to_all | solution.py:269
  19.3 1.3 %grad_kernel.1 = f32[64,512]{1,0:T(8,128)S(1)} custom-call(bf16[16,8,384]{2,1,0:T(8,128)(2,1)S(1)} %all_to_all.25.in_ref, s32[64,16]{1,0:T(8,128)S(1)} %broadcast_bitcast_fusion.bound_ref, bf16[6144,512]{1,0:T(8,128)(2,1)S(1)} %bitcast.14), custom_call_target="tpu_custom_call" | custom-call | tf_op jit(solution)/shard_map/grad_kernel/pallas_call | solution.py:43
  20.5 2.1 %collective-permute-start = (f32[64,512]{1,0:T(8,128)S(1)}, f32[64,512]{1,0:T(8,128)S(1)}, u32[]{:S(2)}, u32[]{:S(2)}) collective-permute-start(f32[64,512]{1,0:T(8,128)S(1)} %grad_kernel.1), channel_id=1, source_target_pairs={{0,16},{16,0},{32,48},{48,32},{64,80},{80,64},{96,112},{112,96},{1... | collective-permute-start | bytes 393224 | tf_op jit(solution)/shard_map/ppermute | solution.py:257
  23.7 3.8 %collective-permute-start.3 = (bf16[64,512]{1,0:T(8,128)(2,1)S(1)}, bf16[64,512]{1,0:T(8,128)(2,1)S(1)}, u32[]{:S(2)}, u32[]{:S(2)}) collective-permute-start(bf16[64,512]{1,0:T(8,128)(2,1)S(1)} %add_convert_fusion.p0_ref), channel_id=1, source_target_pairs={{0,96},{16,112},{32,64},{48,80},{64,32},{80,48},{96,0},{112,16},{1... | collective-permute-start | bytes 196616 | tf_op jit(solution)/shard_map/ppermute | solution.py:257
  28.2 1.4 %collective-permute-done.3.p6_ref = bf16[64,512]{1,0:T(8,128)(2,1)S(1)} collective-permute-done((bf16[64,512]{1,0:T(8,128)(2,1)S(1)}, bf16[64,512]{1,0:T(8,128)(2,1)S(1)}, u32[]{:S(2)}, u32[]{:S(2)}) %collective-permute-start.3) | collective-permute-done | bytes 65568 | tf_op jit(solution)/shard_map/ppermute | solution.py:257
  29.6 2.5 %collective-permute-done.2.p4_ref = bf16[64,512]{1,0:T(8,128)(2,1)S(1)} collective-permute-done((bf16[64,512]{1,0:T(8,128)(2,1)S(1)}, bf16[64,512]{1,0:T(8,128)(2,1)S(1)}, u32[]{:S(2)}, u32[]{:S(2)}) %collective-permute-start.2) | collective-permute-done | bytes 65568 | tf_op jit(solution)/shard_map/ppermute | solution.py:257
  32.1 2.0 %coef_kernel.1 = (bf16[16,8,512]{2,1,0:T(8,128)(2,1)S(1)}, f32[64,512]{1,0:T(8,128)S(1)}) custom-call(bf16[64,512]{1,0:T(8,128)(2,1)S(1)} %add_convert_fusion.p0_ref, bf16[64,512]{1,0:T(8,128)(2,1)S(1)} %collective-permute-done.1.p2_ref, bf16[64,512]{1,0:T(8,128)(2,1)S(1)} %collective-permute-done.2.p4_ref, ...), custom_call_target="tpu_custom_call" | custom-call | tf_op jit(solution)/shard_map/coef_kernel/pallas_call | solution.py:43
  34.2 9.7 %all_to_all.26.in_ref = bf16[16,8,512]{2,1,0:T(8,128)(2,1)S(1)} all-to-all(bf16[16,8,512]{2,1,0:T(8,128)(2,1)S(1)} %get-tuple-element.25), channel_id=1, replica_groups=mesh['row'=8,'col'=16] {'col'}, dimensions={0} | all-to-all | bytes 262144 | tf_op jit(solution)/shard_map/all_to_all | solution.py:269
  43.8 2.6 %image_back_kernel.1 = (f32[8,512]{1,0:T(8,128)S(1)}, f32[8,128]{1,0:T(8,128)S(1)}, bf16[16,8,512]{2,1,0:T(8,128)(2,1)S(1)}) custom-call(bf16[16,8,512]{2,1,0:T(8,128)(2,1)S(1)} %all_to_all.26.in_ref, bf16[6144,512]{1,0:T(8,128)(2,1)S(1)} %get-tuple-element.26.u_ref), custom_call_target="tpu_custom_call" | custom-call | tf_op jit(solution)/shard_map/image_back_kernel/pallas_call | solution.py:43
  46.4 9.9 %all_to_all.27.in_ref = bf16[16,8,512]{2,1,0:T(8,128)(2,1)S(1)} all-to-all(bf16[16,8,512]{2,1,0:T(8,128)(2,1)S(1)} %get-tuple-element.27), channel_id=1, replica_groups=mesh['row'=8,'col'=16] {'col'}, dimensions={0} | all-to-all | bytes 262144 | tf_op jit(solution)/shard_map/all_to_all | solution.py:269
  56.4 1.3 %grad_norm_kernel.1.own_ref = f32[72,512]{1,0:T(8,128)S(1)} custom-call(bf16[16,8,512]{2,1,0:T(8,128)(2,1)S(1)} %all_to_all.27.in_ref, s32[64,16]{1,0:T(8,128)S(1)} %broadcast_bitcast_fusion.bound_ref, bf16[6144,512]{1,0:T(8,128)(2,1)S(1)} %bitcast.16), custom_call_target="tpu_custom_call" | custom-call | tf_op jit(solution)/shard_map/grad_norm_kernel/pallas_call | solution.py:43
  57.6 4.7 %collective-permute-start.4 = (f32[72,512]{1,0:T(8,128)S(1)}, f32[72,512]{1,0:T(8,128)S(1)}, u32[]{:S(2)}, u32[]{:S(2)}) collective-permute-start(f32[72,512]{1,0:T(8,128)S(1)} %grad_norm_kernel.1.own_ref), channel_id=1, source_target_pairs={{0,16},{16,0},{32,48},{48,32},{64,80},{80,64},{96,112},{112,96},{1... | collective-permute-start | bytes 442376 | tf_op jit(solution)/shard_map/ppermute | solution.py:257
  65.0 1.7 %collective-permute-start.5 = (bf16[72,512]{1,0:T(8,128)(2,1)S(1)}, bf16[72,512]{1,0:T(8,128)(2,1)S(1)}, u32[]{:S(2)}, u32[]{:S(2)}) collective-permute-start(bf16[72,512]{1,0:T(8,128)(2,1)S(1)} %pair_kernel.1.p0_ref), channel_id=1, source_target_pairs={{0,32},{16,48},{32,0},{48,16},{64,96},{80,112},{96,64},{112,80},{1... | collective-permute-start | bytes 221192 | tf_op jit(solution)/shard_map/ppermute | solution.py:257
  66.8 1.2 %collective-permute-done.7.p6_ref = bf16[72,512]{1,0:T(8,128)(2,1)S(1)} collective-permute-done((bf16[72,512]{1,0:T(8,128)(2,1)S(1)}, bf16[72,512]{1,0:T(8,128)(2,1)S(1)}, u32[]{:S(2)}, u32[]{:S(2)}) %collective-permute-start.7) | collective-permute-done | bytes 73760 | tf_op jit(solution)/shard_map/ppermute | solution.py:257
  67.9 1.4 %collective-permute-done.6.p4_ref = bf16[72,512]{1,0:T(8,128)(2,1)S(1)} collective-permute-done((bf16[72,512]{1,0:T(8,128)(2,1)S(1)}, bf16[72,512]{1,0:T(8,128)(2,1)S(1)}, u32[]{:S(2)}, u32[]{:S(2)}) %collective-permute-start.6) | collective-permute-done | bytes 73760 | tf_op jit(solution)/shard_map/ppermute | solution.py:257
  70.1 4.3 %coef_far_kernel.1 = (bf16[16,8,1536]{2,1,0:T(8,128)(2,1)S(1)}, f32[64,512]{1,0:T(8,128)S(1)}, f32[64,512]{1,0:T(8,128)S(1)}, f32[8,128]{1,0:T(8,128)S(1)}, bf16[8,1024]{1,0:T(8,128)(2,1)S(1)}) custom-call(bf16[72,512]{1,0:T(8,128)(2,1)S(1)} %pair_kernel.1.p0_ref, bf16[72,512]{1,0:T(8,128)(2,1)S(1)} %collective-permute-done.5.p2_ref, ...), custom_call_target="tpu_custom_call" | custom-call | tf_op jit(solution)/shard_map/coef_far_kernel/pallas_call | solution.py:43
  74.4 11.1 %all_to_all.28.in_ref = bf16[16,8,1536]{2,1,0:T(8,128)(2,1)S(1)} all-to-all(bf16[16,8,1536]{2,1,0:T(8,128)(2,1)S(1)} %get-tuple-element.30), channel_id=1, replica_groups=mesh['row'=8,'col'=16] {'col'}, dimensions={0} | all-to-all | bytes 786432 | tf_op jit(solution)/shard_map/all_to_all | solution.py:269
  86.6 3.0 %collective-permute-start.8 = (bf16[4,8,1024]{2,1,0:T(8,128)(2,1)S(1)}, bf16[4,8,1024]{2,1,0:T(8,128)(2,1)S(1)}, u32[]{:S(2)}, u32[]{:S(2)}) collective-permute-start(bf16[4,8,1024]{2,1,0:T(8,128)(2,1)S(1)} %get-tuple-element.40), channel_id=1, source_target_pairs={{0,16},{16,0},{32,48},{48,32},{64,80},{80,64},{96,112},{112,96},{1... | collective-permute-start | bytes 196616 | tf_op jit(solution)/shard_map/ppermute | solution.py:257
  89.6 1.3 %collective-permute-start.12 = (bf16[8,1024]{1,0:T(8,128)(2,1)S(1)}, bf16[8,1024]{1,0:T(8,128)(2,1)S(1)}, u32[]{:S(2)}, u32[]{:S(2)}) collective-permute-start(bf16[8,1024]{1,0:T(8,128)(2,1)S(1)} %get-tuple-element.38.even_ref), channel_id=1, source_target_pairs={{1,0},{3,2},{5,4},{7,6},{9,8},{11,10},{13,12},{15,14},{17,16},{19,... | collective-permute-start | bytes 49160 | tf_op jit(solution)/shard_map/ppermute | solution.py:328
  90.9 1.7 %image_last_kernel.1 = (f32[8,512]{1,0:T(8,128)S(1)}, f32[8,128]{1,0:T(8,128)S(1)}, f32[128,1,128]{2,1,0:T(1,128)}) custom-call(bf16[16,8,1536]{2,1,0:T(8,128)(2,1)S(1)} %all_to_all.28.in_ref, bf16[6144,512]{1,0:T(8,128)(2,1)S(1)} %get-tuple-element.26.u_ref), custom_call_target="tpu_custom_call" | custom-call | tf_op jit(solution)/shard_map/image_last_kernel/pallas_call | solution.py:43
  92.5 5.2 %all-to-all-start.4 = ((f32[128,1,128]{2,1,0:T(1,128)}), f32[128,1,128]{2,1,0:T(1,128)S(1)}, u32[]{:S(2)}, u32[]{:S(2)}) async-start(f32[128,1,128]{2,1,0:T(1,128)} %get-tuple-element.31), calls=%async_computation.4 | async-start | bytes 131072 | tf_op jit(solution)/shard_map/all_to_all | solution.py:319
  97.7 3.3 %collective-permute-start.11 = (bf16[8,1024]{1,0:T(8,128)(2,1)S(1)}, bf16[8,1024]{1,0:T(8,128)(2,1)S(1)}, u32[]{:S(2)}, u32[]{:S(2)}) collective-permute-start(bf16[8,1024]{1,0:T(8,128)(2,1)S(1)} %get-tuple-element.41), channel_id=1, source_target_pairs={{0,96},{16,112},{32,64},{48,80},{64,32},{80,48},{96,0},{112,16},{1... | collective-permute-start | bytes 49160 | tf_op jit(solution)/shard_map/ppermute | solution.py:257
  101.7 5.5 %all-to-all-done.4.norm_ref = f32[128,1,128]{2,1,0:T(1,128)S(1)} async-done(((f32[128,1,128]{2,1,0:T(1,128)}), f32[128,1,128]{2,1,0:T(1,128)S(1)}, u32[]{:S(2)}, u32[]{:S(2)}) %all-to-all-start.4) | async-done | bytes 65568 | tf_op jit(solution)/shard_map/all_to_all | solution.py:319
  (37 shorter events, 7.9 us)
Async XLA Ops:
  0.6 18.6 %copy-start = (s32[16,8]{0,1:T(8,128)S(1)}, s32[16,8]{0,1:T(8,128)}, u32[]{:S(2)}) copy-start(s32[16,8]{0,1:T(8,128)} %param.10) | copy-start | bytes 1540
  0.6 18.6 %copy-start.1 = (bf16[16,8,48,512]{3,2,1,0:T(8,128)(2,1)S(1)}, bf16[16,8,48,512]{3,2,1,0:T(8,128)(2,1)}, u32[]{:S(2)}) copy-start(bf16[16,8,48,512]{3,2,1,0:T(8,128)(2,1)} %param.9) | copy-start | bytes 18874372
  20.5 3.1 %collective-permute-start = (f32[64,512]{1,0:T(8,128)S(1)}, f32[64,512]{1,0:T(8,128)S(1)}, u32[]{:S(2)}, u32[]{:S(2)}) collective-permute-start(f32[64,512]{1,0:T(8,128)S(1)} %grad_kernel.1), channel_id=1, source_target_pairs={{0,16},{16,0},{32,48},{48,32},{64,80},{80,64},{96,112},{112,96},{1... | collective-permute-start | bytes 393224 | tf_op jit(solution)/shard_map/ppermute | solution.py:257
  23.7 5.9 %collective-permute-start.3 = (bf16[64,512]{1,0:T(8,128)(2,1)S(1)}, bf16[64,512]{1,0:T(8,128)(2,1)S(1)}, u32[]{:S(2)}, u32[]{:S(2)}) collective-permute-start(bf16[64,512]{1,0:T(8,128)(2,1)S(1)} %add_convert_fusion.p0_ref), channel_id=1, source_target_pairs={{0,96},{16,112},{32,64},{48,80},{64,32},{80,48},{96,0},{112,16},{1... | collective-permute-start | bytes 196616 | tf_op jit(solution)/shard_map/ppermute | solution.py:257
  27.5 4.6 %collective-permute-start.2 = (bf16[64,512]{1,0:T(8,128)(2,1)S(1)}, bf16[64,512]{1,0:T(8,128)(2,1)S(1)}, u32[]{:S(2)}, u32[]{:S(2)}) collective-permute-start(bf16[64,512]{1,0:T(8,128)(2,1)S(1)} %add_convert_fusion.p0_ref), channel_id=1, source_target_pairs={{0,64},{16,80},{32,96},{48,112},{64,0},{80,16},{96,32},{112,48},{1... | collective-permute-start | bytes 196616 | tf_op jit(solution)/shard_map/ppermute | solution.py:257
  27.5 4.6 %collective-permute-start.1 = (bf16[64,512]{1,0:T(8,128)(2,1)S(1)}, bf16[64,512]{1,0:T(8,128)(2,1)S(1)}, u32[]{:S(2)}, u32[]{:S(2)}) collective-permute-start(bf16[64,512]{1,0:T(8,128)(2,1)S(1)} %add_convert_fusion.p0_ref), channel_id=1, source_target_pairs={{0,32},{16,48},{32,0},{48,16},{64,96},{80,112},{96,64},{112,80},{1... | collective-permute-start | bytes 196616 | tf_op jit(solution)/shard_map/ppermute | solution.py:257
  32.1 37.9 %slice-start = ((s8[8388608]{0:T(1024)(128)(4,1)}), s8[4194304]{0:T(1024)(128)(4,1)S(1)}, s32[]{:S(2)}) async-start(s8[8388608]{0:T(1024)(128)(4,1)} %bitcast.18), calls=%async_computation.5 | async-start | bytes 8388608
  43.8 26.2 %slice-start.1 = ((s8[8388608]{0:T(1024)(128)(4,1)}), s8[4194304]{0:T(1024)(128)(4,1)S(1)}, s32[]{:S(2)}) async-start(s8[8388608]{0:T(1024)(128)(4,1)} %bitcast.18), calls=%async_computation.6 | async-start | bytes 8388608
  57.6 5.7 %collective-permute-start.4 = (f32[72,512]{1,0:T(8,128)S(1)}, f32[72,512]{1,0:T(8,128)S(1)}, u32[]{:S(2)}, u32[]{:S(2)}) collective-permute-start(f32[72,512]{1,0:T(8,128)S(1)} %grad_norm_kernel.1.own_ref), channel_id=1, source_target_pairs={{0,16},{16,0},{32,48},{48,32},{64,80},{80,64},{96,112},{112,96},{1... | collective-permute-start | bytes 442376 | tf_op jit(solution)/shard_map/ppermute | solution.py:257
  63.5 4.4 %collective-permute-start.7 = (bf16[72,512]{1,0:T(8,128)(2,1)S(1)}, bf16[72,512]{1,0:T(8,128)(2,1)S(1)}, u32[]{:S(2)}, u32[]{:S(2)}) collective-permute-start(bf16[72,512]{1,0:T(8,128)(2,1)S(1)} %pair_kernel.1.p0_ref), channel_id=1, source_target_pairs={{0,96},{16,112},{32,64},{48,80},{64,32},{80,48},{96,0},{112,16},{1... | collective-permute-start | bytes 221192 | tf_op jit(solution)/shard_map/ppermute | solution.py:257
  64.5 4.8 %collective-permute-start.6 = (bf16[72,512]{1,0:T(8,128)(2,1)S(1)}, bf16[72,512]{1,0:T(8,128)(2,1)S(1)}, u32[]{:S(2)}, u32[]{:S(2)}) collective-permute-start(bf16[72,512]{1,0:T(8,128)(2,1)S(1)} %pair_kernel.1.p0_ref), channel_id=1, source_target_pairs={{0,64},{16,80},{32,96},{48,112},{64,0},{80,16},{96,32},{112,48},{1... | collective-permute-start | bytes 221192 | tf_op jit(solution)/shard_map/ppermute | solution.py:257
  65.0 5.0 %collective-permute-start.5 = (bf16[72,512]{1,0:T(8,128)(2,1)S(1)}, bf16[72,512]{1,0:T(8,128)(2,1)S(1)}, u32[]{:S(2)}, u32[]{:S(2)}) collective-permute-start(bf16[72,512]{1,0:T(8,128)(2,1)S(1)} %pair_kernel.1.p0_ref), channel_id=1, source_target_pairs={{0,32},{16,48},{32,0},{48,16},{64,96},{80,112},{96,64},{112,80},{1... | collective-permute-start | bytes 221192 | tf_op jit(solution)/shard_map/ppermute | solution.py:257
  70.1 15.4 %copy-start.3 = (s32[16,16]{1,0:T(8,128)S(1)}, s32[16,16]{1,0:T(8,128)}, u32[]{:S(2)}) copy-start(s32[16,16]{1,0:T(8,128)} %target_ref.1) | copy-start | bytes 3076
  70.1 15.4 %copy-start.4 = (s32[128]{0:T(128)S(1)}, s32[128]{0:T(128)}, u32[]{:S(2)}) copy-start(s32[128]{0:T(128)} %order_ref.1) | copy-start | bytes 1540
  74.4 32.9 %copy-start.2 = (f32[8,512]{1,0:T(8,128)S(1)}, f32[8,512]{1,0:T(8,128)}, u32[]{:S(2)}) copy-start(f32[8,512]{1,0:T(8,128)} %res_ref.1) | copy-start | bytes 49156
  86.6 11.1 %collective-permute-start.8 = (bf16[4,8,1024]{2,1,0:T(8,128)(2,1)S(1)}, bf16[4,8,1024]{2,1,0:T(8,128)(2,1)S(1)}, u32[]{:S(2)}, u32[]{:S(2)}) collective-permute-start(bf16[4,8,1024]{2,1,0:T(8,128)(2,1)S(1)} %get-tuple-element.40), channel_id=1, source_target_pairs={{0,16},{16,0},{32,48},{48,32},{64,80},{80,64},{96,112},{112,96},{1... | collective-permute-start | bytes 196616 | tf_op jit(solution)/shard_map/ppermute | solution.py:257
  89.6 12.2 %collective-permute-start.12 = (bf16[8,1024]{1,0:T(8,128)(2,1)S(1)}, bf16[8,1024]{1,0:T(8,128)(2,1)S(1)}, u32[]{:S(2)}, u32[]{:S(2)}) collective-permute-start(bf16[8,1024]{1,0:T(8,128)(2,1)S(1)} %get-tuple-element.38.even_ref), channel_id=1, source_target_pairs={{1,0},{3,2},{5,4},{7,6},{9,8},{11,10},{13,12},{15,14},{17,16},{19,... | collective-permute-start | bytes 49160 | tf_op jit(solution)/shard_map/ppermute | solution.py:328
  92.5 14.7 %all-to-all-start.4 = ((f32[128,1,128]{2,1,0:T(1,128)}), f32[128,1,128]{2,1,0:T(1,128)S(1)}, u32[]{:S(2)}, u32[]{:S(2)}) async-start(f32[128,1,128]{2,1,0:T(1,128)} %get-tuple-element.31), calls=%async_computation.4 | async-start | bytes 131072 | tf_op jit(solution)/shard_map/all_to_all | solution.py:319
  97.7 9.5 %collective-permute-start.11 = (bf16[8,1024]{1,0:T(8,128)(2,1)S(1)}, bf16[8,1024]{1,0:T(8,128)(2,1)S(1)}, u32[]{:S(2)}, u32[]{:S(2)}) collective-permute-start(bf16[8,1024]{1,0:T(8,128)(2,1)S(1)} %get-tuple-element.41), channel_id=1, source_target_pairs={{0,96},{16,112},{32,64},{48,80},{64,32},{80,48},{96,0},{112,16},{1... | collective-permute-start | bytes 49160 | tf_op jit(solution)/shard_map/ppermute | solution.py:257
  101.1 6.2 %collective-permute-start.10 = (bf16[8,1024]{1,0:T(8,128)(2,1)S(1)}, bf16[8,1024]{1,0:T(8,128)(2,1)S(1)}, u32[]{:S(2)}, u32[]{:S(2)}) collective-permute-start(bf16[8,1024]{1,0:T(8,128)(2,1)S(1)} %get-tuple-element.42), channel_id=1, source_target_pairs={{0,64},{16,80},{32,96},{48,112},{64,0},{80,16},{96,32},{112,48},{1... | collective-permute-start | bytes 49160 | tf_op jit(solution)/shard_map/ppermute | solution.py:257
  101.2 6.1 %collective-permute-start.9 = (bf16[8,1024]{1,0:T(8,128)(2,1)S(1)}, bf16[8,1024]{1,0:T(8,128)(2,1)S(1)}, u32[]{:S(2)}, u32[]{:S(2)}) collective-permute-start(bf16[8,1024]{1,0:T(8,128)(2,1)S(1)} %get-tuple-element.43), channel_id=1, source_target_pairs={{0,32},{16,48},{32,0},{48,16},{64,96},{80,112},{96,64},{112,80},{1... | collective-permute-start | bytes 49160 | tf_op jit(solution)/shard_map/ppermute | solution.py:257

commit v3 on v2

--- a/solution.py
+++ b/solution.py
@@ -4,6 +4,7 @@
 from jax.experimental import pallas as pl
 from jax.experimental.pallas import tpu as pltpu
 from jax.sharding import PartitionSpec as P
+
 
 F32, BF16 = jnp.float32, jnp.bfloat16
 MIB = 1 << 20
@@ -52,7 +53,6 @@
         out_specs=tuple(vm for _ in outs),
         scratch_shapes=list(scratch),
         compiler_params=pltpu.CompilerParams(vmem_limit_bytes=limit * MIB),
-        name=kernel.__name__,
     )(*args)
 
 
@@ -70,9 +70,9 @@
     u_flat = pltpu.with_memory_space_constraint(
         u_factors.reshape(all_cols * slots, patch), pltpu.HBM
     )
-    v_all = pltpu.with_memory_space_constraint(v_factors.reshape(rows * wide, patch), pltpu.VMEM)
     far_all = pltpu.with_memory_space_constraint(far_blocks, pltpu.VMEM)
     parts = 8
+
     def kept_lanes(bound_ref, row_patch):
         lane = lax.broadcasted_iota(jnp.int32, (tall, wide), 1)
         first = lax.broadcasted_iota(jnp.int32, (tall, wide), 0) // dens * slots
@@ -246,7 +246,7 @@
         out_res_ref[...] = (
             res_ref[...] - step_ref[:, 0:1] * image1_ref[...] - step * image2_ref[...]
         )
-        both = side_ref[...].astype(F32)
+        both = side_ref[...].astype(F32) * jnp.where(lax.axis_index("col") % 2 == 0, 1.0, 0.0)
         for ref in (f0_ref, f2_ref, f4_ref, f6_ref):
             both = both + ref[...].astype(F32)
         field = both[:, 0:patch] + step * both[:, patch : 2 * patch]
@@ -278,6 +278,8 @@
         keep=(1,),
         scratch=(pltpu.VMEM((dens, patch), F32), dma((parts + 1,))),
     )
+    sent, v_flat = lax.optimization_barrier((sent, v_factors.reshape(rows * wide, patch)))
+    v_all = pltpu.with_memory_space_constraint(v_flat, pltpu.VMEM)
     landed, known = lax.optimization_barrier((over_col(sent), ranks))
     bound = jnp.repeat(known.T, dens, axis=0)
     (part,) = call(
@@ -317,6 +319,7 @@
         [landed, u_all],
     )
     norms = lax.all_to_all(sent, ("row", "col"), split_axis=0, concat_axis=0, tiled=True)
+    even, landed, image2 = lax.optimization_barrier((even, landed, image2))
     keep, give = call(
         route_kernel,
         [((n_row // 2, dens, 2 * patch), BF16)] * 2,
@@ -325,7 +328,7 @@
     )
     near = keep + row_shift(give, 1)
     pieces = [near[0]] + [row_shift(near[k], 2 * k) for k in range(1, n_row // 2)]
-    side = lax.ppermute(even, "col", [(c, c - 1) for c in range(1, peers, 2)])
+    side = lax.ppermute(even, "col", [(c, c ^ 1) for c in range(peers)])
     densities, residual, far_field = call(
         finish_kernel,
         [((dens, cols * patch), F32), ((dens, patch), F32), ((1, dens * patch), F32)],

time: 109 us -> 107 us (0.982)
  starting transfers between devices: 28 us -> 26.9 us
  transfers between devices with their start and end apart: 14 -> 14, of which waited for: 8 -> 8; matrix products, arithmetic and copies ran while one was open for 0% -> 0% of each run, Pallas kernels for 2% -> 0%
where the time goes in v3:
time: 107 us
  blocking collectives  44.9 us (42%)
  starting transfers between devices  26.9 us (25%)
  Pallas kernels  19.8 us (19%)
  waiting for transfers between devices  14.7 us (14%)
    all_to_all x4, blocking collectives, over_col(): return lax.all_to_all(x, 'col', split_axis=0, concat_axis=0, tiled=True)  44.9 us
    ppermute x12, starting transfers between devices, row_shift(): return lax.ppermute(x, 'row', [(i, i ^ k) for i in range(n_row)])  21.6 us
    pallas_call x10, Pallas kernels, call(): pl.pallas_call(kernel, out_shape=tuple((pltpu.VMEM(s, d) if at in keep el...  19.8 us
    ppermute x12, waiting for transfers between devices, row_shift(): return lax.ppermute(x, 'row', [(i, i ^ k) for i in range(n_row)])  9.25 us
    all_to_all x1, waiting for transfers between devices, per_device(): lax.all_to_all(sent, ('row', 'col'), split_axis=0, concat_axis=0, tiled=T...  5.5 us
    all_to_all x1, starting transfers between devices, per_device(): lax.all_to_all(sent, ('row', 'col'), split_axis=0, concat_axis=0, tiled=T...  4.99 us
  transfers between devices with their start and end apart: 14, of which 8 were waited for; matrix products, arithmetic and copies ran while one was open for 0% of the time, Pallas kernels for 0%

profile of v3, /device:TPU:1, one launch (start us, length us, event | category | flops | bytes accessed | tf_op | source)
XLA Modules:
  0.0 107.2 jit_solution(14924352662557843900)
XLA Ops:
  0.7 4.5 %shard_map.94 = (bf16[16,8,384]{2,1,0:T(8,128)(2,1)S(1)}, bf16[6144,512]{1,0:T(8,128)(2,1)S(1)}) custom-call(f32[8,512]{1,0:T(8,128)} %res_ref.1, bf16[6144,512]{1,0:T(8,128)(2,1)} %bitcast.20), custom_call_target="tpu_custom_call" | custom-call | tf_op jit(solution)/shard_map/pallas_call | solution.py:44
  5.1 14.1 %all_to_all.25.in_ref = bf16[16,8,384]{2,1,0:T(8,128)(2,1)S(1)} all-to-all(bf16[16,8,384]{2,1,0:T(8,128)(2,1)S(1)} %get-tuple-element.28), channel_id=1, replica_groups=mesh['row'=8,'col'=16] {'col'}, dimensions={0} | all-to-all | bytes 196608 | tf_op jit(solution)/shard_map/all_to_all | solution.py:269
  19.3 1.3 %shard_map.95 = f32[64,512]{1,0:T(8,128)S(1)} custom-call(bf16[16,8,384]{2,1,0:T(8,128)(2,1)S(1)} %all_to_all.25.in_ref, s32[64,16]{1,0:T(8,128)S(1)} %broadcast_bitcast_fusion.bound_ref, bf16[6144,512]{1,0:T(8,128)(2,1)S(1)} %bitcast.14), custom_call_target="tpu_custom_call" | custom-call | tf_op jit(solution)/shard_map/pallas_call | solution.py:44
  20.5 2.1 %collective-permute-start = (f32[64,512]{1,0:T(8,128)S(1)}, f32[64,512]{1,0:T(8,128)S(1)}, u32[]{:S(2)}, u32[]{:S(2)}) collective-permute-start(f32[64,512]{1,0:T(8,128)S(1)} %shard_map.95), channel_id=1, source_target_pairs={{0,16},{16,0},{32,48},{48,32},{64,80},{80,64},{96,112},{112,96},{1... | collective-permute-start | bytes 393224 | tf_op jit(solution)/shard_map/ppermute | solution.py:257
  23.7 3.8 %collective-permute-start.3 = (bf16[64,512]{1,0:T(8,128)(2,1)S(1)}, bf16[64,512]{1,0:T(8,128)(2,1)S(1)}, u32[]{:S(2)}, u32[]{:S(2)}) collective-permute-start(bf16[64,512]{1,0:T(8,128)(2,1)S(1)} %add_convert_fusion.p0_ref), channel_id=1, source_target_pairs={{0,96},{16,112},{32,64},{48,80},{64,32},{80,48},{96,0},{112,16},{1... | collective-permute-start | bytes 196616 | tf_op jit(solution)/shard_map/ppermute | solution.py:257
  28.2 1.4 %collective-permute-done.3.p6_ref = bf16[64,512]{1,0:T(8,128)(2,1)S(1)} collective-permute-done((bf16[64,512]{1,0:T(8,128)(2,1)S(1)}, bf16[64,512]{1,0:T(8,128)(2,1)S(1)}, u32[]{:S(2)}, u32[]{:S(2)}) %collective-permute-start.3) | collective-permute-done | bytes 65568 | tf_op jit(solution)/shard_map/ppermute | solution.py:257
  29.6 2.5 %collective-permute-done.2.p4_ref = bf16[64,512]{1,0:T(8,128)(2,1)S(1)} collective-permute-done((bf16[64,512]{1,0:T(8,128)(2,1)S(1)}, bf16[64,512]{1,0:T(8,128)(2,1)S(1)}, u32[]{:S(2)}, u32[]{:S(2)}) %collective-permute-start.2) | collective-permute-done | bytes 65568 | tf_op jit(solution)/shard_map/ppermute | solution.py:257
  32.1 2.0 %shard_map.96 = (bf16[16,8,512]{2,1,0:T(8,128)(2,1)S(1)}, f32[64,512]{1,0:T(8,128)S(1)}) custom-call(bf16[64,512]{1,0:T(8,128)(2,1)S(1)} %add_convert_fusion.p0_ref, bf16[64,512]{1,0:T(8,128)(2,1)S(1)} %collective-permute-done.1.p2_ref, bf16[64,512]{1,0:T(8,128)(2,1)S(1)} %collective-permute-done.2.p4_ref, ...), custom_call_target="tpu_custom_call" | custom-call | tf_op jit(solution)/shard_map/pallas_call | solution.py:44
  34.2 9.7 %all_to_all.26.in_ref = bf16[16,8,512]{2,1,0:T(8,128)(2,1)S(1)} all-to-all(bf16[16,8,512]{2,1,0:T(8,128)(2,1)S(1)} %get-tuple-element.32), channel_id=1, replica_groups=mesh['row'=8,'col'=16] {'col'}, dimensions={0} | all-to-all | bytes 262144 | tf_op jit(solution)/shard_map/all_to_all | solution.py:269
  43.8 2.6 %shard_map.97 = (f32[8,512]{1,0:T(8,128)S(1)}, f32[8,128]{1,0:T(8,128)S(1)}, bf16[16,8,512]{2,1,0:T(8,128)(2,1)S(1)}) custom-call(bf16[16,8,512]{2,1,0:T(8,128)(2,1)S(1)} %all_to_all.26.in_ref, bf16[6144,512]{1,0:T(8,128)(2,1)S(1)} %get-tuple-element.33.u_ref), custom_call_target="tpu_custom_call" | custom-call | tf_op jit(solution)/shard_map/pallas_call | solution.py:44
  46.4 9.9 %all_to_all.27.in_ref = bf16[16,8,512]{2,1,0:T(8,128)(2,1)S(1)} all-to-all(bf16[16,8,512]{2,1,0:T(8,128)(2,1)S(1)} %get-tuple-element.34), channel_id=1, replica_groups=mesh['row'=8,'col'=16] {'col'}, dimensions={0} | all-to-all | bytes 262144 | tf_op jit(solution)/shard_map/all_to_all | solution.py:269
  56.4 1.3 %shard_map.98.own_ref = f32[72,512]{1,0:T(8,128)S(1)} custom-call(bf16[16,8,512]{2,1,0:T(8,128)(2,1)S(1)} %all_to_all.27.in_ref, s32[64,16]{1,0:T(8,128)S(1)} %broadcast_bitcast_fusion.bound_ref, bf16[6144,512]{1,0:T(8,128)(2,1)S(1)} %bitcast.16), custom_call_target="tpu_custom_call" | custom-call | tf_op jit(solution)/shard_map/pallas_call | solution.py:44
  57.6 4.7 %collective-permute-start.4 = (f32[72,512]{1,0:T(8,128)S(1)}, f32[72,512]{1,0:T(8,128)S(1)}, u32[]{:S(2)}, u32[]{:S(2)}) collective-permute-start(f32[72,512]{1,0:T(8,128)S(1)} %shard_map.98.own_ref), channel_id=1, source_target_pairs={{0,16},{16,0},{32,48},{48,32},{64,80},{80,64},{96,112},{112,96},{1... | collective-permute-start | bytes 442376 | tf_op jit(solution)/shard_map/ppermute | solution.py:257
  65.0 1.7 %collective-permute-start.5 = (bf16[72,512]{1,0:T(8,128)(2,1)S(1)}, bf16[72,512]{1,0:T(8,128)(2,1)S(1)}, u32[]{:S(2)}, u32[]{:S(2)}) collective-permute-start(bf16[72,512]{1,0:T(8,128)(2,1)S(1)} %shard_map.99.p0_ref), channel_id=1, source_target_pairs={{0,32},{16,48},{32,0},{48,16},{64,96},{80,112},{96,64},{112,80},{1... | collective-permute-start | bytes 221192 | tf_op jit(solution)/shard_map/ppermute | solution.py:257
  66.8 1.2 %collective-permute-done.7.p6_ref = bf16[72,512]{1,0:T(8,128)(2,1)S(1)} collective-permute-done((bf16[72,512]{1,0:T(8,128)(2,1)S(1)}, bf16[72,512]{1,0:T(8,128)(2,1)S(1)}, u32[]{:S(2)}, u32[]{:S(2)}) %collective-permute-start.7) | collective-permute-done | bytes 73760 | tf_op jit(solution)/shard_map/ppermute | solution.py:257
  67.9 1.4 %collective-permute-done.6.p4_ref = bf16[72,512]{1,0:T(8,128)(2,1)S(1)} collective-permute-done((bf16[72,512]{1,0:T(8,128)(2,1)S(1)}, bf16[72,512]{1,0:T(8,128)(2,1)S(1)}, u32[]{:S(2)}, u32[]{:S(2)}) %collective-permute-start.6) | collective-permute-done | bytes 73760 | tf_op jit(solution)/shard_map/ppermute | solution.py:257
  70.1 4.3 %shard_map.100 = (bf16[16,8,1536]{2,1,0:T(8,128)(2,1)S(1)}, f32[64,512]{1,0:T(8,128)S(1)}, f32[64,512]{1,0:T(8,128)S(1)}, f32[8,128]{1,0:T(8,128)S(1)}, bf16[8,1024]{1,0:T(8,128)(2,1)S(1)}) custom-call(bf16[72,512]{1,0:T(8,128)(2,1)S(1)} %shard_map.99.p0_ref, bf16[72,512]{1,0:T(8,128)(2,1)S(1)} %collective-permute-done.5.p2_ref, ...), custom_call_target="tpu_custom_call" | custom-call | tf_op jit(solution)/shard_map/pallas_call | solution.py:44
  74.4 11.2 %all_to_all.28.in_ref = bf16[16,8,1536]{2,1,0:T(8,128)(2,1)S(1)} all-to-all(bf16[16,8,1536]{2,1,0:T(8,128)(2,1)S(1)} %get-tuple-element.37), channel_id=1, replica_groups=mesh['row'=8,'col'=16] {'col'}, dimensions={0} | all-to-all | bytes 786432 | tf_op jit(solution)/shard_map/all_to_all | solution.py:269
  85.6 1.7 %shard_map.101 = (f32[8,512]{1,0:T(8,128)S(1)}, f32[8,128]{1,0:T(8,128)S(1)}, f32[128,1,128]{2,1,0:T(1,128)}) custom-call(bf16[16,8,1536]{2,1,0:T(8,128)(2,1)S(1)} %all_to_all.28.in_ref, bf16[6144,512]{1,0:T(8,128)(2,1)S(1)} %get-tuple-element.33.u_ref), custom_call_target="tpu_custom_call" | custom-call | tf_op jit(solution)/shard_map/pallas_call | solution.py:44
  87.3 1.1 %shard_map.102 = (bf16[4,8,1024]{2,1,0:T(8,128)(2,1)S(1)}, bf16[4,8,1024]{2,1,0:T(8,128)(2,1)S(1)}) custom-call(s32[16,16]{1,0:T(8,128)S(1)} %copy-done.3, s32[128]{0:T(128)S(1)} %copy-done.4, bf16[8,1024]{1,0:T(8,128)(2,1)S(1)} %get-tuple-element.47.even_ref, bf16[16,8,1536]{2,1,0:T(8,128)(2,1)S(1)} %all_to_all.28.in_ref), custom_call_target="tpu_custom_call" | custom-call | tf_op jit(solution)/shard_map/pallas_call | solution.py:44
  88.4 3.0 %collective-permute-start.8 = (bf16[4,8,1024]{2,1,0:T(8,128)(2,1)S(1)}, bf16[4,8,1024]{2,1,0:T(8,128)(2,1)S(1)}, u32[]{:S(2)}, u32[]{:S(2)}) collective-permute-start(bf16[4,8,1024]{2,1,0:T(8,128)(2,1)S(1)} %get-tuple-element.50), channel_id=1, source_target_pairs={{0,16},{16,0},{32,48},{48,32},{64,80},{80,64},{96,112},{112,96},{1... | collective-permute-start | bytes 196616 | tf_op jit(solution)/shard_map/ppermute | solution.py:257
  91.7 5.0 %all-to-all-start.4 = ((f32[128,1,128]{2,1,0:T(1,128)}), f32[128,1,128]{2,1,0:T(1,128)S(1)}, u32[]{:S(2)}, u32[]{:S(2)}) async-start(f32[128,1,128]{2,1,0:T(1,128)} %get-tuple-element.38), calls=%async_computation.4 | async-start | bytes 131072 | tf_op jit(solution)/shard_map/all_to_all | solution.py:321
  96.7 3.3 %collective-permute-start.11 = (bf16[8,1024]{1,0:T(8,128)(2,1)S(1)}, bf16[8,1024]{1,0:T(8,128)(2,1)S(1)}, u32[]{:S(2)}, u32[]{:S(2)}) collective-permute-start(bf16[8,1024]{1,0:T(8,128)(2,1)S(1)} %get-tuple-element.51), channel_id=1, source_target_pairs={{0,96},{16,112},{32,64},{48,80},{64,32},{80,48},{96,0},{112,16},{1... | collective-permute-start | bytes 49160 | tf_op jit(solution)/shard_map/ppermute | solution.py:257
  100.7 5.5 %all-to-all-done.4.norm_ref = f32[128,1,128]{2,1,0:T(1,128)S(1)} async-done(((f32[128,1,128]{2,1,0:T(1,128)}), f32[128,1,128]{2,1,0:T(1,128)S(1)}, u32[]{:S(2)}, u32[]{:S(2)}) %all-to-all-start.4) | async-done | bytes 65568 | tf_op jit(solution)/shard_map/all_to_all | solution.py:321
  (37 shorter events, 7.1 us)
Async XLA Ops:
  0.6 18.6 %copy-start = (s32[16,8]{0,1:T(8,128)S(1)}, s32[16,8]{0,1:T(8,128)}, u32[]{:S(2)}) copy-start(s32[16,8]{0,1:T(8,128)} %param.10) | copy-start | bytes 1540
  0.6 18.6 %copy-start.1 = (bf16[16,8,48,512]{3,2,1,0:T(8,128)(2,1)S(1)}, bf16[16,8,48,512]{3,2,1,0:T(8,128)(2,1)}, u32[]{:S(2)}) copy-start(bf16[16,8,48,512]{3,2,1,0:T(8,128)(2,1)} %param.9) | copy-start | bytes 18874372
  20.5 3.1 %collective-permute-start = (f32[64,512]{1,0:T(8,128)S(1)}, f32[64,512]{1,0:T(8,128)S(1)}, u32[]{:S(2)}, u32[]{:S(2)}) collective-permute-start(f32[64,512]{1,0:T(8,128)S(1)} %shard_map.95), channel_id=1, source_target_pairs={{0,16},{16,0},{32,48},{48,32},{64,80},{80,64},{96,112},{112,96},{1... | collective-permute-start | bytes 393224 | tf_op jit(solution)/shard_map/ppermute | solution.py:257
  23.7 5.9 %collective-permute-start.3 = (bf16[64,512]{1,0:T(8,128)(2,1)S(1)}, bf16[64,512]{1,0:T(8,128)(2,1)S(1)}, u32[]{:S(2)}, u32[]{:S(2)}) collective-permute-start(bf16[64,512]{1,0:T(8,128)(2,1)S(1)} %add_convert_fusion.p0_ref), channel_id=1, source_target_pairs={{0,96},{16,112},{32,64},{48,80},{64,32},{80,48},{96,0},{112,16},{1... | collective-permute-start | bytes 196616 | tf_op jit(solution)/shard_map/ppermute | solution.py:257
  27.5 4.6 %collective-permute-start.2 = (bf16[64,512]{1,0:T(8,128)(2,1)S(1)}, bf16[64,512]{1,0:T(8,128)(2,1)S(1)}, u32[]{:S(2)}, u32[]{:S(2)}) collective-permute-start(bf16[64,512]{1,0:T(8,128)(2,1)S(1)} %add_convert_fusion.p0_ref), channel_id=1, source_target_pairs={{0,64},{16,80},{32,96},{48,112},{64,0},{80,16},{96,32},{112,48},{1... | collective-permute-start | bytes 196616 | tf_op jit(solution)/shard_map/ppermute | solution.py:257
  27.5 4.6 %collective-permute-start.1 = (bf16[64,512]{1,0:T(8,128)(2,1)S(1)}, bf16[64,512]{1,0:T(8,128)(2,1)S(1)}, u32[]{:S(2)}, u32[]{:S(2)}) collective-permute-start(bf16[64,512]{1,0:T(8,128)(2,1)S(1)} %add_convert_fusion.p0_ref), channel_id=1, source_target_pairs={{0,32},{16,48},{32,0},{48,16},{64,96},{80,112},{96,64},{112,80},{1... | collective-permute-start | bytes 196616 | tf_op jit(solution)/shard_map/ppermute | solution.py:257
  32.1 37.9 %slice-start = ((s8[8388608]{0:T(1024)(128)(4,1)}), s8[4194304]{0:T(1024)(128)(4,1)S(1)}, s32[]{:S(2)}) async-start(s8[8388608]{0:T(1024)(128)(4,1)} %bitcast.18), calls=%async_computation.5 | async-start | bytes 8388608
  43.8 26.2 %slice-start.1 = ((s8[8388608]{0:T(1024)(128)(4,1)}), s8[4194304]{0:T(1024)(128)(4,1)S(1)}, s32[]{:S(2)}) async-start(s8[8388608]{0:T(1024)(128)(4,1)} %bitcast.18), calls=%async_computation.6 | async-start | bytes 8388608
  57.6 5.7 %collective-permute-start.4 = (f32[72,512]{1,0:T(8,128)S(1)}, f32[72,512]{1,0:T(8,128)S(1)}, u32[]{:S(2)}, u32[]{:S(2)}) collective-permute-start(f32[72,512]{1,0:T(8,128)S(1)} %shard_map.98.own_ref), channel_id=1, source_target_pairs={{0,16},{16,0},{32,48},{48,32},{64,80},{80,64},{96,112},{112,96},{1... | collective-permute-start | bytes 442376 | tf_op jit(solution)/shard_map/ppermute | solution.py:257
  63.5 4.4 %collective-permute-start.7 = (bf16[72,512]{1,0:T(8,128)(2,1)S(1)}, bf16[72,512]{1,0:T(8,128)(2,1)S(1)}, u32[]{:S(2)}, u32[]{:S(2)}) collective-permute-start(bf16[72,512]{1,0:T(8,128)(2,1)S(1)} %shard_map.99.p0_ref), channel_id=1, source_target_pairs={{0,96},{16,112},{32,64},{48,80},{64,32},{80,48},{96,0},{112,16},{1... | collective-permute-start | bytes 221192 | tf_op jit(solution)/shard_map/ppermute | solution.py:257
  64.5 4.8 %collective-permute-start.6 = (bf16[72,512]{1,0:T(8,128)(2,1)S(1)}, bf16[72,512]{1,0:T(8,128)(2,1)S(1)}, u32[]{:S(2)}, u32[]{:S(2)}) collective-permute-start(bf16[72,512]{1,0:T(8,128)(2,1)S(1)} %shard_map.99.p0_ref), channel_id=1, source_target_pairs={{0,64},{16,80},{32,96},{48,112},{64,0},{80,16},{96,32},{112,48},{1... | collective-permute-start | bytes 221192 | tf_op jit(solution)/shard_map/ppermute | solution.py:257
  65.0 5.0 %collective-permute-start.5 = (bf16[72,512]{1,0:T(8,128)(2,1)S(1)}, bf16[72,512]{1,0:T(8,128)(2,1)S(1)}, u32[]{:S(2)}, u32[]{:S(2)}) collective-permute-start(bf16[72,512]{1,0:T(8,128)(2,1)S(1)} %shard_map.99.p0_ref), channel_id=1, source_target_pairs={{0,32},{16,48},{32,0},{48,16},{64,96},{80,112},{96,64},{112,80},{1... | collective-permute-start | bytes 221192 | tf_op jit(solution)/shard_map/ppermute | solution.py:257
  74.4 12.9 %copy-start.3 = (s32[16,16]{1,0:T(8,128)S(1)}, s32[16,16]{1,0:T(8,128)}, u32[]{:S(2)}) copy-start(s32[16,16]{1,0:T(8,128)} %target_ref.1) | copy-start | bytes 3076
  74.4 12.9 %copy-start.4 = (s32[128]{0:T(128)S(1)}, s32[128]{0:T(128)}, u32[]{:S(2)}) copy-start(s32[128]{0:T(128)} %order_ref.1) | copy-start | bytes 1540
  74.4 31.8 %copy-start.2 = (f32[8,512]{1,0:T(8,128)S(1)}, f32[8,512]{1,0:T(8,128)}, u32[]{:S(2)}) copy-start(f32[8,512]{1,0:T(8,128)} %res_ref.1) | copy-start | bytes 49156
  88.4 8.3 %collective-permute-start.8 = (bf16[4,8,1024]{2,1,0:T(8,128)(2,1)S(1)}, bf16[4,8,1024]{2,1,0:T(8,128)(2,1)S(1)}, u32[]{:S(2)}, u32[]{:S(2)}) collective-permute-start(bf16[4,8,1024]{2,1,0:T(8,128)(2,1)S(1)} %get-tuple-element.50), channel_id=1, source_target_pairs={{0,16},{16,0},{32,48},{48,32},{64,80},{80,64},{96,112},{112,96},{1... | collective-permute-start | bytes 196616 | tf_op jit(solution)/shard_map/ppermute | solution.py:257
  91.4 9.3 %collective-permute-start.12 = (bf16[8,1024]{1,0:T(8,128)(2,1)S(1)}, bf16[8,1024]{1,0:T(8,128)(2,1)S(1)}, u32[]{:S(2)}, u32[]{:S(2)}) collective-permute-start(bf16[8,1024]{1,0:T(8,128)(2,1)S(1)} %get-tuple-element.47.even_ref), channel_id=1, source_target_pairs={{0,1},{1,0},{2,3},{3,2},{4,5},{5,4},{6,7},{7,6},{8,9},{9,8},{10,11... | collective-permute-start | bytes 49160 | tf_op jit(solution)/shard_map/ppermute | solution.py:331
  91.7 14.5 %all-to-all-start.4 = ((f32[128,1,128]{2,1,0:T(1,128)}), f32[128,1,128]{2,1,0:T(1,128)S(1)}, u32[]{:S(2)}, u32[]{:S(2)}) async-start(f32[128,1,128]{2,1,0:T(1,128)} %get-tuple-element.38), calls=%async_computation.4 | async-start | bytes 131072 | tf_op jit(solution)/shard_map/all_to_all | solution.py:321
  96.7 9.5 %collective-permute-start.11 = (bf16[8,1024]{1,0:T(8,128)(2,1)S(1)}, bf16[8,1024]{1,0:T(8,128)(2,1)S(1)}, u32[]{:S(2)}, u32[]{:S(2)}) collective-permute-start(bf16[8,1024]{1,0:T(8,128)(2,1)S(1)} %get-tuple-element.51), channel_id=1, source_target_pairs={{0,96},{16,112},{32,64},{48,80},{64,32},{80,48},{96,0},{112,16},{1... | collective-permute-start | bytes 49160 | tf_op jit(solution)/shard_map/ppermute | solution.py:257
  100.0 6.2 %collective-permute-start.10 = (bf16[8,1024]{1,0:T(8,128)(2,1)S(1)}, bf16[8,1024]{1,0:T(8,128)(2,1)S(1)}, u32[]{:S(2)}, u32[]{:S(2)}) collective-permute-start(bf16[8,1024]{1,0:T(8,128)(2,1)S(1)} %get-tuple-element.52), channel_id=1, source_target_pairs={{0,64},{16,80},{32,96},{48,112},{64,0},{80,16},{96,32},{112,48},{1... | collective-permute-start | bytes 49160 | tf_op jit(solution)/shard_map/ppermute | solution.py:257
  100.1 6.1 %collective-permute-start.9 = (bf16[8,1024]{1,0:T(8,128)(2,1)S(1)}, bf16[8,1024]{1,0:T(8,128)(2,1)S(1)}, u32[]{:S(2)}, u32[]{:S(2)}) collective-permute-start(bf16[8,1024]{1,0:T(8,128)(2,1)S(1)} %get-tuple-element.53), channel_id=1, source_target_pairs={{0,32},{16,48},{32,0},{48,16},{64,96},{80,112},{96,64},{112,80},{1... | collective-permute-start | bytes 49160 | tf_op jit(solution)/shard_map/ppermute | solution.py:257

commit v4 on v3

--- a/solution.py
+++ b/solution.py
@@ -37,7 +37,7 @@
     return total
 
 
-def call(kernel, outs, args, smem=(), hbm=(), keep=(), scratch=(), limit=8):
+def call(kernel, outs, args, smem=(), hbm=(), keep=(), scratch=(), limit=8, smem_out=False):
     vm = pl.BlockSpec(memory_space=pltpu.VMEM)
     sm = pl.BlockSpec(memory_space=pltpu.SMEM)
     far_away = pl.BlockSpec(memory_space=pltpu.HBM)
@@ -50,7 +50,7 @@
         in_specs=[
             sm if at in smem else far_away if at in hbm else vm for at in range(len(args))
         ],
-        out_specs=tuple(vm for _ in outs),
+        out_specs=tuple(sm if smem_out else vm for _ in outs),
         scratch_shapes=list(scratch),
         compiler_params=pltpu.CompilerParams(vmem_limit_bytes=limit * MIB),
     )(*args)
@@ -71,7 +71,7 @@
         u_factors.reshape(all_cols * slots, patch), pltpu.HBM
     )
     far_all = pltpu.with_memory_space_constraint(far_blocks, pltpu.VMEM)
-    parts = 8
+    parts = 4
 
     def kept_lanes(bound_ref, row_patch):
         lane = lax.broadcasted_iota(jnp.int32, (tall, wide), 1)
@@ -208,19 +208,32 @@
         for peer in range(devices):
             out_ref[peer] = line
 
-    def route_kernel(target_ref, order_ref, even_ref, in_ref, keep_ref, give_ref):
+    def slot_kernel(target_ref, order_ref, slot_ref):
         row, col = lax.axis_index("row"), lax.axis_index("col")
+        mine = [order_ref[lax.bitwise_xor(row, m) * peers + col] for m in range(n_row)]
+        for source in range(peers):
+            target = target_ref[row * blocks + 1, source]
+            slot = jnp.int32(n_row)
+            for m in range(n_row):
+                slot = jnp.where(target == mine[m], m, slot)
+            slot_ref[source] = slot
+
+    def route_kernel(slot_ref, even_ref, in_ref, keep_ref, give_ref, sum_ref):
+        sum_ref[...] = jnp.zeros_like(sum_ref)
+        sum_ref[n_row // 2] = even_ref[...].astype(F32) * jnp.where(
+            lax.axis_index("col") % 2 == 0, 1.0, 0.0
+        )
+        for source in range(peers):
+            slot = slot_ref[source]
+
+            @pl.when(slot < n_row)
+            def _():
+                piece = in_ref[source, :, far_low : far_low + 2 * patch].astype(F32)
+                sum_ref[slot] = sum_ref[slot] + piece
+
         for m in range(n_row):
-            mine = order_ref[lax.bitwise_xor(row, m) * peers + col]
-            total = jnp.zeros((dens, 2 * patch), F32)
-            if m == n_row // 2:
-                total = even_ref[...].astype(F32) * jnp.where(col % 2 == 0, 1.0, 0.0)
-            for source in range(peers):
-                hit = jnp.where(target_ref[row * blocks + 1, source] == mine, 1.0, 0.0)
-                piece = in_ref[source, :, far_low : far_low + 2 * patch].astype(F32)
-                total = total + piece * hit
             out_ref = keep_ref if m % 2 == 0 else give_ref
-            out_ref[m // 2] = total.astype(BF16)
+            out_ref[m // 2] = sum_ref[m].astype(BF16)
 
     def pair_kernel(own_ref, other_ref, out_ref):
         out_ref[0:tall, :] = (own_ref[0:tall] + other_ref[0:tall]).astype(BF16)
@@ -256,6 +269,12 @@
     def row_shift(x, k):
         return lax.ppermute(x, "row", [(i, i ^ k) for i in range(n_row)])
 
+    def hops(halves):
+        arrived = []
+        for k, half in zip((2, 4, 6), halves):
+            arrived.append(row_shift(half, k))
+        return arrived
+
     def over_rows(part):
         other = row_shift(part, 1)
         if part.shape[0] > tall:
@@ -263,7 +282,7 @@
         else:
             half = (part + other).astype(BF16)
         half = lax.optimization_barrier(half)
-        return [half] + [row_shift(half, k) for k in (2, 4, 6)]
+        return [half] + hops([half] * 3)
 
     def over_col(x):
         return lax.all_to_all(x, "col", split_axis=0, concat_axis=0, tiled=True)
@@ -285,10 +304,13 @@
     (part,) = call(
         grad_kernel, [((tall, patch), F32)], [landed, bound, v_all], scratch=left_scratch
     )
+    part, *tables = lax.optimization_barrier((part, block_target, recv_order))
+    (slot,) = call(slot_kernel, [((peers,), jnp.int32)], tables, smem=(0, 1), smem_out=True)
+    *arrived, slot = lax.optimization_barrier((*over_rows(part), slot))
     sent, grad = call(
         coef_kernel,
         [((rows, dens, wide + 128), BF16), ((tall, patch), F32)],
-        over_rows(part) + [bound, v_all],
+        arrived + [bound, v_all],
     )
     image1, gsq1, sent = call(
         image_back_kernel,
@@ -323,11 +345,12 @@
     keep, give = call(
         route_kernel,
         [((n_row // 2, dens, 2 * patch), BF16)] * 2,
-        [block_target, recv_order, even, landed],
-        smem=(0, 1),
+        [slot, even, landed],
+        smem=(0,),
+        scratch=(pltpu.VMEM((n_row, dens, 2 * patch), F32),),
     )
     near = keep + row_shift(give, 1)
-    pieces = [near[0]] + [row_shift(near[k], 2 * k) for k in range(1, n_row // 2)]
+    pieces = [near[0]] + hops([near[k] for k in range(1, n_row // 2)])
     side = lax.ppermute(even, "col", [(c, c ^ 1) for c in range(peers)])
     densities, residual, far_field = call(
         finish_kernel,

time: 107 us -> 106 us (level)
  waiting for transfers between devices: 14.7 us -> 13.4 us
    ppermute x12, waiting for transfers between devices: 9.25 us -> 7.87 us  [row_shift(): return lax.ppermute(x, 'row', [(i, i ^ k) for i in range(n_row)])]
    pallas_call x10 -> x11, Pallas kernels: 19.8 us -> 20 us  [call(): pl.pallas_call(kernel, out_shape=tuple((pltpu.VMEM(s, d) if at in keep el...]
  transfers between devices with their start and end apart: 14 -> 14, of which waited for: 8 -> 8; matrix products, arithmetic and copies ran while one was open for 0% -> 0% of each run, Pallas kernels for 0% -> 1%
where the time goes in v4:
time: 106 us
  blocking collectives  44.8 us (42%)
  starting transfers between devices  26.9 us (25%)
  Pallas kernels  20 us (19%)
  waiting for transfers between devices  13.4 us (13%)
    all_to_all x4, blocking collectives, over_col(): return lax.all_to_all(x, 'col', split_axis=0, concat_axis=0, tiled=True)  44.8 us
    ppermute x12, starting transfers between devices, row_shift(): return lax.ppermute(x, 'row', [(i, i ^ k) for i in range(n_row)])  21.6 us
    pallas_call x11, Pallas kernels, call(): pl.pallas_call(kernel, out_shape=tuple((pltpu.VMEM(s, d) if at in keep el...  20 us
    ppermute x12, waiting for transfers between devices, row_shift(): return lax.ppermute(x, 'row', [(i, i ^ k) for i in range(n_row)])  7.87 us
    all_to_all x1, waiting for transfers between devices, per_device(): lax.all_to_all(sent, ('row', 'col'), split_axis=0, concat_axis=0, tiled=T...  5.5 us
    all_to_all x1, starting transfers between devices, per_device(): lax.all_to_all(sent, ('row', 'col'), split_axis=0, concat_axis=0, tiled=T...  4.99 us
  transfers between devices with their start and end apart: 14, of which 8 were waited for; matrix products, arithmetic and copies ran while one was open for 0% of the time, Pallas kernels for 1%

profile of v4, /device:TPU:1, one launch (start us, length us, event | category | flops | bytes accessed | tf_op | source)
XLA Modules:
  0.0 105.9 jit_solution(3699718891843257156)
XLA Ops:
  0.7 3.7 %shard_map.94 = (bf16[16,8,384]{2,1,0:T(8,128)(2,1)S(1)}, bf16[6144,512]{1,0:T(8,128)(2,1)S(1)}) custom-call(f32[8,512]{1,0:T(8,128)} %res_ref.1, bf16[6144,512]{1,0:T(8,128)(2,1)} %bitcast.20), custom_call_target="tpu_custom_call" | custom-call | tf_op jit(solution)/shard_map/pallas_call | solution.py:44
  4.4 14.1 %all_to_all.25.in_ref = bf16[16,8,384]{2,1,0:T(8,128)(2,1)S(1)} all-to-all(bf16[16,8,384]{2,1,0:T(8,128)(2,1)S(1)} %get-tuple-element.36), channel_id=1, replica_groups=mesh['row'=8,'col'=16] {'col'}, dimensions={0} | all-to-all | bytes 196608 | tf_op jit(solution)/shard_map/all_to_all | solution.py:288
  18.5 1.3 %shard_map.95 = f32[64,512]{1,0:T(8,128)S(1)} custom-call(bf16[16,8,384]{2,1,0:T(8,128)(2,1)S(1)} %all_to_all.25.in_ref, s32[64,16]{1,0:T(8,128)S(1)} %broadcast_bitcast_fusion.bound_ref, bf16[6144,512]{1,0:T(8,128)(2,1)S(1)} %bitcast.14), custom_call_target="tpu_custom_call" | custom-call | tf_op jit(solution)/shard_map/pallas_call | solution.py:44
  19.8 2.1 %collective-permute-start = (f32[64,512]{1,0:T(8,128)S(1)}, f32[64,512]{1,0:T(8,128)S(1)}, u32[]{:S(2)}, u32[]{:S(2)}) collective-permute-start(f32[64,512]{1,0:T(8,128)S(1)} %shard_map.95), channel_id=1, source_target_pairs={{0,16},{16,0},{32,48},{48,32},{64,80},{80,64},{96,112},{112,96},{1... | collective-permute-start | bytes 393224 | tf_op jit(solution)/shard_map/ppermute | solution.py:270
  22.9 3.8 %collective-permute-start.3 = (bf16[64,512]{1,0:T(8,128)(2,1)S(1)}, bf16[64,512]{1,0:T(8,128)(2,1)S(1)}, u32[]{:S(2)}, u32[]{:S(2)}) collective-permute-start(bf16[64,512]{1,0:T(8,128)(2,1)S(1)} %add_convert_fusion.p0_ref), channel_id=1, source_target_pairs={{0,96},{16,112},{32,64},{48,80},{64,32},{80,48},{96,0},{112,16},{1... | collective-permute-start | bytes 196616 | tf_op jit(solution)/shard_map/ppermute | solution.py:270
  27.4 1.4 %shard_map.96.slot_ref = s32[16]{0:T(128)S(1)} custom-call(s32[16,16]{1,0:T(8,128)S(1)} %copy-done.3, s32[128]{0:T(128)S(1)} %copy-done.4), custom_call_target="tpu_custom_call" | custom-call | tf_op jit(solution)/shard_map/pallas_call | solution.py:44
  28.9 2.5 %collective-permute-done.2.p4_ref = bf16[64,512]{1,0:T(8,128)(2,1)S(1)} collective-permute-done((bf16[64,512]{1,0:T(8,128)(2,1)S(1)}, bf16[64,512]{1,0:T(8,128)(2,1)S(1)}, u32[]{:S(2)}, u32[]{:S(2)}) %collective-permute-start.2) | collective-permute-done | bytes 65568 | tf_op jit(solution)/shard_map/ppermute | solution.py:270
  31.4 2.0 %shard_map.97 = (bf16[16,8,512]{2,1,0:T(8,128)(2,1)S(1)}, f32[64,512]{1,0:T(8,128)S(1)}) custom-call(bf16[64,512]{1,0:T(8,128)(2,1)S(1)} %add_convert_fusion.p0_ref, bf16[64,512]{1,0:T(8,128)(2,1)S(1)} %collective-permute-done.1.p2_ref, bf16[64,512]{1,0:T(8,128)(2,1)S(1)} %collective-permute-done.2.p4_ref, ...), custom_call_target="tpu_custom_call" | custom-call | tf_op jit(solution)/shard_map/pallas_call | solution.py:44
  33.4 9.7 %all_to_all.26.in_ref = bf16[16,8,512]{2,1,0:T(8,128)(2,1)S(1)} all-to-all(bf16[16,8,512]{2,1,0:T(8,128)(2,1)S(1)} %get-tuple-element.47), channel_id=1, replica_groups=mesh['row'=8,'col'=16] {'col'}, dimensions={0} | all-to-all | bytes 262144 | tf_op jit(solution)/shard_map/all_to_all | solution.py:288
  43.1 2.6 %shard_map.98 = (f32[8,512]{1,0:T(8,128)S(1)}, f32[8,128]{1,0:T(8,128)S(1)}, bf16[16,8,512]{2,1,0:T(8,128)(2,1)S(1)}) custom-call(bf16[16,8,512]{2,1,0:T(8,128)(2,1)S(1)} %all_to_all.26.in_ref, bf16[6144,512]{1,0:T(8,128)(2,1)S(1)} %get-tuple-element.48.u_ref), custom_call_target="tpu_custom_call" | custom-call | tf_op jit(solution)/shard_map/pallas_call | solution.py:44
  45.7 9.9 %all_to_all.27.in_ref = bf16[16,8,512]{2,1,0:T(8,128)(2,1)S(1)} all-to-all(bf16[16,8,512]{2,1,0:T(8,128)(2,1)S(1)} %get-tuple-element.49), channel_id=1, replica_groups=mesh['row'=8,'col'=16] {'col'}, dimensions={0} | all-to-all | bytes 262144 | tf_op jit(solution)/shard_map/all_to_all | solution.py:288
  55.6 1.3 %shard_map.99.own_ref = f32[72,512]{1,0:T(8,128)S(1)} custom-call(bf16[16,8,512]{2,1,0:T(8,128)(2,1)S(1)} %all_to_all.27.in_ref, s32[64,16]{1,0:T(8,128)S(1)} %broadcast_bitcast_fusion.bound_ref, bf16[6144,512]{1,0:T(8,128)(2,1)S(1)} %bitcast.16), custom_call_target="tpu_custom_call" | custom-call | tf_op jit(solution)/shard_map/pallas_call | solution.py:44
  56.9 4.7 %collective-permute-start.4 = (f32[72,512]{1,0:T(8,128)S(1)}, f32[72,512]{1,0:T(8,128)S(1)}, u32[]{:S(2)}, u32[]{:S(2)}) collective-permute-start(f32[72,512]{1,0:T(8,128)S(1)} %shard_map.99.own_ref), channel_id=1, source_target_pairs={{0,16},{16,0},{32,48},{48,32},{64,80},{80,64},{96,112},{112,96},{1... | collective-permute-start | bytes 442376 | tf_op jit(solution)/shard_map/ppermute | solution.py:270
  61.6 1.0 collective-permute-done.4.other_ref
  64.3 1.7 %collective-permute-start.5 = (bf16[72,512]{1,0:T(8,128)(2,1)S(1)}, bf16[72,512]{1,0:T(8,128)(2,1)S(1)}, u32[]{:S(2)}, u32[]{:S(2)}) collective-permute-start(bf16[72,512]{1,0:T(8,128)(2,1)S(1)} %shard_map.100.p0_ref), channel_id=1, source_target_pairs={{0,32},{16,48},{32,0},{48,16},{64,96},{80,112},{96,64},{112,80},{1... | collective-permute-start | bytes 221192 | tf_op jit(solution)/shard_map/ppermute | solution.py:270
  66.0 1.2 %collective-permute-done.7.p6_ref = bf16[72,512]{1,0:T(8,128)(2,1)S(1)} collective-permute-done((bf16[72,512]{1,0:T(8,128)(2,1)S(1)}, bf16[72,512]{1,0:T(8,128)(2,1)S(1)}, u32[]{:S(2)}, u32[]{:S(2)}) %collective-permute-start.7) | collective-permute-done | bytes 73760 | tf_op jit(solution)/shard_map/ppermute | solution.py:270
  67.2 1.4 %collective-permute-done.6.p4_ref = bf16[72,512]{1,0:T(8,128)(2,1)S(1)} collective-permute-done((bf16[72,512]{1,0:T(8,128)(2,1)S(1)}, bf16[72,512]{1,0:T(8,128)(2,1)S(1)}, u32[]{:S(2)}, u32[]{:S(2)}) %collective-permute-start.6) | collective-permute-done | bytes 73760 | tf_op jit(solution)/shard_map/ppermute | solution.py:270
  69.3 4.3 %shard_map.101 = (bf16[16,8,1536]{2,1,0:T(8,128)(2,1)S(1)}, f32[64,512]{1,0:T(8,128)S(1)}, f32[64,512]{1,0:T(8,128)S(1)}, f32[8,128]{1,0:T(8,128)S(1)}, bf16[8,1024]{1,0:T(8,128)(2,1)S(1)}) custom-call(bf16[72,512]{1,0:T(8,128)(2,1)S(1)} %shard_map.100.p0_ref, bf16[72,512]{1,0:T(8,128)(2,1)S(1)} %collective-permute-done.5.p2_ref, ...), custom_call_target="tpu_custom_call" | custom-call | tf_op jit(solution)/shard_map/pallas_call | solution.py:44
  73.6 11.1 %all_to_all.28.in_ref = bf16[16,8,1536]{2,1,0:T(8,128)(2,1)S(1)} all-to-all(bf16[16,8,1536]{2,1,0:T(8,128)(2,1)S(1)} %get-tuple-element.52), channel_id=1, replica_groups=mesh['row'=8,'col'=16] {'col'}, dimensions={0} | all-to-all | bytes 786432 | tf_op jit(solution)/shard_map/all_to_all | solution.py:288
  84.7 1.7 %shard_map.102 = (f32[8,512]{1,0:T(8,128)S(1)}, f32[8,128]{1,0:T(8,128)S(1)}, f32[128,1,128]{2,1,0:T(1,128)}) custom-call(bf16[16,8,1536]{2,1,0:T(8,128)(2,1)S(1)} %all_to_all.28.in_ref, bf16[6144,512]{1,0:T(8,128)(2,1)S(1)} %get-tuple-element.48.u_ref), custom_call_target="tpu_custom_call" | custom-call | tf_op jit(solution)/shard_map/pallas_call | solution.py:44
  87.1 3.0 %collective-permute-start.8 = (bf16[4,8,1024]{2,1,0:T(8,128)(2,1)S(1)}, bf16[4,8,1024]{2,1,0:T(8,128)(2,1)S(1)}, u32[]{:S(2)}, u32[]{:S(2)}) collective-permute-start(bf16[4,8,1024]{2,1,0:T(8,128)(2,1)S(1)} %get-tuple-element.66), channel_id=1, source_target_pairs={{0,16},{16,0},{32,48},{48,32},{64,80},{80,64},{96,112},{112,96},{1... | collective-permute-start | bytes 196616 | tf_op jit(solution)/shard_map/ppermute | solution.py:270
  90.3 5.0 %all-to-all-start.4 = ((f32[128,1,128]{2,1,0:T(1,128)}), f32[128,1,128]{2,1,0:T(1,128)S(1)}, u32[]{:S(2)}, u32[]{:S(2)}) async-start(f32[128,1,128]{2,1,0:T(1,128)} %get-tuple-element.53), calls=%async_computation.4 | async-start | bytes 131072 | tf_op jit(solution)/shard_map/all_to_all | solution.py:343
  95.4 3.3 %collective-permute-start.11 = (bf16[8,1024]{1,0:T(8,128)(2,1)S(1)}, bf16[8,1024]{1,0:T(8,128)(2,1)S(1)}, u32[]{:S(2)}, u32[]{:S(2)}) collective-permute-start(bf16[8,1024]{1,0:T(8,128)(2,1)S(1)} %get-tuple-element.67), channel_id=1, source_target_pairs={{0,96},{16,112},{32,64},{48,80},{64,32},{80,48},{96,0},{112,16},{1... | collective-permute-start | bytes 49160 | tf_op jit(solution)/shard_map/ppermute | solution.py:270
  99.4 5.5 %all-to-all-done.4.norm_ref = f32[128,1,128]{2,1,0:T(1,128)S(1)} async-done(((f32[128,1,128]{2,1,0:T(1,128)}), f32[128,1,128]{2,1,0:T(1,128)S(1)}, u32[]{:S(2)}, u32[]{:S(2)}) %all-to-all-start.4) | async-done | bytes 65568 | tf_op jit(solution)/shard_map/all_to_all | solution.py:343
  (38 shorter events, 6.8 us)
Async XLA Ops:
  0.6 17.9 %copy-start = (s32[16,8]{0,1:T(8,128)S(1)}, s32[16,8]{0,1:T(8,128)}, u32[]{:S(2)}) copy-start(s32[16,8]{0,1:T(8,128)} %param.10) | copy-start | bytes 1540
  0.6 17.9 %copy-start.1 = (bf16[16,8,48,512]{3,2,1,0:T(8,128)(2,1)S(1)}, bf16[16,8,48,512]{3,2,1,0:T(8,128)(2,1)}, u32[]{:S(2)}) copy-start(bf16[16,8,48,512]{3,2,1,0:T(8,128)(2,1)} %param.9) | copy-start | bytes 18874372
  0.7 26.8 %copy-start.3 = (s32[16,16]{1,0:T(8,128)S(1)}, s32[16,16]{1,0:T(8,128)}, u32[]{:S(2)}) copy-start(s32[16,16]{1,0:T(8,128)} %target_ref) | copy-start | bytes 3076
  0.7 26.8 %copy-start.4 = (s32[128]{0:T(128)S(1)}, s32[128]{0:T(128)}, u32[]{:S(2)}) copy-start(s32[128]{0:T(128)} %order_ref) | copy-start | bytes 1540
  19.8 3.1 %collective-permute-start = (f32[64,512]{1,0:T(8,128)S(1)}, f32[64,512]{1,0:T(8,128)S(1)}, u32[]{:S(2)}, u32[]{:S(2)}) collective-permute-start(f32[64,512]{1,0:T(8,128)S(1)} %shard_map.95), channel_id=1, source_target_pairs={{0,16},{16,0},{32,48},{48,32},{64,80},{80,64},{96,112},{112,96},{1... | collective-permute-start | bytes 393224 | tf_op jit(solution)/shard_map/ppermute | solution.py:270
  22.9 5.9 %collective-permute-start.3 = (bf16[64,512]{1,0:T(8,128)(2,1)S(1)}, bf16[64,512]{1,0:T(8,128)(2,1)S(1)}, u32[]{:S(2)}, u32[]{:S(2)}) collective-permute-start(bf16[64,512]{1,0:T(8,128)(2,1)S(1)} %add_convert_fusion.p0_ref), channel_id=1, source_target_pairs={{0,96},{16,112},{32,64},{48,80},{64,32},{80,48},{96,0},{112,16},{1... | collective-permute-start | bytes 196616 | tf_op jit(solution)/shard_map/ppermute | solution.py:270
  26.8 4.6 %collective-permute-start.2 = (bf16[64,512]{1,0:T(8,128)(2,1)S(1)}, bf16[64,512]{1,0:T(8,128)(2,1)S(1)}, u32[]{:S(2)}, u32[]{:S(2)}) collective-permute-start(bf16[64,512]{1,0:T(8,128)(2,1)S(1)} %add_convert_fusion.p0_ref), channel_id=1, source_target_pairs={{0,64},{16,80},{32,96},{48,112},{64,0},{80,16},{96,32},{112,48},{1... | collective-permute-start | bytes 196616 | tf_op jit(solution)/shard_map/ppermute | solution.py:270
  26.8 4.6 %collective-permute-start.1 = (bf16[64,512]{1,0:T(8,128)(2,1)S(1)}, bf16[64,512]{1,0:T(8,128)(2,1)S(1)}, u32[]{:S(2)}, u32[]{:S(2)}) collective-permute-start(bf16[64,512]{1,0:T(8,128)(2,1)S(1)} %add_convert_fusion.p0_ref), channel_id=1, source_target_pairs={{0,32},{16,48},{32,0},{48,16},{64,96},{80,112},{96,64},{112,80},{1... | collective-permute-start | bytes 196616 | tf_op jit(solution)/shard_map/ppermute | solution.py:270
  31.4 37.9 %slice-start = ((s8[8388608]{0:T(1024)(128)(4,1)}), s8[4194304]{0:T(1024)(128)(4,1)S(1)}, s32[]{:S(2)}) async-start(s8[8388608]{0:T(1024)(128)(4,1)} %bitcast.18), calls=%async_computation.5 | async-start | bytes 8388608
  43.1 26.2 %slice-start.1 = ((s8[8388608]{0:T(1024)(128)(4,1)}), s8[4194304]{0:T(1024)(128)(4,1)S(1)}, s32[]{:S(2)}) async-start(s8[8388608]{0:T(1024)(128)(4,1)} %bitcast.18), calls=%async_computation.6 | async-start | bytes 8388608
  56.9 5.7 %collective-permute-start.4 = (f32[72,512]{1,0:T(8,128)S(1)}, f32[72,512]{1,0:T(8,128)S(1)}, u32[]{:S(2)}, u32[]{:S(2)}) collective-permute-start(f32[72,512]{1,0:T(8,128)S(1)} %shard_map.99.own_ref), channel_id=1, source_target_pairs={{0,16},{16,0},{32,48},{48,32},{64,80},{80,64},{96,112},{112,96},{1... | collective-permute-start | bytes 442376 | tf_op jit(solution)/shard_map/ppermute | solution.py:270
  62.7 4.4 %collective-permute-start.7 = (bf16[72,512]{1,0:T(8,128)(2,1)S(1)}, bf16[72,512]{1,0:T(8,128)(2,1)S(1)}, u32[]{:S(2)}, u32[]{:S(2)}) collective-permute-start(bf16[72,512]{1,0:T(8,128)(2,1)S(1)} %shard_map.100.p0_ref), channel_id=1, source_target_pairs={{0,96},{16,112},{32,64},{48,80},{64,32},{80,48},{96,0},{112,16},{1... | collective-permute-start | bytes 221192 | tf_op jit(solution)/shard_map/ppermute | solution.py:270
  63.7 4.8 %collective-permute-start.6 = (bf16[72,512]{1,0:T(8,128)(2,1)S(1)}, bf16[72,512]{1,0:T(8,128)(2,1)S(1)}, u32[]{:S(2)}, u32[]{:S(2)}) collective-permute-start(bf16[72,512]{1,0:T(8,128)(2,1)S(1)} %shard_map.100.p0_ref), channel_id=1, source_target_pairs={{0,64},{16,80},{32,96},{48,112},{64,0},{80,16},{96,32},{112,48},{1... | collective-permute-start | bytes 221192 | tf_op jit(solution)/shard_map/ppermute | solution.py:270
  64.3 5.0 %collective-permute-start.5 = (bf16[72,512]{1,0:T(8,128)(2,1)S(1)}, bf16[72,512]{1,0:T(8,128)(2,1)S(1)}, u32[]{:S(2)}, u32[]{:S(2)}) collective-permute-start(bf16[72,512]{1,0:T(8,128)(2,1)S(1)} %shard_map.100.p0_ref), channel_id=1, source_target_pairs={{0,32},{16,48},{32,0},{48,16},{64,96},{80,112},{96,64},{112,80},{1... | collective-permute-start | bytes 221192 | tf_op jit(solution)/shard_map/ppermute | solution.py:270
  73.6 31.3 %copy-start.2 = (f32[8,512]{1,0:T(8,128)S(1)}, f32[8,512]{1,0:T(8,128)}, u32[]{:S(2)}) copy-start(f32[8,512]{1,0:T(8,128)} %res_ref.1) | copy-start | bytes 49156
  87.1 8.3 %collective-permute-start.8 = (bf16[4,8,1024]{2,1,0:T(8,128)(2,1)S(1)}, bf16[4,8,1024]{2,1,0:T(8,128)(2,1)S(1)}, u32[]{:S(2)}, u32[]{:S(2)}) collective-permute-start(bf16[4,8,1024]{2,1,0:T(8,128)(2,1)S(1)} %get-tuple-element.66), channel_id=1, source_target_pairs={{0,16},{16,0},{32,48},{48,32},{64,80},{80,64},{96,112},{112,96},{1... | collective-permute-start | bytes 196616 | tf_op jit(solution)/shard_map/ppermute | solution.py:270
  90.1 9.3 %collective-permute-start.12 = (bf16[8,1024]{1,0:T(8,128)(2,1)S(1)}, bf16[8,1024]{1,0:T(8,128)(2,1)S(1)}, u32[]{:S(2)}, u32[]{:S(2)}) collective-permute-start(bf16[8,1024]{1,0:T(8,128)(2,1)S(1)} %get-tuple-element.63.even_ref), channel_id=1, source_target_pairs={{0,1},{1,0},{2,3},{3,2},{4,5},{5,4},{6,7},{7,6},{8,9},{9,8},{10,11... | collective-permute-start | bytes 49160 | tf_op jit(solution)/shard_map/ppermute | solution.py:354
  90.3 14.5 %all-to-all-start.4 = ((f32[128,1,128]{2,1,0:T(1,128)}), f32[128,1,128]{2,1,0:T(1,128)S(1)}, u32[]{:S(2)}, u32[]{:S(2)}) async-start(f32[128,1,128]{2,1,0:T(1,128)} %get-tuple-element.53), calls=%async_computation.4 | async-start | bytes 131072 | tf_op jit(solution)/shard_map/all_to_all | solution.py:343
  95.4 9.5 %collective-permute-start.11 = (bf16[8,1024]{1,0:T(8,128)(2,1)S(1)}, bf16[8,1024]{1,0:T(8,128)(2,1)S(1)}, u32[]{:S(2)}, u32[]{:S(2)}) collective-permute-start(bf16[8,1024]{1,0:T(8,128)(2,1)S(1)} %get-tuple-element.67), channel_id=1, source_target_pairs={{0,96},{16,112},{32,64},{48,80},{64,32},{80,48},{96,0},{112,16},{1... | collective-permute-start | bytes 49160 | tf_op jit(solution)/shard_map/ppermute | solution.py:270
  98.7 6.2 %collective-permute-start.10 = (bf16[8,1024]{1,0:T(8,128)(2,1)S(1)}, bf16[8,1024]{1,0:T(8,128)(2,1)S(1)}, u32[]{:S(2)}, u32[]{:S(2)}) collective-permute-start(bf16[8,1024]{1,0:T(8,128)(2,1)S(1)} %get-tuple-element.68), channel_id=1, source_target_pairs={{0,64},{16,80},{32,96},{48,112},{64,0},{80,16},{96,32},{112,48},{1... | collective-permute-start | bytes 49160 | tf_op jit(solution)/shard_map/ppermute | solution.py:270
  98.8 6.1 %collective-permute-start.9 = (bf16[8,1024]{1,0:T(8,128)(2,1)S(1)}, bf16[8,1024]{1,0:T(8,128)(2,1)S(1)}, u32[]{:S(2)}, u32[]{:S(2)}) collective-permute-start(bf16[8,1024]{1,0:T(8,128)(2,1)S(1)} %get-tuple-element.69), channel_id=1, source_target_pairs={{0,32},{16,48},{32,0},{48,16},{64,96},{80,112},{96,64},{112,80},{1... | collective-permute-start | bytes 49160 | tf_op jit(solution)/shard_map/ppermute | solution.py:270

commit v5 on v4

--- a/solution.py
+++ b/solution.py
@@ -114,10 +114,23 @@
         norm = jnp.sum(gather_sum(in_ref, wide, 128), axis=1, keepdims=True)
         out_ref[tall : tall + dens, :] = jnp.broadcast_to(norm, (dens, patch))
 
+    def flip_kernel(in_ref, out_ref):
+        for at in range(0, in_ref.shape[0], patch):
+            out_ref[:, at : at + patch] = in_ref[at : at + patch, :].T
+
+    def flip_far_kernel(in_ref, out_ref):
+        for block in range(blocks):
+            for at in range(0, in_ref.shape[2], patch):
+                out_ref[block, at : at + patch, :] = in_ref[block, :, at : at + patch].T
+
+    def flip(kernel, x, shape):
+        (out,) = call(kernel, [(shape, BF16)], [x], keep=(0,))
+        return out
+
     def coefficients(grad, bound_ref, v_ref, out_ref):
         half = grad.astype(BF16)
         for i in range(0, rows, 2):
-            both = dot_nt(half, v_ref[i * wide : (i + 2) * wide, :])
+            both = dot_nn(half, v_ref[:, i * wide : (i + 2) * wide])
             for k in range(2):
                 part = jnp.where(
                     kept_lanes(bound_ref, i + k), both[:, k * wide : (k + 1) * wide], 0.0
@@ -148,7 +161,7 @@
         left = jnp.concatenate([in_ref[c, :, 0:wide] for c in range(peers)], axis=1)
         return dot_nn(left, u_ref[...])
 
-    def image_back_kernel(in_ref, u_ref, image_ref, gsq_ref, out_ref):
+    def image_back_kernel(in_ref, u_ref, ut_ref, image_ref, gsq_ref, out_ref):
         image = image_of(in_ref, u_ref)
         image_ref[...] = image
         gsq_ref[...] = jnp.broadcast_to(
@@ -156,7 +169,7 @@
         )
         high = image.astype(BF16)
         low = (image - high.astype(F32)).astype(BF16)
-        both = dot_nt(jnp.concatenate([high, low], axis=0), u_ref[...])
+        both = dot_nn(jnp.concatenate([high, low], axis=0), ut_ref[...])
         back = both[0:dens] + both[dens : 2 * dens]
         mine = spread(norm_of(image))
         for peer in range(peers):
@@ -187,8 +200,8 @@
             for x in (first, second)
         ]
         left = jnp.concatenate(lines, axis=0).astype(BF16)
-        even = dot_nt(left, far_ref[0])
-        odd = dot_nt(left, far_ref[1])
+        even = dot_nn(left, far_ref[0])
+        odd = dot_nn(left, far_ref[1])
         even_ref[...] = jnp.concatenate([even[0:dens], even[dens : 2 * dens]], axis=1).astype(BF16)
         send = jnp.concatenate([odd[0:dens], odd[dens : 2 * dens]], axis=1).astype(BF16)
         for i in range(rows):
@@ -304,18 +317,19 @@
     (part,) = call(
         grad_kernel, [((tall, patch), F32)], [landed, bound, v_all], scratch=left_scratch
     )
-    part, *tables = lax.optimization_barrier((part, block_target, recv_order))
-    (slot,) = call(slot_kernel, [((peers,), jnp.int32)], tables, smem=(0, 1), smem_out=True)
-    *arrived, slot = lax.optimization_barrier((*over_rows(part), slot))
+    part, v_now, u_now = lax.optimization_barrier((part, v_all, u_all))
+    v_flip = flip(flip_kernel, v_now, (patch, v_now.shape[0]))
+    u_flip = flip(flip_kernel, u_now, (patch, u_now.shape[0]))
+    *arrived, v_flip, u_flip = lax.optimization_barrier((*over_rows(part), v_flip, u_flip))
     sent, grad = call(
         coef_kernel,
         [((rows, dens, wide + 128), BF16), ((tall, patch), F32)],
-        arrived + [bound, v_all],
+        arrived + [bound, v_flip],
     )
     image1, gsq1, sent = call(
         image_back_kernel,
         [((dens, patch), F32), ((dens, 128), F32), ((peers, dens, wide + 128), BF16)],
-        [over_col(sent), u_all],
+        [over_col(sent), u_all, u_flip],
     )
     (part,) = call(
         grad_norm_kernel,
@@ -323,6 +337,10 @@
         [over_col(sent), bound, v_all],
         scratch=left_scratch,
     )
+    part, far_now, *tables = lax.optimization_barrier((part, far_all, block_target, recv_order))
+    far_flip = flip(flip_far_kernel, far_now, (blocks, far_now.shape[2], patch))
+    (slot,) = call(slot_kernel, [((peers,), jnp.int32)], tables, smem=(0, 1), smem_out=True)
+    *arrived, far_flip, slot = lax.optimization_barrier((*over_rows(part), far_flip, slot))
     sent, first, second, step1, even = call(
         coef_far_kernel,
         [
@@ -332,7 +350,7 @@
             ((dens, 128), F32),
             ((dens, 2 * patch), BF16),
         ],
-        over_rows(part) + [grad, gsq1, bound, v_all, far_all],
+        arrived + [grad, gsq1, bound, v_flip, far_flip],
     )
     landed = over_col(sent)
     image2, gsq2, sent = call(

time: 106 us -> 104 us (0.981)
  waiting for transfers between devices: 13.4 us -> 7.81 us
  Pallas kernels: 20 us -> 22.6 us
    ppermute x12, waiting for transfers between devices: 7.87 us -> 2.31 us  [row_shift(): return lax.ppermute(x, 'row', [(i, i ^ k) for i in range(n_row)])]
    pallas_call x11 -> x14, Pallas kernels: 20 us -> 22.6 us  [call(): pl.pallas_call(kernel, out_shape=tuple((pltpu.VMEM(s, d) if at in keep el...]
  transfers between devices with their start and end apart: 14 -> 14, of which waited for: 8 -> 4; matrix products, arithmetic and copies ran while one was open for 0% -> 0% of each run, Pallas kernels for 1% -> 7%
where the time goes in v5:
time: 104 us; the launch traced here: 103 us
  blocking collectives  45 us (43%)
  starting transfers between devices  26.8 us (26%)
  Pallas kernels  22.6 us (22%)
  waiting for transfers between devices  7.81 us (8%)
    all_to_all x4, blocking collectives, over_col(): return lax.all_to_all(x, 'col', split_axis=0, concat_axis=0, tiled=True)  45 us
    pallas_call x14, Pallas kernels, call(): pl.pallas_call(kernel, out_shape=tuple((pltpu.VMEM(s, d) if at in keep el...  22.6 us
    ppermute x12, starting transfers between devices, row_shift(): return lax.ppermute(x, 'row', [(i, i ^ k) for i in range(n_row)])  21.6 us
    all_to_all x1, waiting for transfers between devices, per_device(): lax.all_to_all(sent, ('row', 'col'), split_axis=0, concat_axis=0, tiled=T...  5.5 us
    all_to_all x1, starting transfers between devices, per_device(): lax.all_to_all(sent, ('row', 'col'), split_axis=0, concat_axis=0, tiled=T...  4.95 us
    ppermute x12, waiting for transfers between devices, row_shift(): return lax.ppermute(x, 'row', [(i, i ^ k) for i in range(n_row)])  2.31 us
  transfers between devices with their start and end apart: 14, of which 4 were waited for; matrix products, arithmetic and copies ran while one was open for 0% of the time, Pallas kernels for 7%

profile of v5, /device:TPU:1, one launch (start us, length us, event | category | flops | bytes accessed | tf_op | source)
XLA Modules:
  0.0 103.3 jit_solution(4688529247392003593)
XLA Ops:
  0.7 3.7 %shard_map.94 = (bf16[16,8,384]{2,1,0:T(8,128)(2,1)S(1)}, bf16[6144,512]{1,0:T(8,128)(2,1)S(1)}) custom-call(f32[8,512]{1,0:T(8,128)} %res_ref.1, bf16[6144,512]{1,0:T(8,128)(2,1)} %bitcast.19), custom_call_target="tpu_custom_call" | custom-call | tf_op jit(solution)/shard_map/pallas_call | solution.py:44
  4.4 14.1 %all_to_all.25.in_ref = bf16[16,8,384]{2,1,0:T(8,128)(2,1)S(1)} all-to-all(bf16[16,8,384]{2,1,0:T(8,128)(2,1)S(1)} %get-tuple-element.47), channel_id=1, replica_groups=mesh['row'=8,'col'=16] {'col'}, dimensions={0} | all-to-all | bytes 196608 | tf_op jit(solution)/shard_map/all_to_all | solution.py:301
  18.5 1.3 %shard_map.95 = f32[64,512]{1,0:T(8,128)S(1)} custom-call(bf16[16,8,384]{2,1,0:T(8,128)(2,1)S(1)} %all_to_all.25.in_ref, s32[64,16]{1,0:T(8,128)S(1)} %broadcast_bitcast_fusion.bound_ref, bf16[6144,512]{1,0:T(8,128)(2,1)S(1)} %bitcast.14), custom_call_target="tpu_custom_call" | custom-call | tf_op jit(solution)/shard_map/pallas_call | solution.py:44
  19.8 2.1 %collective-permute-start = (f32[64,512]{1,0:T(8,128)S(1)}, f32[64,512]{1,0:T(8,128)S(1)}, u32[]{:S(2)}, u32[]{:S(2)}) collective-permute-start(f32[64,512]{1,0:T(8,128)S(1)} %shard_map.95), channel_id=1, source_target_pairs={{0,16},{16,0},{32,48},{48,32},{64,80},{80,64},{96,112},{112,96},{1... | collective-permute-start | bytes 393224 | tf_op jit(solution)/shard_map/ppermute | solution.py:283
  22.9 3.8 %collective-permute-start.3 = (bf16[64,512]{1,0:T(8,128)(2,1)S(1)}, bf16[64,512]{1,0:T(8,128)(2,1)S(1)}, u32[]{:S(2)}, u32[]{:S(2)}) collective-permute-start(bf16[64,512]{1,0:T(8,128)(2,1)S(1)} %add_convert_fusion.p0_ref), channel_id=1, source_target_pairs={{0,96},{16,112},{32,64},{48,80},{64,32},{80,48},{96,0},{112,16},{1... | collective-permute-start | bytes 196616 | tf_op jit(solution)/shard_map/ppermute | solution.py:283
  27.4 1.8 %shard_map.96.v_ref = bf16[512,6144]{1,0:T(8,128)(2,1)S(1)} custom-call(bf16[6144,512]{1,0:T(8,128)(2,1)S(1)} %bitcast.15), custom_call_target="tpu_custom_call" | custom-call | tf_op jit(solution)/shard_map/pallas_call | solution.py:44
  29.3 1.8 %shard_map.97.ut_ref = bf16[512,6144]{1,0:T(8,128)(2,1)S(1)} custom-call(bf16[6144,512]{1,0:T(8,128)(2,1)S(1)} %get-tuple-element.54.in_ref.u_ref), custom_call_target="tpu_custom_call" | custom-call | tf_op jit(solution)/shard_map/pallas_call | solution.py:44
  31.4 1.3 %shard_map.98 = (bf16[16,8,512]{2,1,0:T(8,128)(2,1)S(1)}, f32[64,512]{1,0:T(8,128)S(1)}) custom-call(bf16[64,512]{1,0:T(8,128)(2,1)S(1)} %add_convert_fusion.p0_ref, bf16[64,512]{1,0:T(8,128)(2,1)S(1)} %collective-permute-done.1.p2_ref, bf16[64,512]{1,0:T(8,128)(2,1)S(1)} %collective-permute-done.2.p4_ref, ...), custom_call_target="tpu_custom_call" | custom-call | tf_op jit(solution)/shard_map/pallas_call | solution.py:44
  32.7 9.9 %all_to_all.26.in_ref = bf16[16,8,512]{2,1,0:T(8,128)(2,1)S(1)} all-to-all(bf16[16,8,512]{2,1,0:T(8,128)(2,1)S(1)} %get-tuple-element.60), channel_id=1, replica_groups=mesh['row'=8,'col'=16] {'col'}, dimensions={0} | all-to-all | bytes 262144 | tf_op jit(solution)/shard_map/all_to_all | solution.py:301
  42.7 1.8 %shard_map.99 = (f32[8,512]{1,0:T(8,128)S(1)}, f32[8,128]{1,0:T(8,128)S(1)}, bf16[16,8,512]{2,1,0:T(8,128)(2,1)S(1)}) custom-call(bf16[16,8,512]{2,1,0:T(8,128)(2,1)S(1)} %all_to_all.26.in_ref, bf16[6144,512]{1,0:T(8,128)(2,1)S(1)} %get-tuple-element.54.in_ref.u_ref, bf16[512,6144]{1,0:T(8,128)(2,1)S(1)} %shard_map.97.ut_ref), custom_call_target="tpu_custom_call" | custom-call | tf_op jit(solution)/shard_map/pallas_call | solution.py:44
  44.5 9.9 %all_to_all.27.in_ref = bf16[16,8,512]{2,1,0:T(8,128)(2,1)S(1)} all-to-all(bf16[16,8,512]{2,1,0:T(8,128)(2,1)S(1)} %get-tuple-element.62), channel_id=1, replica_groups=mesh['row'=8,'col'=16] {'col'}, dimensions={0} | all-to-all | bytes 262144 | tf_op jit(solution)/shard_map/all_to_all | solution.py:301
  54.4 1.3 %shard_map.100.own_ref = f32[72,512]{1,0:T(8,128)S(1)} custom-call(bf16[16,8,512]{2,1,0:T(8,128)(2,1)S(1)} %all_to_all.27.in_ref, s32[64,16]{1,0:T(8,128)S(1)} %broadcast_bitcast_fusion.bound_ref, bf16[6144,512]{1,0:T(8,128)(2,1)S(1)} %bitcast.16), custom_call_target="tpu_custom_call" | custom-call | tf_op jit(solution)/shard_map/pallas_call | solution.py:44
  55.7 4.7 %collective-permute-start.4 = (f32[72,512]{1,0:T(8,128)S(1)}, f32[72,512]{1,0:T(8,128)S(1)}, u32[]{:S(2)}, u32[]{:S(2)}) collective-permute-start(f32[72,512]{1,0:T(8,128)S(1)} %shard_map.100.own_ref), channel_id=1, source_target_pairs={{0,16},{16,0},{32,48},{48,32},{64,80},{80,64},{96,112},{112,96},{1... | collective-permute-start | bytes 442376 | tf_op jit(solution)/shard_map/ppermute | solution.py:283
  61.5 1.5 %collective-permute-start.7 = (bf16[72,512]{1,0:T(8,128)(2,1)S(1)}, bf16[72,512]{1,0:T(8,128)(2,1)S(1)}, u32[]{:S(2)}, u32[]{:S(2)}) collective-permute-start(bf16[72,512]{1,0:T(8,128)(2,1)S(1)} %shard_map.101.p0_ref), channel_id=1, source_target_pairs={{0,96},{16,112},{32,64},{48,80},{64,32},{80,48},{96,0},{112,16},{1... | collective-permute-start | bytes 221192 | tf_op jit(solution)/shard_map/ppermute | solution.py:283
  63.1 1.7 %collective-permute-start.5 = (bf16[72,512]{1,0:T(8,128)(2,1)S(1)}, bf16[72,512]{1,0:T(8,128)(2,1)S(1)}, u32[]{:S(2)}, u32[]{:S(2)}) collective-permute-start(bf16[72,512]{1,0:T(8,128)(2,1)S(1)} %shard_map.101.p0_ref), channel_id=1, source_target_pairs={{0,32},{16,48},{32,0},{48,16},{64,96},{80,112},{96,64},{112,80},{1... | collective-permute-start | bytes 221192 | tf_op jit(solution)/shard_map/ppermute | solution.py:283
  64.8 2.2 %shard_map.102.far_ref = bf16[2,4096,512]{2,1,0:T(8,128)(2,1)S(1)} custom-call(bf16[2,512,4096]{2,1,0:T(8,128)(2,1)S(1)} %bitcast.18), custom_call_target="tpu_custom_call" | custom-call | tf_op jit(solution)/shard_map/pallas_call | solution.py:44
  67.1 1.4 %shard_map.103.slot_ref = s32[16]{0:T(128)S(1)} custom-call(s32[16,16]{1,0:T(8,128)S(1)} %copy-done.3, s32[128]{0:T(128)S(1)} %copy-done.4), custom_call_target="tpu_custom_call" | custom-call | tf_op jit(solution)/shard_map/pallas_call | solution.py:44
  68.5 2.6 %shard_map.104 = (bf16[16,8,1536]{2,1,0:T(8,128)(2,1)S(1)}, f32[64,512]{1,0:T(8,128)S(1)}, f32[64,512]{1,0:T(8,128)S(1)}, f32[8,128]{1,0:T(8,128)S(1)}, bf16[8,1024]{1,0:T(8,128)(2,1)S(1)}) custom-call(bf16[72,512]{1,0:T(8,128)(2,1)S(1)} %shard_map.101.p0_ref, bf16[72,512]{1,0:T(8,128)(2,1)S(1)} %collective-permute-done.5.p2_ref, ...), custom_call_target="tpu_custom_call" | custom-call | tf_op jit(solution)/shard_map/pallas_call | solution.py:44
  71.1 11.1 %all_to_all.28.in_ref = bf16[16,8,1536]{2,1,0:T(8,128)(2,1)S(1)} all-to-all(bf16[16,8,1536]{2,1,0:T(8,128)(2,1)S(1)} %get-tuple-element.74), channel_id=1, replica_groups=mesh['row'=8,'col'=16] {'col'}, dimensions={0} | all-to-all | bytes 786432 | tf_op jit(solution)/shard_map/all_to_all | solution.py:301
  82.1 1.7 %shard_map.105 = (f32[8,512]{1,0:T(8,128)S(1)}, f32[8,128]{1,0:T(8,128)S(1)}, f32[128,1,128]{2,1,0:T(1,128)}) custom-call(bf16[16,8,1536]{2,1,0:T(8,128)(2,1)S(1)} %all_to_all.28.in_ref, bf16[6144,512]{1,0:T(8,128)(2,1)S(1)} %get-tuple-element.54.in_ref.u_ref), custom_call_target="tpu_custom_call" | custom-call | tf_op jit(solution)/shard_map/pallas_call | solution.py:44
  84.5 3.0 %collective-permute-start.8 = (bf16[4,8,1024]{2,1,0:T(8,128)(2,1)S(1)}, bf16[4,8,1024]{2,1,0:T(8,128)(2,1)S(1)}, u32[]{:S(2)}, u32[]{:S(2)}) collective-permute-start(bf16[4,8,1024]{2,1,0:T(8,128)(2,1)S(1)} %get-tuple-element.88), channel_id=1, source_target_pairs={{0,16},{16,0},{32,48},{48,32},{64,80},{80,64},{96,112},{112,96},{1... | collective-permute-start | bytes 196616 | tf_op jit(solution)/shard_map/ppermute | solution.py:283
  87.8 5.0 %all-to-all-start.4 = ((f32[128,1,128]{2,1,0:T(1,128)}), f32[128,1,128]{2,1,0:T(1,128)S(1)}, u32[]{:S(2)}, u32[]{:S(2)}) async-start(f32[128,1,128]{2,1,0:T(1,128)} %get-tuple-element.75), calls=%async_computation.4 | async-start | bytes 131072 | tf_op jit(solution)/shard_map/all_to_all | solution.py:361
  92.8 3.3 %collective-permute-start.11 = (bf16[8,1024]{1,0:T(8,128)(2,1)S(1)}, bf16[8,1024]{1,0:T(8,128)(2,1)S(1)}, u32[]{:S(2)}, u32[]{:S(2)}) collective-permute-start(bf16[8,1024]{1,0:T(8,128)(2,1)S(1)} %get-tuple-element.89), channel_id=1, source_target_pairs={{0,96},{16,112},{32,64},{48,80},{64,32},{80,48},{96,0},{112,16},{1... | collective-permute-start | bytes 49160 | tf_op jit(solution)/shard_map/ppermute | solution.py:283
  96.8 5.5 %all-to-all-done.4.norm_ref = f32[128,1,128]{2,1,0:T(1,128)S(1)} async-done(((f32[128,1,128]{2,1,0:T(1,128)}), f32[128,1,128]{2,1,0:T(1,128)S(1)}, u32[]{:S(2)}, u32[]{:S(2)}) %all-to-all-start.4) | async-done | bytes 65568 | tf_op jit(solution)/shard_map/all_to_all | solution.py:361
  (41 shorter events, 5.9 us)
Async XLA Ops:
  0.6 17.9 %copy-start = (s32[16,8]{0,1:T(8,128)S(1)}, s32[16,8]{0,1:T(8,128)}, u32[]{:S(2)}) copy-start(s32[16,8]{0,1:T(8,128)} %param.10) | copy-start | bytes 1540
  0.6 17.8 %copy-start.1 = (bf16[16,8,48,512]{3,2,1,0:T(8,128)(2,1)S(1)}, bf16[16,8,48,512]{3,2,1,0:T(8,128)(2,1)}, u32[]{:S(2)}) copy-start(bf16[16,8,48,512]{3,2,1,0:T(8,128)(2,1)} %param.9) | copy-start | bytes 18874372
  19.8 3.1 %collective-permute-start = (f32[64,512]{1,0:T(8,128)S(1)}, f32[64,512]{1,0:T(8,128)S(1)}, u32[]{:S(2)}, u32[]{:S(2)}) collective-permute-start(f32[64,512]{1,0:T(8,128)S(1)} %shard_map.95), channel_id=1, source_target_pairs={{0,16},{16,0},{32,48},{48,32},{64,80},{80,64},{96,112},{112,96},{1... | collective-permute-start | bytes 393224 | tf_op jit(solution)/shard_map/ppermute | solution.py:283
  22.9 8.2 %collective-permute-start.3 = (bf16[64,512]{1,0:T(8,128)(2,1)S(1)}, bf16[64,512]{1,0:T(8,128)(2,1)S(1)}, u32[]{:S(2)}, u32[]{:S(2)}) collective-permute-start(bf16[64,512]{1,0:T(8,128)(2,1)S(1)} %add_convert_fusion.p0_ref), channel_id=1, source_target_pairs={{0,96},{16,112},{32,64},{48,80},{64,32},{80,48},{96,0},{112,16},{1... | collective-permute-start | bytes 196616 | tf_op jit(solution)/shard_map/ppermute | solution.py:283
  26.8 4.6 %collective-permute-start.2 = (bf16[64,512]{1,0:T(8,128)(2,1)S(1)}, bf16[64,512]{1,0:T(8,128)(2,1)S(1)}, u32[]{:S(2)}, u32[]{:S(2)}) collective-permute-start(bf16[64,512]{1,0:T(8,128)(2,1)S(1)} %add_convert_fusion.p0_ref), channel_id=1, source_target_pairs={{0,64},{16,80},{32,96},{48,112},{64,0},{80,16},{96,32},{112,48},{1... | collective-permute-start | bytes 196616 | tf_op jit(solution)/shard_map/ppermute | solution.py:283
  26.8 4.6 %collective-permute-start.1 = (bf16[64,512]{1,0:T(8,128)(2,1)S(1)}, bf16[64,512]{1,0:T(8,128)(2,1)S(1)}, u32[]{:S(2)}, u32[]{:S(2)}) collective-permute-start(bf16[64,512]{1,0:T(8,128)(2,1)S(1)} %add_convert_fusion.p0_ref), channel_id=1, source_target_pairs={{0,32},{16,48},{32,0},{48,16},{64,96},{80,112},{96,64},{112,80},{1... | collective-permute-start | bytes 196616 | tf_op jit(solution)/shard_map/ppermute | solution.py:283
  32.7 32.1 %slice-start = ((s8[8388608]{0:T(1024)(128)(4,1)}), s8[4194304]{0:T(1024)(128)(4,1)S(1)}, s32[]{:S(2)}) async-start(s8[8388608]{0:T(1024)(128)(4,1)} %bitcast.17), calls=%async_computation.5 | async-start | bytes 8388608
  42.7 22.2 %slice-start.1 = ((s8[8388608]{0:T(1024)(128)(4,1)}), s8[4194304]{0:T(1024)(128)(4,1)S(1)}, s32[]{:S(2)}) async-start(s8[8388608]{0:T(1024)(128)(4,1)} %bitcast.17), calls=%async_computation.6 | async-start | bytes 8388608
  55.7 5.7 %collective-permute-start.4 = (f32[72,512]{1,0:T(8,128)S(1)}, f32[72,512]{1,0:T(8,128)S(1)}, u32[]{:S(2)}, u32[]{:S(2)}) collective-permute-start(f32[72,512]{1,0:T(8,128)S(1)} %shard_map.100.own_ref), channel_id=1, source_target_pairs={{0,16},{16,0},{32,48},{48,32},{64,80},{80,64},{96,112},{112,96},{1... | collective-permute-start | bytes 442376 | tf_op jit(solution)/shard_map/ppermute | solution.py:283
  61.5 5.5 %copy-start.3 = (s32[16,16]{1,0:T(8,128)S(1)}, s32[16,16]{1,0:T(8,128)}, u32[]{:S(2)}) copy-start(s32[16,16]{1,0:T(8,128)} %target_ref) | copy-start | bytes 3076
  61.5 5.5 %copy-start.4 = (s32[128]{0:T(128)S(1)}, s32[128]{0:T(128)}, u32[]{:S(2)}) copy-start(s32[128]{0:T(128)} %order_ref) | copy-start | bytes 1540
  61.5 6.9 %collective-permute-start.7 = (bf16[72,512]{1,0:T(8,128)(2,1)S(1)}, bf16[72,512]{1,0:T(8,128)(2,1)S(1)}, u32[]{:S(2)}, u32[]{:S(2)}) collective-permute-start(bf16[72,512]{1,0:T(8,128)(2,1)S(1)} %shard_map.101.p0_ref), channel_id=1, source_target_pairs={{0,96},{16,112},{32,64},{48,80},{64,32},{80,48},{96,0},{112,16},{1... | collective-permute-start | bytes 221192 | tf_op jit(solution)/shard_map/ppermute | solution.py:283
  63.0 5.5 %collective-permute-start.6 = (bf16[72,512]{1,0:T(8,128)(2,1)S(1)}, bf16[72,512]{1,0:T(8,128)(2,1)S(1)}, u32[]{:S(2)}, u32[]{:S(2)}) collective-permute-start(bf16[72,512]{1,0:T(8,128)(2,1)S(1)} %shard_map.101.p0_ref), channel_id=1, source_target_pairs={{0,64},{16,80},{32,96},{48,112},{64,0},{80,16},{96,32},{112,48},{1... | collective-permute-start | bytes 221192 | tf_op jit(solution)/shard_map/ppermute | solution.py:283
  63.1 5.4 %collective-permute-start.5 = (bf16[72,512]{1,0:T(8,128)(2,1)S(1)}, bf16[72,512]{1,0:T(8,128)(2,1)S(1)}, u32[]{:S(2)}, u32[]{:S(2)}) collective-permute-start(bf16[72,512]{1,0:T(8,128)(2,1)S(1)} %shard_map.101.p0_ref), channel_id=1, source_target_pairs={{0,32},{16,48},{32,0},{48,16},{64,96},{80,112},{96,64},{112,80},{1... | collective-permute-start | bytes 221192 | tf_op jit(solution)/shard_map/ppermute | solution.py:283
  71.1 31.2 %copy-start.2 = (f32[8,512]{1,0:T(8,128)S(1)}, f32[8,512]{1,0:T(8,128)}, u32[]{:S(2)}) copy-start(f32[8,512]{1,0:T(8,128)} %res_ref.1) | copy-start | bytes 49156
  84.5 8.2 %collective-permute-start.8 = (bf16[4,8,1024]{2,1,0:T(8,128)(2,1)S(1)}, bf16[4,8,1024]{2,1,0:T(8,128)(2,1)S(1)}, u32[]{:S(2)}, u32[]{:S(2)}) collective-permute-start(bf16[4,8,1024]{2,1,0:T(8,128)(2,1)S(1)} %get-tuple-element.88), channel_id=1, source_target_pairs={{0,16},{16,0},{32,48},{48,32},{64,80},{80,64},{96,112},{112,96},{1... | collective-permute-start | bytes 196616 | tf_op jit(solution)/shard_map/ppermute | solution.py:283
  87.5 9.3 %collective-permute-start.12 = (bf16[8,1024]{1,0:T(8,128)(2,1)S(1)}, bf16[8,1024]{1,0:T(8,128)(2,1)S(1)}, u32[]{:S(2)}, u32[]{:S(2)}) collective-permute-start(bf16[8,1024]{1,0:T(8,128)(2,1)S(1)} %get-tuple-element.85.even_ref), channel_id=1, source_target_pairs={{0,1},{1,0},{2,3},{3,2},{4,5},{5,4},{6,7},{7,6},{8,9},{9,8},{10,11... | collective-permute-start | bytes 49160 | tf_op jit(solution)/shard_map/ppermute | solution.py:372
  87.8 14.5 %all-to-all-start.4 = ((f32[128,1,128]{2,1,0:T(1,128)}), f32[128,1,128]{2,1,0:T(1,128)S(1)}, u32[]{:S(2)}, u32[]{:S(2)}) async-start(f32[128,1,128]{2,1,0:T(1,128)} %get-tuple-element.75), calls=%async_computation.4 | async-start | bytes 131072 | tf_op jit(solution)/shard_map/all_to_all | solution.py:361
  92.8 9.5 %collective-permute-start.11 = (bf16[8,1024]{1,0:T(8,128)(2,1)S(1)}, bf16[8,1024]{1,0:T(8,128)(2,1)S(1)}, u32[]{:S(2)}, u32[]{:S(2)}) collective-permute-start(bf16[8,1024]{1,0:T(8,128)(2,1)S(1)} %get-tuple-element.89), channel_id=1, source_target_pairs={{0,96},{16,112},{32,64},{48,80},{64,32},{80,48},{96,0},{112,16},{1... | collective-permute-start | bytes 49160 | tf_op jit(solution)/shard_map/ppermute | solution.py:283
  96.1 6.2 %collective-permute-start.10 = (bf16[8,1024]{1,0:T(8,128)(2,1)S(1)}, bf16[8,1024]{1,0:T(8,128)(2,1)S(1)}, u32[]{:S(2)}, u32[]{:S(2)}) collective-permute-start(bf16[8,1024]{1,0:T(8,128)(2,1)S(1)} %get-tuple-element.90), channel_id=1, source_target_pairs={{0,64},{16,80},{32,96},{48,112},{64,0},{80,16},{96,32},{112,48},{1... | collective-permute-start | bytes 49160 | tf_op jit(solution)/shard_map/ppermute | solution.py:283
  96.2 6.1 %collective-permute-start.9 = (bf16[8,1024]{1,0:T(8,128)(2,1)S(1)}, bf16[8,1024]{1,0:T(8,128)(2,1)S(1)}, u32[]{:S(2)}, u32[]{:S(2)}) collective-permute-start(bf16[8,1024]{1,0:T(8,128)(2,1)S(1)} %get-tuple-element.91), channel_id=1, source_target_pairs={{0,32},{16,48},{32,0},{48,16},{64,96},{80,112},{96,64},{112,80},{1... | collective-permute-start | bytes 49160 | tf_op jit(solution)/shard_map/ppermute | solution.py:283

commit v6 on v5

--- a/solution.py
+++ b/solution.py
@@ -8,10 +8,6 @@
 
 F32, BF16 = jnp.float32, jnp.bfloat16
 MIB = 1 << 20
-
-
-def dot_nt(a, b):
-    return lax.dot_general(a, b, (((1,), (1,)), ((), ())), preferred_element_type=F32)
 
 
 def dot_nn(a, b):
@@ -79,7 +75,7 @@
         at = lane - first
         return (at >= 0) & (at < bound_ref[:, row_patch : row_patch + 1])
 
-    def back_kernel(res_hbm, u_hbm, out_ref, u_ref, res_ref, sems):
+    def back_kernel(res_hbm, u_hbm, out_ref, u_ref, ut_ref, res_ref, sems):
         share = u_flat.shape[0] // parts
         each = peers // parts
         copies = [pltpu.make_async_copy(res_hbm, res_ref, sems.at[parts])]
@@ -92,7 +88,9 @@
         half = res_ref[...].astype(BF16)
         for part in range(parts):
             copies[part + 1].wait()
-            back = dot_nt(half, u_ref[part * share : (part + 1) * share, :])
+            turned = u_ref[part * share : (part + 1) * share, :].T
+            ut_ref[:, part * share : (part + 1) * share] = turned
+            back = dot_nn(half, turned)
             for k in range(each):
                 out_ref[part * each + k] = back[:, k * wide : (k + 1) * wide].astype(BF16)
 
@@ -302,12 +300,12 @@
 
     left_scratch = (pltpu.VMEM((tall, rows * wide), BF16),)
     dma = pltpu.SemaphoreType.DMA
-    sent, u_all = call(
+    sent, u_all, u_flip = call(
         back_kernel,
-        [((peers, dens, wide), BF16), (u_flat.shape, BF16)],
+        [((peers, dens, wide), BF16), (u_flat.shape, BF16), (u_flat.shape[::-1], BF16)],
         [pltpu.with_memory_space_constraint(right_side, pltpu.HBM), u_flat],
         hbm=(0, 1),
-        keep=(1,),
+        keep=(1, 2),
         scratch=(pltpu.VMEM((dens, patch), F32), dma((parts + 1,))),
     )
     sent, v_flat = lax.optimization_barrier((sent, v_factors.reshape(rows * wide, patch)))
@@ -317,10 +315,10 @@
     (part,) = call(
         grad_kernel, [((tall, patch), F32)], [landed, bound, v_all], scratch=left_scratch
     )
-    part, v_now, u_now = lax.optimization_barrier((part, v_all, u_all))
+    part, v_now, *tables = lax.optimization_barrier((part, v_all, block_target, recv_order))
     v_flip = flip(flip_kernel, v_now, (patch, v_now.shape[0]))
-    u_flip = flip(flip_kernel, u_now, (patch, u_now.shape[0]))
-    *arrived, v_flip, u_flip = lax.optimization_barrier((*over_rows(part), v_flip, u_flip))
+    (slot,) = call(slot_kernel, [((peers,), jnp.int32)], tables, smem=(0, 1), smem_out=True)
+    *arrived, v_flip, slot = lax.optimization_barrier((*over_rows(part), v_flip, slot))
     sent, grad = call(
         coef_kernel,
         [((rows, dens, wide + 128), BF16), ((tall, patch), F32)],
@@ -337,10 +335,9 @@
         [over_col(sent), bound, v_all],
         scratch=left_scratch,
     )
-    part, far_now, *tables = lax.optimization_barrier((part, far_all, block_target, recv_order))
+    part, far_now = lax.optimization_barrier((part, far_all))
     far_flip = flip(flip_far_kernel, far_now, (blocks, far_now.shape[2], patch))
-    (slot,) = call(slot_kernel, [((peers,), jnp.int32)], tables, smem=(0, 1), smem_out=True)
-    *arrived, far_flip, slot = lax.optimization_barrier((*over_rows(part), far_flip, slot))
+    *arrived, far_flip = lax.optimization_barrier((*over_rows(part), far_flip))
     sent, first, second, step1, even = call(
         coef_far_kernel,
         [
@@ -359,7 +356,6 @@
         [landed, u_all],
     )
     norms = lax.all_to_all(sent, ("row", "col"), split_axis=0, concat_axis=0, tiled=True)
-    even, landed, image2 = lax.optimization_barrier((even, landed, image2))
     keep, give = call(
         route_kernel,
         [((n_row // 2, dens, 2 * patch), BF16)] * 2,

time: 104 us -> 103 us (level)
  Pallas kernels: 22.6 us -> 21 us
  waiting for transfers between devices: 7.81 us -> 9.29 us
    pallas_call x14 -> x13, Pallas kernels: 22.6 us -> 21 us  [call(): pl.pallas_call(kernel, out_shape=tuple((pltpu.VMEM(s, d) if at in keep el...]
    ppermute x12, waiting for transfers between devices: 2.31 us -> 3.79 us  [row_shift(): return lax.ppermute(x, 'row', [(i, i ^ k) for i in range(n_row)])]
  transfers between devices with their start and end apart: 14 -> 14, of which waited for: 4 -> 6; matrix products, arithmetic and copies ran while one was open for 0% -> 0% of each run, Pallas kernels for 7% -> 7%
where the time goes in v6:
time: 103 us
  blocking collectives  44.9 us (44%)
  starting transfers between devices  26.9 us (26%)
  Pallas kernels  21 us (20%)
  waiting for transfers between devices  9.29 us (9%)
    all_to_all x4, blocking collectives, over_col(): return lax.all_to_all(x, 'col', split_axis=0, concat_axis=0, tiled=True)  44.9 us
    ppermute x12, starting transfers between devices, row_shift(): return lax.ppermute(x, 'row', [(i, i ^ k) for i in range(n_row)])  21.6 us
    pallas_call x13, Pallas kernels, call(): pl.pallas_call(kernel, out_shape=tuple((pltpu.VMEM(s, d) if at in keep el...  21 us
    all_to_all x1, waiting for transfers between devices, per_device(): lax.all_to_all(sent, ('row', 'col'), split_axis=0, concat_axis=0, tiled=T...  5.5 us
    all_to_all x1, starting transfers between devices, per_device(): lax.all_to_all(sent, ('row', 'col'), split_axis=0, concat_axis=0, tiled=T...  4.98 us
    ppermute x12, waiting for transfers between devices, row_shift(): return lax.ppermute(x, 'row', [(i, i ^ k) for i in range(n_row)])  3.79 us
  transfers between devices with their start and end apart: 14, of which 6 were waited for; matrix products, arithmetic and copies ran while one was open for 0% of the time, Pallas kernels for 7%

profile of v6, /device:TPU:1, one launch (start us, length us, event | category | flops | bytes accessed | tf_op | source)
XLA Modules:
  0.0 103.0 jit_solution(10461454458032103125)
XLA Ops:
  0.7 3.9 %shard_map.94 = (bf16[16,8,384]{2,1,0:T(8,128)(2,1)S(1)}, bf16[6144,512]{1,0:T(8,128)(2,1)S(1)}, bf16[512,6144]{1,0:T(8,128)(2,1)S(1)}) custom-call(f32[8,512]{1,0:T(8,128)} %res_ref.1, bf16[6144,512]{1,0:T(8,128)(2,1)} %bitcast.19), custom_call_target="tpu_custom_call" | custom-call | tf_op jit(solution)/shard_map/pallas_call | solution.py:40
  4.6 14.1 %all_to_all.25.in_ref = bf16[16,8,384]{2,1,0:T(8,128)(2,1)S(1)} all-to-all(bf16[16,8,384]{2,1,0:T(8,128)(2,1)S(1)} %get-tuple-element.43), channel_id=1, replica_groups=mesh['row'=8,'col'=16] {'col'}, dimensions={0} | all-to-all | bytes 196608 | tf_op jit(solution)/shard_map/all_to_all | solution.py:299
  18.7 1.3 %shard_map.95 = f32[64,512]{1,0:T(8,128)S(1)} custom-call(bf16[16,8,384]{2,1,0:T(8,128)(2,1)S(1)} %all_to_all.25.in_ref, s32[64,16]{1,0:T(8,128)S(1)} %broadcast_bitcast_fusion.bound_ref, bf16[6144,512]{1,0:T(8,128)(2,1)S(1)} %bitcast.14), custom_call_target="tpu_custom_call" | custom-call | tf_op jit(solution)/shard_map/pallas_call | solution.py:40
  20.0 2.1 %collective-permute-start = (f32[64,512]{1,0:T(8,128)S(1)}, f32[64,512]{1,0:T(8,128)S(1)}, u32[]{:S(2)}, u32[]{:S(2)}) collective-permute-start(f32[64,512]{1,0:T(8,128)S(1)} %shard_map.95), channel_id=1, source_target_pairs={{0,16},{16,0},{32,48},{48,32},{64,80},{80,64},{96,112},{112,96},{1... | collective-permute-start | bytes 393224 | tf_op jit(solution)/shard_map/ppermute | solution.py:281
  23.2 3.8 %collective-permute-start.3 = (bf16[64,512]{1,0:T(8,128)(2,1)S(1)}, bf16[64,512]{1,0:T(8,128)(2,1)S(1)}, u32[]{:S(2)}, u32[]{:S(2)}) collective-permute-start(bf16[64,512]{1,0:T(8,128)(2,1)S(1)} %add_convert_fusion.p0_ref), channel_id=1, source_target_pairs={{0,96},{16,112},{32,64},{48,80},{64,32},{80,48},{96,0},{112,16},{1... | collective-permute-start | bytes 196616 | tf_op jit(solution)/shard_map/ppermute | solution.py:281
  27.7 1.8 %shard_map.96.v_ref = bf16[512,6144]{1,0:T(8,128)(2,1)S(1)} custom-call(bf16[6144,512]{1,0:T(8,128)(2,1)S(1)} %bitcast.15), custom_call_target="tpu_custom_call" | custom-call | tf_op jit(solution)/shard_map/pallas_call | solution.py:40
  29.5 1.4 %shard_map.97.slot_ref = s32[16]{0:T(128)S(1)} custom-call(s32[16,16]{1,0:T(8,128)S(1)} %copy-done.3, s32[128]{0:T(128)S(1)} %copy-done.4), custom_call_target="tpu_custom_call" | custom-call | tf_op jit(solution)/shard_map/pallas_call | solution.py:40
  31.6 1.3 %shard_map.98 = (bf16[16,8,512]{2,1,0:T(8,128)(2,1)S(1)}, f32[64,512]{1,0:T(8,128)S(1)}) custom-call(bf16[64,512]{1,0:T(8,128)(2,1)S(1)} %add_convert_fusion.p0_ref, bf16[64,512]{1,0:T(8,128)(2,1)S(1)} %collective-permute-done.1.p2_ref, bf16[64,512]{1,0:T(8,128)(2,1)S(1)} %collective-permute-done.2.p4_ref, ...), custom_call_target="tpu_custom_call" | custom-call | tf_op jit(solution)/shard_map/pallas_call | solution.py:40
  32.9 9.7 %all_to_all.26.in_ref = bf16[16,8,512]{2,1,0:T(8,128)(2,1)S(1)} all-to-all(bf16[16,8,512]{2,1,0:T(8,128)(2,1)S(1)} %get-tuple-element.56), channel_id=1, replica_groups=mesh['row'=8,'col'=16] {'col'}, dimensions={0} | all-to-all | bytes 262144 | tf_op jit(solution)/shard_map/all_to_all | solution.py:299
  42.6 1.8 %shard_map.99 = (f32[8,512]{1,0:T(8,128)S(1)}, f32[8,128]{1,0:T(8,128)S(1)}, bf16[16,8,512]{2,1,0:T(8,128)(2,1)S(1)}) custom-call(bf16[16,8,512]{2,1,0:T(8,128)(2,1)S(1)} %all_to_all.26.in_ref, bf16[6144,512]{1,0:T(8,128)(2,1)S(1)} %get-tuple-element.57.u_ref, bf16[512,6144]{1,0:T(8,128)(2,1)S(1)} %get-tuple-element.58.ut_ref), custom_call_target="tpu_custom_call" | custom-call | tf_op jit(solution)/shard_map/pallas_call | solution.py:40
  44.4 10.1 %all_to_all.27.in_ref = bf16[16,8,512]{2,1,0:T(8,128)(2,1)S(1)} all-to-all(bf16[16,8,512]{2,1,0:T(8,128)(2,1)S(1)} %get-tuple-element.59), channel_id=1, replica_groups=mesh['row'=8,'col'=16] {'col'}, dimensions={0} | all-to-all | bytes 262144 | tf_op jit(solution)/shard_map/all_to_all | solution.py:299
  54.5 1.3 %shard_map.100.own_ref = f32[72,512]{1,0:T(8,128)S(1)} custom-call(bf16[16,8,512]{2,1,0:T(8,128)(2,1)S(1)} %all_to_all.27.in_ref, s32[64,16]{1,0:T(8,128)S(1)} %broadcast_bitcast_fusion.bound_ref, bf16[6144,512]{1,0:T(8,128)(2,1)S(1)} %bitcast.16), custom_call_target="tpu_custom_call" | custom-call | tf_op jit(solution)/shard_map/pallas_call | solution.py:40
  55.8 4.7 %collective-permute-start.4 = (f32[72,512]{1,0:T(8,128)S(1)}, f32[72,512]{1,0:T(8,128)S(1)}, u32[]{:S(2)}, u32[]{:S(2)}) collective-permute-start(f32[72,512]{1,0:T(8,128)S(1)} %shard_map.100.own_ref), channel_id=1, source_target_pairs={{0,16},{16,0},{32,48},{48,32},{64,80},{80,64},{96,112},{112,96},{1... | collective-permute-start | bytes 442376 | tf_op jit(solution)/shard_map/ppermute | solution.py:281
  60.5 1.0 collective-permute-done.4.other_ref
  61.6 1.0 collective-permute-start.7
  63.1 1.7 %collective-permute-start.5 = (bf16[72,512]{1,0:T(8,128)(2,1)S(1)}, bf16[72,512]{1,0:T(8,128)(2,1)S(1)}, u32[]{:S(2)}, u32[]{:S(2)}) collective-permute-start(bf16[72,512]{1,0:T(8,128)(2,1)S(1)} %shard_map.101.p0_ref), channel_id=1, source_target_pairs={{0,32},{16,48},{32,0},{48,16},{64,96},{80,112},{96,64},{112,80},{1... | collective-permute-start | bytes 221192 | tf_op jit(solution)/shard_map/ppermute | solution.py:281
  64.9 2.2 %shard_map.102.far_ref = bf16[2,4096,512]{2,1,0:T(8,128)(2,1)S(1)} custom-call(bf16[2,512,4096]{2,1,0:T(8,128)(2,1)S(1)} %bitcast.18), custom_call_target="tpu_custom_call" | custom-call | tf_op jit(solution)/shard_map/pallas_call | solution.py:40
  68.2 2.6 %shard_map.103 = (bf16[16,8,1536]{2,1,0:T(8,128)(2,1)S(1)}, f32[64,512]{1,0:T(8,128)S(1)}, f32[64,512]{1,0:T(8,128)S(1)}, f32[8,128]{1,0:T(8,128)S(1)}, bf16[8,1024]{1,0:T(8,128)(2,1)S(1)}) custom-call(bf16[72,512]{1,0:T(8,128)(2,1)S(1)} %shard_map.101.p0_ref, bf16[72,512]{1,0:T(8,128)(2,1)S(1)} %collective-permute-done.5.p2_ref, ...), custom_call_target="tpu_custom_call" | custom-call | tf_op jit(solution)/shard_map/pallas_call | solution.py:40
  70.7 11.1 %all_to_all.28.in_ref = bf16[16,8,1536]{2,1,0:T(8,128)(2,1)S(1)} all-to-all(bf16[16,8,1536]{2,1,0:T(8,128)(2,1)S(1)} %get-tuple-element.69), channel_id=1, replica_groups=mesh['row'=8,'col'=16] {'col'}, dimensions={0} | all-to-all | bytes 786432 | tf_op jit(solution)/shard_map/all_to_all | solution.py:299
  82.5 3.0 %collective-permute-start.8 = (bf16[4,8,1024]{2,1,0:T(8,128)(2,1)S(1)}, bf16[4,8,1024]{2,1,0:T(8,128)(2,1)S(1)}, u32[]{:S(2)}, u32[]{:S(2)}) collective-permute-start(bf16[4,8,1024]{2,1,0:T(8,128)(2,1)S(1)} %get-tuple-element.80), channel_id=1, source_target_pairs={{0,16},{16,0},{32,48},{48,32},{64,80},{80,64},{96,112},{112,96},{1... | collective-permute-start | bytes 196616 | tf_op jit(solution)/shard_map/ppermute | solution.py:281
  85.8 1.7 %shard_map.104 = (f32[8,512]{1,0:T(8,128)S(1)}, f32[8,128]{1,0:T(8,128)S(1)}, f32[128,1,128]{2,1,0:T(1,128)}) custom-call(bf16[16,8,1536]{2,1,0:T(8,128)(2,1)S(1)} %all_to_all.28.in_ref, bf16[6144,512]{1,0:T(8,128)(2,1)S(1)} %get-tuple-element.57.u_ref), custom_call_target="tpu_custom_call" | custom-call | tf_op jit(solution)/shard_map/pallas_call | solution.py:40
  87.5 5.0 %all-to-all-start.4 = ((f32[128,1,128]{2,1,0:T(1,128)}), f32[128,1,128]{2,1,0:T(1,128)S(1)}, u32[]{:S(2)}, u32[]{:S(2)}) async-start(f32[128,1,128]{2,1,0:T(1,128)} %get-tuple-element.70), calls=%async_computation.4 | async-start | bytes 131072 | tf_op jit(solution)/shard_map/all_to_all | solution.py:358
  92.5 3.3 %collective-permute-start.11 = (bf16[8,1024]{1,0:T(8,128)(2,1)S(1)}, bf16[8,1024]{1,0:T(8,128)(2,1)S(1)}, u32[]{:S(2)}, u32[]{:S(2)}) collective-permute-start(bf16[8,1024]{1,0:T(8,128)(2,1)S(1)} %get-tuple-element.81), channel_id=1, source_target_pairs={{0,96},{16,112},{32,64},{48,80},{64,32},{80,48},{96,0},{112,16},{1... | collective-permute-start | bytes 49160 | tf_op jit(solution)/shard_map/ppermute | solution.py:281
  96.5 5.5 %all-to-all-done.4.norm_ref = f32[128,1,128]{2,1,0:T(1,128)S(1)} async-done(((f32[128,1,128]{2,1,0:T(1,128)}), f32[128,1,128]{2,1,0:T(1,128)S(1)}, u32[]{:S(2)}, u32[]{:S(2)}) %all-to-all-start.4) | async-done | bytes 65568 | tf_op jit(solution)/shard_map/all_to_all | solution.py:358
  (40 shorter events, 6.8 us)
Async XLA Ops:
  0.6 18.1 %copy-start = (s32[16,8]{0,1:T(8,128)S(1)}, s32[16,8]{0,1:T(8,128)}, u32[]{:S(2)}) copy-start(s32[16,8]{0,1:T(8,128)} %param.10) | copy-start | bytes 1540
  0.6 18.1 %copy-start.1 = (bf16[16,8,48,512]{3,2,1,0:T(8,128)(2,1)S(1)}, bf16[16,8,48,512]{3,2,1,0:T(8,128)(2,1)}, u32[]{:S(2)}) copy-start(bf16[16,8,48,512]{3,2,1,0:T(8,128)(2,1)} %param.9) | copy-start | bytes 18874372
  20.0 3.1 %collective-permute-start = (f32[64,512]{1,0:T(8,128)S(1)}, f32[64,512]{1,0:T(8,128)S(1)}, u32[]{:S(2)}, u32[]{:S(2)}) collective-permute-start(f32[64,512]{1,0:T(8,128)S(1)} %shard_map.95), channel_id=1, source_target_pairs={{0,16},{16,0},{32,48},{48,32},{64,80},{80,64},{96,112},{112,96},{1... | collective-permute-start | bytes 393224 | tf_op jit(solution)/shard_map/ppermute | solution.py:281
  23.1 6.4 %copy-start.3 = (s32[16,16]{1,0:T(8,128)S(1)}, s32[16,16]{1,0:T(8,128)}, u32[]{:S(2)}) copy-start(s32[16,16]{1,0:T(8,128)} %target_ref) | copy-start | bytes 3076
  23.1 6.4 %copy-start.4 = (s32[128]{0:T(128)S(1)}, s32[128]{0:T(128)}, u32[]{:S(2)}) copy-start(s32[128]{0:T(128)} %order_ref) | copy-start | bytes 1540
  23.2 7.7 %collective-permute-start.3 = (bf16[64,512]{1,0:T(8,128)(2,1)S(1)}, bf16[64,512]{1,0:T(8,128)(2,1)S(1)}, u32[]{:S(2)}, u32[]{:S(2)}) collective-permute-start(bf16[64,512]{1,0:T(8,128)(2,1)S(1)} %add_convert_fusion.p0_ref), channel_id=1, source_target_pairs={{0,96},{16,112},{32,64},{48,80},{64,32},{80,48},{96,0},{112,16},{1... | collective-permute-start | bytes 196616 | tf_op jit(solution)/shard_map/ppermute | solution.py:281
  27.0 4.6 %collective-permute-start.2 = (bf16[64,512]{1,0:T(8,128)(2,1)S(1)}, bf16[64,512]{1,0:T(8,128)(2,1)S(1)}, u32[]{:S(2)}, u32[]{:S(2)}) collective-permute-start(bf16[64,512]{1,0:T(8,128)(2,1)S(1)} %add_convert_fusion.p0_ref), channel_id=1, source_target_pairs={{0,64},{16,80},{32,96},{48,112},{64,0},{80,16},{96,32},{112,48},{1... | collective-permute-start | bytes 196616 | tf_op jit(solution)/shard_map/ppermute | solution.py:281
  27.0 4.6 %collective-permute-start.1 = (bf16[64,512]{1,0:T(8,128)(2,1)S(1)}, bf16[64,512]{1,0:T(8,128)(2,1)S(1)}, u32[]{:S(2)}, u32[]{:S(2)}) collective-permute-start(bf16[64,512]{1,0:T(8,128)(2,1)S(1)} %add_convert_fusion.p0_ref), channel_id=1, source_target_pairs={{0,32},{16,48},{32,0},{48,16},{64,96},{80,112},{96,64},{112,80},{1... | collective-permute-start | bytes 196616 | tf_op jit(solution)/shard_map/ppermute | solution.py:281
  42.6 22.3 %slice-start = ((s8[8388608]{0:T(1024)(128)(4,1)}), s8[4194304]{0:T(1024)(128)(4,1)S(1)}, s32[]{:S(2)}) async-start(s8[8388608]{0:T(1024)(128)(4,1)} %bitcast.17), calls=%async_computation.5 | async-start | bytes 8388608
  42.6 22.3 %slice-start.1 = ((s8[8388608]{0:T(1024)(128)(4,1)}), s8[4194304]{0:T(1024)(128)(4,1)S(1)}, s32[]{:S(2)}) async-start(s8[8388608]{0:T(1024)(128)(4,1)} %bitcast.17), calls=%async_computation.6 | async-start | bytes 8388608
  55.8 5.7 %collective-permute-start.4 = (f32[72,512]{1,0:T(8,128)S(1)}, f32[72,512]{1,0:T(8,128)S(1)}, u32[]{:S(2)}, u32[]{:S(2)}) collective-permute-start(f32[72,512]{1,0:T(8,128)S(1)} %shard_map.100.own_ref), channel_id=1, source_target_pairs={{0,16},{16,0},{32,48},{48,32},{64,80},{80,64},{96,112},{112,96},{1... | collective-permute-start | bytes 442376 | tf_op jit(solution)/shard_map/ppermute | solution.py:281
  61.6 5.5 %collective-permute-start.7 = (bf16[72,512]{1,0:T(8,128)(2,1)S(1)}, bf16[72,512]{1,0:T(8,128)(2,1)S(1)}, u32[]{:S(2)}, u32[]{:S(2)}) collective-permute-start(bf16[72,512]{1,0:T(8,128)(2,1)S(1)} %shard_map.101.p0_ref), channel_id=1, source_target_pairs={{0,96},{16,112},{32,64},{48,80},{64,32},{80,48},{96,0},{112,16},{1... | collective-permute-start | bytes 221192 | tf_op jit(solution)/shard_map/ppermute | solution.py:281
  62.6 4.8 %collective-permute-start.6 = (bf16[72,512]{1,0:T(8,128)(2,1)S(1)}, bf16[72,512]{1,0:T(8,128)(2,1)S(1)}, u32[]{:S(2)}, u32[]{:S(2)}) collective-permute-start(bf16[72,512]{1,0:T(8,128)(2,1)S(1)} %shard_map.101.p0_ref), channel_id=1, source_target_pairs={{0,64},{16,80},{32,96},{48,112},{64,0},{80,16},{96,32},{112,48},{1... | collective-permute-start | bytes 221192 | tf_op jit(solution)/shard_map/ppermute | solution.py:281
  63.1 5.0 %collective-permute-start.5 = (bf16[72,512]{1,0:T(8,128)(2,1)S(1)}, bf16[72,512]{1,0:T(8,128)(2,1)S(1)}, u32[]{:S(2)}, u32[]{:S(2)}) collective-permute-start(bf16[72,512]{1,0:T(8,128)(2,1)S(1)} %shard_map.101.p0_ref), channel_id=1, source_target_pairs={{0,32},{16,48},{32,0},{48,16},{64,96},{80,112},{96,64},{112,80},{1... | collective-permute-start | bytes 221192 | tf_op jit(solution)/shard_map/ppermute | solution.py:281
  70.7 31.3 %copy-start.2 = (f32[8,512]{1,0:T(8,128)S(1)}, f32[8,512]{1,0:T(8,128)}, u32[]{:S(2)}) copy-start(f32[8,512]{1,0:T(8,128)} %res_ref.1) | copy-start | bytes 49156
  82.5 9.9 %collective-permute-start.8 = (bf16[4,8,1024]{2,1,0:T(8,128)(2,1)S(1)}, bf16[4,8,1024]{2,1,0:T(8,128)(2,1)S(1)}, u32[]{:S(2)}, u32[]{:S(2)}) collective-permute-start(bf16[4,8,1024]{2,1,0:T(8,128)(2,1)S(1)} %get-tuple-element.80), channel_id=1, source_target_pairs={{0,16},{16,0},{32,48},{48,32},{64,80},{80,64},{96,112},{112,96},{1... | collective-permute-start | bytes 196616 | tf_op jit(solution)/shard_map/ppermute | solution.py:281
  85.5 11.0 %collective-permute-start.12 = (bf16[8,1024]{1,0:T(8,128)(2,1)S(1)}, bf16[8,1024]{1,0:T(8,128)(2,1)S(1)}, u32[]{:S(2)}, u32[]{:S(2)}) collective-permute-start(bf16[8,1024]{1,0:T(8,128)(2,1)S(1)} %get-tuple-element.78.even_ref), channel_id=1, source_target_pairs={{0,1},{1,0},{2,3},{3,2},{4,5},{5,4},{6,7},{7,6},{8,9},{9,8},{10,11... | collective-permute-start | bytes 49160 | tf_op jit(solution)/shard_map/ppermute | solution.py:368
  87.5 14.5 %all-to-all-start.4 = ((f32[128,1,128]{2,1,0:T(1,128)}), f32[128,1,128]{2,1,0:T(1,128)S(1)}, u32[]{:S(2)}, u32[]{:S(2)}) async-start(f32[128,1,128]{2,1,0:T(1,128)} %get-tuple-element.70), calls=%async_computation.4 | async-start | bytes 131072 | tf_op jit(solution)/shard_map/all_to_all | solution.py:358
  92.5 9.5 %collective-permute-start.11 = (bf16[8,1024]{1,0:T(8,128)(2,1)S(1)}, bf16[8,1024]{1,0:T(8,128)(2,1)S(1)}, u32[]{:S(2)}, u32[]{:S(2)}) collective-permute-start(bf16[8,1024]{1,0:T(8,128)(2,1)S(1)} %get-tuple-element.81), channel_id=1, source_target_pairs={{0,96},{16,112},{32,64},{48,80},{64,32},{80,48},{96,0},{112,16},{1... | collective-permute-start | bytes 49160 | tf_op jit(solution)/shard_map/ppermute | solution.py:281
  95.8 6.2 %collective-permute-start.10 = (bf16[8,1024]{1,0:T(8,128)(2,1)S(1)}, bf16[8,1024]{1,0:T(8,128)(2,1)S(1)}, u32[]{:S(2)}, u32[]{:S(2)}) collective-permute-start(bf16[8,1024]{1,0:T(8,128)(2,1)S(1)} %get-tuple-element.82), channel_id=1, source_target_pairs={{0,64},{16,80},{32,96},{48,112},{64,0},{80,16},{96,32},{112,48},{1... | collective-permute-start | bytes 49160 | tf_op jit(solution)/shard_map/ppermute | solution.py:281
  95.9 6.1 %collective-permute-start.9 = (bf16[8,1024]{1,0:T(8,128)(2,1)S(1)}, bf16[8,1024]{1,0:T(8,128)(2,1)S(1)}, u32[]{:S(2)}, u32[]{:S(2)}) collective-permute-start(bf16[8,1024]{1,0:T(8,128)(2,1)S(1)} %get-tuple-element.83), channel_id=1, source_target_pairs={{0,32},{16,48},{32,0},{48,16},{64,96},{80,112},{96,64},{112,80},{1... | collective-permute-start | bytes 49160 | tf_op jit(solution)/shard_map/ppermute | solution.py:281

commit v7 on v6

--- a/solution.py
+++ b/solution.py
@@ -33,7 +33,7 @@
     return total
 
 
-def call(kernel, outs, args, smem=(), hbm=(), keep=(), scratch=(), limit=8, smem_out=False):
+def call(kernel, outs, args, smem=(), hbm=(), keep=(), scratch=(), limit=8, smem_out=False, hbm_out=()):
     vm = pl.BlockSpec(memory_space=pltpu.VMEM)
     sm = pl.BlockSpec(memory_space=pltpu.SMEM)
     far_away = pl.BlockSpec(memory_space=pltpu.HBM)
@@ -46,7 +46,9 @@
         in_specs=[
             sm if at in smem else far_away if at in hbm else vm for at in range(len(args))
         ],
-        out_specs=tuple(sm if smem_out else vm for _ in outs),
+        out_specs=tuple(
+            sm if smem_out else far_away if at in hbm_out else vm for at in range(len(outs))
+        ),
         scratch_shapes=list(scratch),
         compiler_params=pltpu.CompilerParams(vmem_limit_bytes=limit * MIB),
     )(*args)
@@ -206,19 +208,6 @@
             out_ref[i, :, wide : wide + 128] = mine
             out_ref[i, :, far_low : far_low + 2 * patch] = send
 
-    def image_last_kernel(in_ref, u_ref, image_ref, gsq_ref, out_ref):
-        image = image_of(in_ref, u_ref)
-        image_ref[...] = image
-        gsq_ref[...] = jnp.broadcast_to(
-            jnp.sum(gather_sum(in_ref, wide, 128), axis=1, keepdims=True), (dens, 128)
-        )
-        here = lax.broadcasted_iota(jnp.int32, (dens, 128), 0) == lax.broadcasted_iota(
-            jnp.int32, (dens, 128), 1
-        )
-        line = jnp.sum(jnp.where(here, norm_of(image), 0.0), axis=0, keepdims=True)
-        for peer in range(devices):
-            out_ref[peer] = line
-
     def slot_kernel(target_ref, order_ref, slot_ref):
         row, col = lax.axis_index("row"), lax.axis_index("col")
         mine = [order_ref[lax.bitwise_xor(row, m) * peers + col] for m in range(n_row)]
@@ -229,7 +218,23 @@
                 slot = jnp.where(target == mine[m], m, slot)
             slot_ref[source] = slot
 
-    def route_kernel(slot_ref, even_ref, in_ref, keep_ref, give_ref, sum_ref):
+    def image_last_kernel(
+        slot_ref, even_ref, in_ref, u_ref, image_ref, gsq_ref, out_hbm, keep_ref, give_ref,
+        sum_ref, out_ref, sem,
+    ):
+        image = image_of(in_ref, u_ref)
+        image_ref[...] = image
+        gsq_ref[...] = jnp.broadcast_to(
+            jnp.sum(gather_sum(in_ref, wide, 128), axis=1, keepdims=True), (dens, 128)
+        )
+        here = lax.broadcasted_iota(jnp.int32, (dens, 128), 0) == lax.broadcasted_iota(
+            jnp.int32, (dens, 128), 1
+        )
+        line = jnp.sum(jnp.where(here, norm_of(image), 0.0), axis=0, keepdims=True)
+        for peer in range(devices):
+            out_ref[peer] = line
+        leave = pltpu.make_async_copy(out_ref, out_hbm, sem)
+        leave.start()
         sum_ref[...] = jnp.zeros_like(sum_ref)
         sum_ref[n_row // 2] = even_ref[...].astype(F32) * jnp.where(
             lax.axis_index("col") % 2 == 0, 1.0, 0.0
@@ -243,8 +248,9 @@
                 sum_ref[slot] = sum_ref[slot] + piece
 
         for m in range(n_row):
-            out_ref = keep_ref if m % 2 == 0 else give_ref
-            out_ref[m // 2] = sum_ref[m].astype(BF16)
+            to_ref = keep_ref if m % 2 == 0 else give_ref
+            to_ref[m // 2] = sum_ref[m].astype(BF16)
+        leave.wait()
 
     def pair_kernel(own_ref, other_ref, out_ref):
         out_ref[0:tall, :] = (own_ref[0:tall] + other_ref[0:tall]).astype(BF16)
@@ -350,19 +356,20 @@
         arrived + [grad, gsq1, bound, v_flip, far_flip],
     )
     landed = over_col(sent)
-    image2, gsq2, sent = call(
+    image2, gsq2, sent, keep, give = call(
         image_last_kernel,
-        [((dens, patch), F32), ((dens, 128), F32), ((devices, 1, 128), F32)],
-        [landed, u_all],
+        [((dens, patch), F32), ((dens, 128), F32), ((devices, 1, 128), F32)]
+        + [((n_row // 2, dens, 2 * patch), BF16)] * 2,
+        [slot, even, landed, u_all],
+        smem=(0,),
+        hbm_out=(2,),
+        scratch=(
+            pltpu.VMEM((n_row, dens, 2 * patch), F32),
+            pltpu.VMEM((devices, 1, 128), F32),
+            dma(()),
+        ),
     )
     norms = lax.all_to_all(sent, ("row", "col"), split_axis=0, concat_axis=0, tiled=True)
-    keep, give = call(
-        route_kernel,
-        [((n_row // 2, dens, 2 * patch), BF16)] * 2,
-        [slot, even, landed],
-        smem=(0,),
-        scratch=(pltpu.VMEM((n_row, dens, 2 * patch), F32),),
-    )
     near = keep + row_shift(give, 1)
     pieces = [near[0]] + hops([near[k] for k in range(1, n_row // 2)])
     side = lax.ppermute(even, "col", [(c, c ^ 1) for c in range(peers)])

time: 103 us -> 103 us (level)
    pallas_call x13 -> x12, Pallas kernels: 21 us -> 20.8 us  [call(): pl.pallas_call(kernel, out_shape=tuple((pltpu.VMEM(s, d) if at in keep el...]
  transfers between devices with their start and end apart: 14 -> 14, of which waited for: 6 -> 6; matrix products, arithmetic and copies ran while one was open for 0% -> 0% of each run, Pallas kernels for 7% -> 5%
where the time goes in v7:
time: 103 us
  blocking collectives  44.9 us (44%)
  starting transfers between devices  26.9 us (26%)
  Pallas kernels  20.8 us (20%)
  waiting for transfers between devices  9.29 us (9%)
    all_to_all x4, blocking collectives, over_col(): return lax.all_to_all(x, 'col', split_axis=0, concat_axis=0, tiled=True)  44.9 us
    ppermute x12, starting transfers between devices, row_shift(): return lax.ppermute(x, 'row', [(i, i ^ k) for i in range(n_row)])  21.6 us
    pallas_call x12, Pallas kernels, call(): pl.pallas_call(kernel, out_shape=tuple((pltpu.VMEM(s, d) if at in keep el...  20.8 us
    all_to_all x1, waiting for transfers between devices, per_device(): lax.all_to_all(sent, ('row', 'col'), split_axis=0, concat_axis=0, tiled=T...  5.5 us
    all_to_all x1, starting transfers between devices, per_device(): lax.all_to_all(sent, ('row', 'col'), split_axis=0, concat_axis=0, tiled=T...  4.98 us
    ppermute x12, waiting for transfers between devices, row_shift(): return lax.ppermute(x, 'row', [(i, i ^ k) for i in range(n_row)])  3.79 us
  transfers between devices with their start and end apart: 14, of which 6 were waited for; matrix products, arithmetic and copies ran while one was open for 0% of the time, Pallas kernels for 5%

profile of v7, /device:TPU:1, one launch (start us, length us, event | category | flops | bytes accessed | tf_op | source)
XLA Modules:
  0.0 102.8 jit_solution(7555637216065345086)
XLA Ops:
  0.7 3.9 %shard_map.94 = (bf16[16,8,384]{2,1,0:T(8,128)(2,1)S(1)}, bf16[6144,512]{1,0:T(8,128)(2,1)S(1)}, bf16[512,6144]{1,0:T(8,128)(2,1)S(1)}) custom-call(f32[8,512]{1,0:T(8,128)} %res_ref.1, bf16[6144,512]{1,0:T(8,128)(2,1)} %bitcast.19), custom_call_target="tpu_custom_call" | custom-call | tf_op jit(solution)/shard_map/pallas_call | solution.py:40
  4.6 14.1 %all_to_all.25.in_ref = bf16[16,8,384]{2,1,0:T(8,128)(2,1)S(1)} all-to-all(bf16[16,8,384]{2,1,0:T(8,128)(2,1)S(1)} %get-tuple-element.43), channel_id=1, replica_groups=mesh['row'=8,'col'=16] {'col'}, dimensions={0} | all-to-all | bytes 196608 | tf_op jit(solution)/shard_map/all_to_all | solution.py:305
  18.7 1.3 %shard_map.95 = f32[64,512]{1,0:T(8,128)S(1)} custom-call(bf16[16,8,384]{2,1,0:T(8,128)(2,1)S(1)} %all_to_all.25.in_ref, s32[64,16]{1,0:T(8,128)S(1)} %broadcast_bitcast_fusion.bound_ref, bf16[6144,512]{1,0:T(8,128)(2,1)S(1)} %bitcast.14), custom_call_target="tpu_custom_call" | custom-call | tf_op jit(solution)/shard_map/pallas_call | solution.py:40
  20.0 2.1 %collective-permute-start = (f32[64,512]{1,0:T(8,128)S(1)}, f32[64,512]{1,0:T(8,128)S(1)}, u32[]{:S(2)}, u32[]{:S(2)}) collective-permute-start(f32[64,512]{1,0:T(8,128)S(1)} %shard_map.95), channel_id=1, source_target_pairs={{0,16},{16,0},{32,48},{48,32},{64,80},{80,64},{96,112},{112,96},{1... | collective-permute-start | bytes 393224 | tf_op jit(solution)/shard_map/ppermute | solution.py:287
  23.2 3.8 %collective-permute-start.3 = (bf16[64,512]{1,0:T(8,128)(2,1)S(1)}, bf16[64,512]{1,0:T(8,128)(2,1)S(1)}, u32[]{:S(2)}, u32[]{:S(2)}) collective-permute-start(bf16[64,512]{1,0:T(8,128)(2,1)S(1)} %add_convert_fusion.p0_ref), channel_id=1, source_target_pairs={{0,96},{16,112},{32,64},{48,80},{64,32},{80,48},{96,0},{112,16},{1... | collective-permute-start | bytes 196616 | tf_op jit(solution)/shard_map/ppermute | solution.py:287
  27.7 1.8 %shard_map.96.v_ref = bf16[512,6144]{1,0:T(8,128)(2,1)S(1)} custom-call(bf16[6144,512]{1,0:T(8,128)(2,1)S(1)} %bitcast.15), custom_call_target="tpu_custom_call" | custom-call | tf_op jit(solution)/shard_map/pallas_call | solution.py:40
  29.5 1.4 %shard_map.97.slot_ref = s32[16]{0:T(128)S(1)} custom-call(s32[16,16]{1,0:T(8,128)S(1)} %copy-done.3, s32[128]{0:T(128)S(1)} %copy-done.4), custom_call_target="tpu_custom_call" | custom-call | tf_op jit(solution)/shard_map/pallas_call | solution.py:40
  31.6 1.3 %shard_map.98 = (bf16[16,8,512]{2,1,0:T(8,128)(2,1)S(1)}, f32[64,512]{1,0:T(8,128)S(1)}) custom-call(bf16[64,512]{1,0:T(8,128)(2,1)S(1)} %add_convert_fusion.p0_ref, bf16[64,512]{1,0:T(8,128)(2,1)S(1)} %collective-permute-done.1.p2_ref, bf16[64,512]{1,0:T(8,128)(2,1)S(1)} %collective-permute-done.2.p4_ref, ...), custom_call_target="tpu_custom_call" | custom-call | tf_op jit(solution)/shard_map/pallas_call | solution.py:40
  32.9 9.7 %all_to_all.26.in_ref = bf16[16,8,512]{2,1,0:T(8,128)(2,1)S(1)} all-to-all(bf16[16,8,512]{2,1,0:T(8,128)(2,1)S(1)} %get-tuple-element.57), channel_id=1, replica_groups=mesh['row'=8,'col'=16] {'col'}, dimensions={0} | all-to-all | bytes 262144 | tf_op jit(solution)/shard_map/all_to_all | solution.py:305
  42.6 1.8 %shard_map.99 = (f32[8,512]{1,0:T(8,128)S(1)}, f32[8,128]{1,0:T(8,128)S(1)}, bf16[16,8,512]{2,1,0:T(8,128)(2,1)S(1)}) custom-call(bf16[16,8,512]{2,1,0:T(8,128)(2,1)S(1)} %all_to_all.26.in_ref, bf16[6144,512]{1,0:T(8,128)(2,1)S(1)} %get-tuple-element.58.u_ref, bf16[512,6144]{1,0:T(8,128)(2,1)S(1)} %get-tuple-element.59.ut_ref), custom_call_target="tpu_custom_call" | custom-call | tf_op jit(solution)/shard_map/pallas_call | solution.py:40
  44.4 10.1 %all_to_all.27.in_ref = bf16[16,8,512]{2,1,0:T(8,128)(2,1)S(1)} all-to-all(bf16[16,8,512]{2,1,0:T(8,128)(2,1)S(1)} %get-tuple-element.60), channel_id=1, replica_groups=mesh['row'=8,'col'=16] {'col'}, dimensions={0} | all-to-all | bytes 262144 | tf_op jit(solution)/shard_map/all_to_all | solution.py:305
  54.5 1.3 %shard_map.100.own_ref = f32[72,512]{1,0:T(8,128)S(1)} custom-call(bf16[16,8,512]{2,1,0:T(8,128)(2,1)S(1)} %all_to_all.27.in_ref, s32[64,16]{1,0:T(8,128)S(1)} %broadcast_bitcast_fusion.bound_ref, bf16[6144,512]{1,0:T(8,128)(2,1)S(1)} %bitcast.16), custom_call_target="tpu_custom_call" | custom-call | tf_op jit(solution)/shard_map/pallas_call | solution.py:40
  55.8 4.7 %collective-permute-start.4 = (f32[72,512]{1,0:T(8,128)S(1)}, f32[72,512]{1,0:T(8,128)S(1)}, u32[]{:S(2)}, u32[]{:S(2)}) collective-permute-start(f32[72,512]{1,0:T(8,128)S(1)} %shard_map.100.own_ref), channel_id=1, source_target_pairs={{0,16},{16,0},{32,48},{48,32},{64,80},{80,64},{96,112},{112,96},{1... | collective-permute-start | bytes 442376 | tf_op jit(solution)/shard_map/ppermute | solution.py:287
  60.5 1.0 collective-permute-done.4.other_ref
  61.6 1.0 collective-permute-start.7
  63.1 1.7 %collective-permute-start.5 = (bf16[72,512]{1,0:T(8,128)(2,1)S(1)}, bf16[72,512]{1,0:T(8,128)(2,1)S(1)}, u32[]{:S(2)}, u32[]{:S(2)}) collective-permute-start(bf16[72,512]{1,0:T(8,128)(2,1)S(1)} %shard_map.101.p0_ref), channel_id=1, source_target_pairs={{0,32},{16,48},{32,0},{48,16},{64,96},{80,112},{96,64},{112,80},{1... | collective-permute-start | bytes 221192 | tf_op jit(solution)/shard_map/ppermute | solution.py:287
  64.9 2.2 %shard_map.102.far_ref = bf16[2,4096,512]{2,1,0:T(8,128)(2,1)S(1)} custom-call(bf16[2,512,4096]{2,1,0:T(8,128)(2,1)S(1)} %bitcast.18), custom_call_target="tpu_custom_call" | custom-call | tf_op jit(solution)/shard_map/pallas_call | solution.py:40
  68.2 2.6 %shard_map.103 = (bf16[16,8,1536]{2,1,0:T(8,128)(2,1)S(1)}, f32[64,512]{1,0:T(8,128)S(1)}, f32[64,512]{1,0:T(8,128)S(1)}, f32[8,128]{1,0:T(8,128)S(1)}, bf16[8,1024]{1,0:T(8,128)(2,1)S(1)}) custom-call(bf16[72,512]{1,0:T(8,128)(2,1)S(1)} %shard_map.101.p0_ref, bf16[72,512]{1,0:T(8,128)(2,1)S(1)} %collective-permute-done.5.p2_ref, ...), custom_call_target="tpu_custom_call" | custom-call | tf_op jit(solution)/shard_map/pallas_call | solution.py:40
  70.7 11.1 %all_to_all.28.in_ref = bf16[16,8,1536]{2,1,0:T(8,128)(2,1)S(1)} all-to-all(bf16[16,8,1536]{2,1,0:T(8,128)(2,1)S(1)} %get-tuple-element.71), channel_id=1, replica_groups=mesh['row'=8,'col'=16] {'col'}, dimensions={0} | all-to-all | bytes 786432 | tf_op jit(solution)/shard_map/all_to_all | solution.py:305
  81.8 2.2 %shard_map.104 = (f32[8,512]{1,0:T(8,128)S(1)}, f32[8,128]{1,0:T(8,128)S(1)}, f32[128,1,128]{2,1,0:T(1,128)}, bf16[4,8,1024]{2,1,0:T(8,128)(2,1)S(1)}, bf16[4,8,1024]{2,1,0:T(8,128)(2,1)S(1)}) custom-call(s32[16]{0:T(128)S(1)} %shard_map.97.slot_ref, bf16[8,1024]{1,0:T(8,128)(2,1)S(1)} %get-tuple-element.70.even_ref, ...), custom_call_target="tpu_custom_call" | custom-call | tf_op jit(solution)/shard_map/pallas_call | solution.py:40
  84.0 3.0 %collective-permute-start.8 = (bf16[4,8,1024]{2,1,0:T(8,128)(2,1)S(1)}, bf16[4,8,1024]{2,1,0:T(8,128)(2,1)S(1)}, u32[]{:S(2)}, u32[]{:S(2)}) collective-permute-start(bf16[4,8,1024]{2,1,0:T(8,128)(2,1)S(1)} %get-tuple-element.80), channel_id=1, source_target_pairs={{0,16},{16,0},{32,48},{48,32},{64,80},{80,64},{96,112},{112,96},{1... | collective-permute-start | bytes 196616 | tf_op jit(solution)/shard_map/ppermute | solution.py:287
  87.3 5.0 %all-to-all-start.4 = ((f32[128,1,128]{2,1,0:T(1,128)}), f32[128,1,128]{2,1,0:T(1,128)S(1)}, u32[]{:S(2)}, u32[]{:S(2)}) async-start(f32[128,1,128]{2,1,0:T(1,128)} %get-tuple-element.72), calls=%async_computation.4 | async-start | bytes 131072 | tf_op jit(solution)/shard_map/all_to_all | solution.py:372
  92.3 3.3 %collective-permute-start.11 = (bf16[8,1024]{1,0:T(8,128)(2,1)S(1)}, bf16[8,1024]{1,0:T(8,128)(2,1)S(1)}, u32[]{:S(2)}, u32[]{:S(2)}) collective-permute-start(bf16[8,1024]{1,0:T(8,128)(2,1)S(1)} %get-tuple-element.81), channel_id=1, source_target_pairs={{0,96},{16,112},{32,64},{48,80},{64,32},{80,48},{96,0},{112,16},{1... | collective-permute-start | bytes 49160 | tf_op jit(solution)/shard_map/ppermute | solution.py:287
  96.3 5.5 %all-to-all-done.4.norm_ref = f32[128,1,128]{2,1,0:T(1,128)S(1)} async-done(((f32[128,1,128]{2,1,0:T(1,128)}), f32[128,1,128]{2,1,0:T(1,128)S(1)}, u32[]{:S(2)}, u32[]{:S(2)}) %all-to-all-start.4) | async-done | bytes 65568 | tf_op jit(solution)/shard_map/all_to_all | solution.py:372
  (39 shorter events, 6.1 us)
Async XLA Ops:
  0.6 18.1 %copy-start = (s32[16,8]{0,1:T(8,128)S(1)}, s32[16,8]{0,1:T(8,128)}, u32[]{:S(2)}) copy-start(s32[16,8]{0,1:T(8,128)} %param.10) | copy-start | bytes 1540
  0.6 18.1 %copy-start.1 = (bf16[16,8,48,512]{3,2,1,0:T(8,128)(2,1)S(1)}, bf16[16,8,48,512]{3,2,1,0:T(8,128)(2,1)}, u32[]{:S(2)}) copy-start(bf16[16,8,48,512]{3,2,1,0:T(8,128)(2,1)} %param.9) | copy-start | bytes 18874372
  20.0 3.1 %collective-permute-start = (f32[64,512]{1,0:T(8,128)S(1)}, f32[64,512]{1,0:T(8,128)S(1)}, u32[]{:S(2)}, u32[]{:S(2)}) collective-permute-start(f32[64,512]{1,0:T(8,128)S(1)} %shard_map.95), channel_id=1, source_target_pairs={{0,16},{16,0},{32,48},{48,32},{64,80},{80,64},{96,112},{112,96},{1... | collective-permute-start | bytes 393224 | tf_op jit(solution)/shard_map/ppermute | solution.py:287
  23.1 6.4 %copy-start.3 = (s32[16,16]{1,0:T(8,128)S(1)}, s32[16,16]{1,0:T(8,128)}, u32[]{:S(2)}) copy-start(s32[16,16]{1,0:T(8,128)} %target_ref) | copy-start | bytes 3076
  23.1 6.4 %copy-start.4 = (s32[128]{0:T(128)S(1)}, s32[128]{0:T(128)}, u32[]{:S(2)}) copy-start(s32[128]{0:T(128)} %order_ref) | copy-start | bytes 1540
  23.2 7.7 %collective-permute-start.3 = (bf16[64,512]{1,0:T(8,128)(2,1)S(1)}, bf16[64,512]{1,0:T(8,128)(2,1)S(1)}, u32[]{:S(2)}, u32[]{:S(2)}) collective-permute-start(bf16[64,512]{1,0:T(8,128)(2,1)S(1)} %add_convert_fusion.p0_ref), channel_id=1, source_target_pairs={{0,96},{16,112},{32,64},{48,80},{64,32},{80,48},{96,0},{112,16},{1... | collective-permute-start | bytes 196616 | tf_op jit(solution)/shard_map/ppermute | solution.py:287
  27.0 4.6 %collective-permute-start.2 = (bf16[64,512]{1,0:T(8,128)(2,1)S(1)}, bf16[64,512]{1,0:T(8,128)(2,1)S(1)}, u32[]{:S(2)}, u32[]{:S(2)}) collective-permute-start(bf16[64,512]{1,0:T(8,128)(2,1)S(1)} %add_convert_fusion.p0_ref), channel_id=1, source_target_pairs={{0,64},{16,80},{32,96},{48,112},{64,0},{80,16},{96,32},{112,48},{1... | collective-permute-start | bytes 196616 | tf_op jit(solution)/shard_map/ppermute | solution.py:287
  27.0 4.6 %collective-permute-start.1 = (bf16[64,512]{1,0:T(8,128)(2,1)S(1)}, bf16[64,512]{1,0:T(8,128)(2,1)S(1)}, u32[]{:S(2)}, u32[]{:S(2)}) collective-permute-start(bf16[64,512]{1,0:T(8,128)(2,1)S(1)} %add_convert_fusion.p0_ref), channel_id=1, source_target_pairs={{0,32},{16,48},{32,0},{48,16},{64,96},{80,112},{96,64},{112,80},{1... | collective-permute-start | bytes 196616 | tf_op jit(solution)/shard_map/ppermute | solution.py:287
  42.6 22.3 %slice-start = ((s8[8388608]{0:T(1024)(128)(4,1)}), s8[4194304]{0:T(1024)(128)(4,1)S(1)}, s32[]{:S(2)}) async-start(s8[8388608]{0:T(1024)(128)(4,1)} %bitcast.17), calls=%async_computation.5 | async-start | bytes 8388608
  42.6 22.3 %slice-start.1 = ((s8[8388608]{0:T(1024)(128)(4,1)}), s8[4194304]{0:T(1024)(128)(4,1)S(1)}, s32[]{:S(2)}) async-start(s8[8388608]{0:T(1024)(128)(4,1)} %bitcast.17), calls=%async_computation.6 | async-start | bytes 8388608
  55.8 5.7 %collective-permute-start.4 = (f32[72,512]{1,0:T(8,128)S(1)}, f32[72,512]{1,0:T(8,128)S(1)}, u32[]{:S(2)}, u32[]{:S(2)}) collective-permute-start(f32[72,512]{1,0:T(8,128)S(1)} %shard_map.100.own_ref), channel_id=1, source_target_pairs={{0,16},{16,0},{32,48},{48,32},{64,80},{80,64},{96,112},{112,96},{1... | collective-permute-start | bytes 442376 | tf_op jit(solution)/shard_map/ppermute | solution.py:287
  61.6 5.5 %collective-permute-start.7 = (bf16[72,512]{1,0:T(8,128)(2,1)S(1)}, bf16[72,512]{1,0:T(8,128)(2,1)S(1)}, u32[]{:S(2)}, u32[]{:S(2)}) collective-permute-start(bf16[72,512]{1,0:T(8,128)(2,1)S(1)} %shard_map.101.p0_ref), channel_id=1, source_target_pairs={{0,96},{16,112},{32,64},{48,80},{64,32},{80,48},{96,0},{112,16},{1... | collective-permute-start | bytes 221192 | tf_op jit(solution)/shard_map/ppermute | solution.py:287
  62.6 4.8 %collective-permute-start.6 = (bf16[72,512]{1,0:T(8,128)(2,1)S(1)}, bf16[72,512]{1,0:T(8,128)(2,1)S(1)}, u32[]{:S(2)}, u32[]{:S(2)}) collective-permute-start(bf16[72,512]{1,0:T(8,128)(2,1)S(1)} %shard_map.101.p0_ref), channel_id=1, source_target_pairs={{0,64},{16,80},{32,96},{48,112},{64,0},{80,16},{96,32},{112,48},{1... | collective-permute-start | bytes 221192 | tf_op jit(solution)/shard_map/ppermute | solution.py:287
  63.1 5.0 %collective-permute-start.5 = (bf16[72,512]{1,0:T(8,128)(2,1)S(1)}, bf16[72,512]{1,0:T(8,128)(2,1)S(1)}, u32[]{:S(2)}, u32[]{:S(2)}) collective-permute-start(bf16[72,512]{1,0:T(8,128)(2,1)S(1)} %shard_map.101.p0_ref), channel_id=1, source_target_pairs={{0,32},{16,48},{32,0},{48,16},{64,96},{80,112},{96,64},{112,80},{1... | collective-permute-start | bytes 221192 | tf_op jit(solution)/shard_map/ppermute | solution.py:287
  70.7 31.1 %copy-start.2 = (f32[8,512]{1,0:T(8,128)S(1)}, f32[8,512]{1,0:T(8,128)}, u32[]{:S(2)}) copy-start(f32[8,512]{1,0:T(8,128)} %res_ref.1) | copy-start | bytes 49156
  84.0 8.3 %collective-permute-start.8 = (bf16[4,8,1024]{2,1,0:T(8,128)(2,1)S(1)}, bf16[4,8,1024]{2,1,0:T(8,128)(2,1)S(1)}, u32[]{:S(2)}, u32[]{:S(2)}) collective-permute-start(bf16[4,8,1024]{2,1,0:T(8,128)(2,1)S(1)} %get-tuple-element.80), channel_id=1, source_target_pairs={{0,16},{16,0},{32,48},{48,32},{64,80},{80,64},{96,112},{112,96},{1... | collective-permute-start | bytes 196616 | tf_op jit(solution)/shard_map/ppermute | solution.py:287
  87.0 9.3 %collective-permute-start.12 = (bf16[8,1024]{1,0:T(8,128)(2,1)S(1)}, bf16[8,1024]{1,0:T(8,128)(2,1)S(1)}, u32[]{:S(2)}, u32[]{:S(2)}) collective-permute-start(bf16[8,1024]{1,0:T(8,128)(2,1)S(1)} %get-tuple-element.70.even_ref), channel_id=1, source_target_pairs={{0,1},{1,0},{2,3},{3,2},{4,5},{5,4},{6,7},{7,6},{8,9},{9,8},{10,11... | collective-permute-start | bytes 49160 | tf_op jit(solution)/shard_map/ppermute | solution.py:375
  87.3 14.5 %all-to-all-start.4 = ((f32[128,1,128]{2,1,0:T(1,128)}), f32[128,1,128]{2,1,0:T(1,128)S(1)}, u32[]{:S(2)}, u32[]{:S(2)}) async-start(f32[128,1,128]{2,1,0:T(1,128)} %get-tuple-element.72), calls=%async_computation.4 | async-start | bytes 131072 | tf_op jit(solution)/shard_map/all_to_all | solution.py:372
  92.3 9.5 %collective-permute-start.11 = (bf16[8,1024]{1,0:T(8,128)(2,1)S(1)}, bf16[8,1024]{1,0:T(8,128)(2,1)S(1)}, u32[]{:S(2)}, u32[]{:S(2)}) collective-permute-start(bf16[8,1024]{1,0:T(8,128)(2,1)S(1)} %get-tuple-element.81), channel_id=1, source_target_pairs={{0,96},{16,112},{32,64},{48,80},{64,32},{80,48},{96,0},{112,16},{1... | collective-permute-start | bytes 49160 | tf_op jit(solution)/shard_map/ppermute | solution.py:287
  95.7 6.2 %collective-permute-start.10 = (bf16[8,1024]{1,0:T(8,128)(2,1)S(1)}, bf16[8,1024]{1,0:T(8,128)(2,1)S(1)}, u32[]{:S(2)}, u32[]{:S(2)}) collective-permute-start(bf16[8,1024]{1,0:T(8,128)(2,1)S(1)} %get-tuple-element.82), channel_id=1, source_target_pairs={{0,64},{16,80},{32,96},{48,112},{64,0},{80,16},{96,32},{112,48},{1... | collective-permute-start | bytes 49160 | tf_op jit(solution)/shard_map/ppermute | solution.py:287
  95.8 6.1 %collective-permute-start.9 = (bf16[8,1024]{1,0:T(8,128)(2,1)S(1)}, bf16[8,1024]{1,0:T(8,128)(2,1)S(1)}, u32[]{:S(2)}, u32[]{:S(2)}) collective-permute-start(bf16[8,1024]{1,0:T(8,128)(2,1)S(1)} %get-tuple-element.83), channel_id=1, source_target_pairs={{0,32},{16,48},{32,0},{48,16},{64,96},{80,112},{96,64},{112,80},{1... | collective-permute-start | bytes 49160 | tf_op jit(solution)/shard_map/ppermute | solution.py:287

commit v8 on v7

--- a/solution.py
+++ b/solution.py
@@ -129,9 +129,9 @@
 
     def coefficients(grad, bound_ref, v_ref, out_ref):
         half = grad.astype(BF16)
-        for i in range(0, rows, 2):
-            both = dot_nn(half, v_ref[:, i * wide : (i + 2) * wide])
-            for k in range(2):
+        for i in range(0, rows, 4):
+            both = dot_nn(half, v_ref[:, i * wide : (i + 4) * wide])
+            for k in range(4):
                 part = jnp.where(
                     kept_lanes(bound_ref, i + k), both[:, k * wide : (k + 1) * wide], 0.0
                 )

time: 103 us -> 103 us (level)
  no operation moved by 1% of the time
where the time goes in v8:
time: 103 us
  blocking collectives  44.9 us (44%)
  starting transfers between devices  26.9 us (26%)
  Pallas kernels  20.8 us (20%)
  waiting for transfers between devices  9.29 us (9%)
    all_to_all x4, blocking collectives, over_col(): return lax.all_to_all(x, 'col', split_axis=0, concat_axis=0, tiled=True)  44.9 us
    ppermute x12, starting transfers between devices, row_shift(): return lax.ppermute(x, 'row', [(i, i ^ k) for i in range(n_row)])  21.6 us
    pallas_call x12, Pallas kernels, call(): pl.pallas_call(kernel, out_shape=tuple((pltpu.VMEM(s, d) if at in keep el...  20.8 us
    all_to_all x1, waiting for transfers between devices, per_device(): lax.all_to_all(sent, ('row', 'col'), split_axis=0, concat_axis=0, tiled=T...  5.5 us
    all_to_all x1, starting transfers between devices, per_device(): lax.all_to_all(sent, ('row', 'col'), split_axis=0, concat_axis=0, tiled=T...  4.98 us
    ppermute x12, waiting for transfers between devices, row_shift(): return lax.ppermute(x, 'row', [(i, i ^ k) for i in range(n_row)])  3.79 us
  transfers between devices with their start and end apart: 14, of which 6 were waited for; matrix products, arithmetic and copies ran while one was open for 0% of the time, Pallas kernels for 5%

profile of v8, /device:TPU:1, one launch (start us, length us, event | category | flops | bytes accessed | tf_op | source)
XLA Modules:
  0.0 102.8 jit_solution(7555637216065345086)
XLA Ops:
  0.7 3.9 %shard_map.94 = (bf16[16,8,384]{2,1,0:T(8,128)(2,1)S(1)}, bf16[6144,512]{1,0:T(8,128)(2,1)S(1)}, bf16[512,6144]{1,0:T(8,128)(2,1)S(1)}) custom-call(f32[8,512]{1,0:T(8,128)} %res_ref.1, bf16[6144,512]{1,0:T(8,128)(2,1)} %bitcast.19), custom_call_target="tpu_custom_call" | custom-call | tf_op jit(solution)/shard_map/pallas_call | solution.py:40
  4.6 14.1 %all_to_all.25.in_ref = bf16[16,8,384]{2,1,0:T(8,128)(2,1)S(1)} all-to-all(bf16[16,8,384]{2,1,0:T(8,128)(2,1)S(1)} %get-tuple-element.43), channel_id=1, replica_groups=mesh['row'=8,'col'=16] {'col'}, dimensions={0} | all-to-all | bytes 196608 | tf_op jit(solution)/shard_map/all_to_all | solution.py:305
  18.7 1.3 %shard_map.95 = f32[64,512]{1,0:T(8,128)S(1)} custom-call(bf16[16,8,384]{2,1,0:T(8,128)(2,1)S(1)} %all_to_all.25.in_ref, s32[64,16]{1,0:T(8,128)S(1)} %broadcast_bitcast_fusion.bound_ref, bf16[6144,512]{1,0:T(8,128)(2,1)S(1)} %bitcast.14), custom_call_target="tpu_custom_call" | custom-call | tf_op jit(solution)/shard_map/pallas_call | solution.py:40
  20.0 2.1 %collective-permute-start = (f32[64,512]{1,0:T(8,128)S(1)}, f32[64,512]{1,0:T(8,128)S(1)}, u32[]{:S(2)}, u32[]{:S(2)}) collective-permute-start(f32[64,512]{1,0:T(8,128)S(1)} %shard_map.95), channel_id=1, source_target_pairs={{0,16},{16,0},{32,48},{48,32},{64,80},{80,64},{96,112},{112,96},{1... | collective-permute-start | bytes 393224 | tf_op jit(solution)/shard_map/ppermute | solution.py:287
  23.2 3.8 %collective-permute-start.3 = (bf16[64,512]{1,0:T(8,128)(2,1)S(1)}, bf16[64,512]{1,0:T(8,128)(2,1)S(1)}, u32[]{:S(2)}, u32[]{:S(2)}) collective-permute-start(bf16[64,512]{1,0:T(8,128)(2,1)S(1)} %add_convert_fusion.p0_ref), channel_id=1, source_target_pairs={{0,96},{16,112},{32,64},{48,80},{64,32},{80,48},{96,0},{112,16},{1... | collective-permute-start | bytes 196616 | tf_op jit(solution)/shard_map/ppermute | solution.py:287
  27.7 1.8 %shard_map.96.v_ref = bf16[512,6144]{1,0:T(8,128)(2,1)S(1)} custom-call(bf16[6144,512]{1,0:T(8,128)(2,1)S(1)} %bitcast.15), custom_call_target="tpu_custom_call" | custom-call | tf_op jit(solution)/shard_map/pallas_call | solution.py:40
  29.5 1.4 %shard_map.97.slot_ref = s32[16]{0:T(128)S(1)} custom-call(s32[16,16]{1,0:T(8,128)S(1)} %copy-done.3, s32[128]{0:T(128)S(1)} %copy-done.4), custom_call_target="tpu_custom_call" | custom-call | tf_op jit(solution)/shard_map/pallas_call | solution.py:40
  31.6 1.3 %shard_map.98 = (bf16[16,8,512]{2,1,0:T(8,128)(2,1)S(1)}, f32[64,512]{1,0:T(8,128)S(1)}) custom-call(bf16[64,512]{1,0:T(8,128)(2,1)S(1)} %add_convert_fusion.p0_ref, bf16[64,512]{1,0:T(8,128)(2,1)S(1)} %collective-permute-done.1.p2_ref, bf16[64,512]{1,0:T(8,128)(2,1)S(1)} %collective-permute-done.2.p4_ref, ...), custom_call_target="tpu_custom_call" | custom-call | tf_op jit(solution)/shard_map/pallas_call | solution.py:40
  32.9 9.7 %all_to_all.26.in_ref = bf16[16,8,512]{2,1,0:T(8,128)(2,1)S(1)} all-to-all(bf16[16,8,512]{2,1,0:T(8,128)(2,1)S(1)} %get-tuple-element.57), channel_id=1, replica_groups=mesh['row'=8,'col'=16] {'col'}, dimensions={0} | all-to-all | bytes 262144 | tf_op jit(solution)/shard_map/all_to_all | solution.py:305
  42.6 1.8 %shard_map.99 = (f32[8,512]{1,0:T(8,128)S(1)}, f32[8,128]{1,0:T(8,128)S(1)}, bf16[16,8,512]{2,1,0:T(8,128)(2,1)S(1)}) custom-call(bf16[16,8,512]{2,1,0:T(8,128)(2,1)S(1)} %all_to_all.26.in_ref, bf16[6144,512]{1,0:T(8,128)(2,1)S(1)} %get-tuple-element.58.u_ref, bf16[512,6144]{1,0:T(8,128)(2,1)S(1)} %get-tuple-element.59.ut_ref), custom_call_target="tpu_custom_call" | custom-call | tf_op jit(solution)/shard_map/pallas_call | solution.py:40
  44.4 10.1 %all_to_all.27.in_ref = bf16[16,8,512]{2,1,0:T(8,128)(2,1)S(1)} all-to-all(bf16[16,8,512]{2,1,0:T(8,128)(2,1)S(1)} %get-tuple-element.60), channel_id=1, replica_groups=mesh['row'=8,'col'=16] {'col'}, dimensions={0} | all-to-all | bytes 262144 | tf_op jit(solution)/shard_map/all_to_all | solution.py:305
  54.5 1.3 %shard_map.100.own_ref = f32[72,512]{1,0:T(8,128)S(1)} custom-call(bf16[16,8,512]{2,1,0:T(8,128)(2,1)S(1)} %all_to_all.27.in_ref, s32[64,16]{1,0:T(8,128)S(1)} %broadcast_bitcast_fusion.bound_ref, bf16[6144,512]{1,0:T(8,128)(2,1)S(1)} %bitcast.16), custom_call_target="tpu_custom_call" | custom-call | tf_op jit(solution)/shard_map/pallas_call | solution.py:40
  55.8 4.7 %collective-permute-start.4 = (f32[72,512]{1,0:T(8,128)S(1)}, f32[72,512]{1,0:T(8,128)S(1)}, u32[]{:S(2)}, u32[]{:S(2)}) collective-permute-start(f32[72,512]{1,0:T(8,128)S(1)} %shard_map.100.own_ref), channel_id=1, source_target_pairs={{0,16},{16,0},{32,48},{48,32},{64,80},{80,64},{96,112},{112,96},{1... | collective-permute-start | bytes 442376 | tf_op jit(solution)/shard_map/ppermute | solution.py:287
  60.5 1.0 collective-permute-done.4.other_ref
  61.6 1.0 collective-permute-start.7
  63.1 1.7 %collective-permute-start.5 = (bf16[72,512]{1,0:T(8,128)(2,1)S(1)}, bf16[72,512]{1,0:T(8,128)(2,1)S(1)}, u32[]{:S(2)}, u32[]{:S(2)}) collective-permute-start(bf16[72,512]{1,0:T(8,128)(2,1)S(1)} %shard_map.101.p0_ref), channel_id=1, source_target_pairs={{0,32},{16,48},{32,0},{48,16},{64,96},{80,112},{96,64},{112,80},{1... | collective-permute-start | bytes 221192 | tf_op jit(solution)/shard_map/ppermute | solution.py:287
  64.9 2.2 %shard_map.102.far_ref = bf16[2,4096,512]{2,1,0:T(8,128)(2,1)S(1)} custom-call(bf16[2,512,4096]{2,1,0:T(8,128)(2,1)S(1)} %bitcast.18), custom_call_target="tpu_custom_call" | custom-call | tf_op jit(solution)/shard_map/pallas_call | solution.py:40
  68.2 2.6 %shard_map.103 = (bf16[16,8,1536]{2,1,0:T(8,128)(2,1)S(1)}, f32[64,512]{1,0:T(8,128)S(1)}, f32[64,512]{1,0:T(8,128)S(1)}, f32[8,128]{1,0:T(8,128)S(1)}, bf16[8,1024]{1,0:T(8,128)(2,1)S(1)}) custom-call(bf16[72,512]{1,0:T(8,128)(2,1)S(1)} %shard_map.101.p0_ref, bf16[72,512]{1,0:T(8,128)(2,1)S(1)} %collective-permute-done.5.p2_ref, ...), custom_call_target="tpu_custom_call" | custom-call | tf_op jit(solution)/shard_map/pallas_call | solution.py:40
  70.7 11.1 %all_to_all.28.in_ref = bf16[16,8,1536]{2,1,0:T(8,128)(2,1)S(1)} all-to-all(bf16[16,8,1536]{2,1,0:T(8,128)(2,1)S(1)} %get-tuple-element.71), channel_id=1, replica_groups=mesh['row'=8,'col'=16] {'col'}, dimensions={0} | all-to-all | bytes 786432 | tf_op jit(solution)/shard_map/all_to_all | solution.py:305
  81.8 2.2 %shard_map.104 = (f32[8,512]{1,0:T(8,128)S(1)}, f32[8,128]{1,0:T(8,128)S(1)}, f32[128,1,128]{2,1,0:T(1,128)}, bf16[4,8,1024]{2,1,0:T(8,128)(2,1)S(1)}, bf16[4,8,1024]{2,1,0:T(8,128)(2,1)S(1)}) custom-call(s32[16]{0:T(128)S(1)} %shard_map.97.slot_ref, bf16[8,1024]{1,0:T(8,128)(2,1)S(1)} %get-tuple-element.70.even_ref, ...), custom_call_target="tpu_custom_call" | custom-call | tf_op jit(solution)/shard_map/pallas_call | solution.py:40
  84.0 3.0 %collective-permute-start.8 = (bf16[4,8,1024]{2,1,0:T(8,128)(2,1)S(1)}, bf16[4,8,1024]{2,1,0:T(8,128)(2,1)S(1)}, u32[]{:S(2)}, u32[]{:S(2)}) collective-permute-start(bf16[4,8,1024]{2,1,0:T(8,128)(2,1)S(1)} %get-tuple-element.80), channel_id=1, source_target_pairs={{0,16},{16,0},{32,48},{48,32},{64,80},{80,64},{96,112},{112,96},{1... | collective-permute-start | bytes 196616 | tf_op jit(solution)/shard_map/ppermute | solution.py:287
  87.3 5.0 %all-to-all-start.4 = ((f32[128,1,128]{2,1,0:T(1,128)}), f32[128,1,128]{2,1,0:T(1,128)S(1)}, u32[]{:S(2)}, u32[]{:S(2)}) async-start(f32[128,1,128]{2,1,0:T(1,128)} %get-tuple-element.72), calls=%async_computation.4 | async-start | bytes 131072 | tf_op jit(solution)/shard_map/all_to_all | solution.py:372
  92.3 3.3 %collective-permute-start.11 = (bf16[8,1024]{1,0:T(8,128)(2,1)S(1)}, bf16[8,1024]{1,0:T(8,128)(2,1)S(1)}, u32[]{:S(2)}, u32[]{:S(2)}) collective-permute-start(bf16[8,1024]{1,0:T(8,128)(2,1)S(1)} %get-tuple-element.81), channel_id=1, source_target_pairs={{0,96},{16,112},{32,64},{48,80},{64,32},{80,48},{96,0},{112,16},{1... | collective-permute-start | bytes 49160 | tf_op jit(solution)/shard_map/ppermute | solution.py:287
  96.3 5.5 %all-to-all-done.4.norm_ref = f32[128,1,128]{2,1,0:T(1,128)S(1)} async-done(((f32[128,1,128]{2,1,0:T(1,128)}), f32[128,1,128]{2,1,0:T(1,128)S(1)}, u32[]{:S(2)}, u32[]{:S(2)}) %all-to-all-start.4) | async-done | bytes 65568 | tf_op jit(solution)/shard_map/all_to_all | solution.py:372
  (39 shorter events, 6.1 us)
Async XLA Ops:
  0.6 18.1 %copy-start = (s32[16,8]{0,1:T(8,128)S(1)}, s32[16,8]{0,1:T(8,128)}, u32[]{:S(2)}) copy-start(s32[16,8]{0,1:T(8,128)} %param.10) | copy-start | bytes 1540
  0.6 18.1 %copy-start.1 = (bf16[16,8,48,512]{3,2,1,0:T(8,128)(2,1)S(1)}, bf16[16,8,48,512]{3,2,1,0:T(8,128)(2,1)}, u32[]{:S(2)}) copy-start(bf16[16,8,48,512]{3,2,1,0:T(8,128)(2,1)} %param.9) | copy-start | bytes 18874372
  20.0 3.1 %collective-permute-start = (f32[64,512]{1,0:T(8,128)S(1)}, f32[64,512]{1,0:T(8,128)S(1)}, u32[]{:S(2)}, u32[]{:S(2)}) collective-permute-start(f32[64,512]{1,0:T(8,128)S(1)} %shard_map.95), channel_id=1, source_target_pairs={{0,16},{16,0},{32,48},{48,32},{64,80},{80,64},{96,112},{112,96},{1... | collective-permute-start | bytes 393224 | tf_op jit(solution)/shard_map/ppermute | solution.py:287
  23.1 6.4 %copy-start.3 = (s32[16,16]{1,0:T(8,128)S(1)}, s32[16,16]{1,0:T(8,128)}, u32[]{:S(2)}) copy-start(s32[16,16]{1,0:T(8,128)} %target_ref) | copy-start | bytes 3076
  23.1 6.4 %copy-start.4 = (s32[128]{0:T(128)S(1)}, s32[128]{0:T(128)}, u32[]{:S(2)}) copy-start(s32[128]{0:T(128)} %order_ref) | copy-start | bytes 1540
  23.2 7.7 %collective-permute-start.3 = (bf16[64,512]{1,0:T(8,128)(2,1)S(1)}, bf16[64,512]{1,0:T(8,128)(2,1)S(1)}, u32[]{:S(2)}, u32[]{:S(2)}) collective-permute-start(bf16[64,512]{1,0:T(8,128)(2,1)S(1)} %add_convert_fusion.p0_ref), channel_id=1, source_target_pairs={{0,96},{16,112},{32,64},{48,80},{64,32},{80,48},{96,0},{112,16},{1... | collective-permute-start | bytes 196616 | tf_op jit(solution)/shard_map/ppermute | solution.py:287
  27.0 4.6 %collective-permute-start.2 = (bf16[64,512]{1,0:T(8,128)(2,1)S(1)}, bf16[64,512]{1,0:T(8,128)(2,1)S(1)}, u32[]{:S(2)}, u32[]{:S(2)}) collective-permute-start(bf16[64,512]{1,0:T(8,128)(2,1)S(1)} %add_convert_fusion.p0_ref), channel_id=1, source_target_pairs={{0,64},{16,80},{32,96},{48,112},{64,0},{80,16},{96,32},{112,48},{1... | collective-permute-start | bytes 196616 | tf_op jit(solution)/shard_map/ppermute | solution.py:287
  27.0 4.6 %collective-permute-start.1 = (bf16[64,512]{1,0:T(8,128)(2,1)S(1)}, bf16[64,512]{1,0:T(8,128)(2,1)S(1)}, u32[]{:S(2)}, u32[]{:S(2)}) collective-permute-start(bf16[64,512]{1,0:T(8,128)(2,1)S(1)} %add_convert_fusion.p0_ref), channel_id=1, source_target_pairs={{0,32},{16,48},{32,0},{48,16},{64,96},{80,112},{96,64},{112,80},{1... | collective-permute-start | bytes 196616 | tf_op jit(solution)/shard_map/ppermute | solution.py:287
  42.6 22.3 %slice-start = ((s8[8388608]{0:T(1024)(128)(4,1)}), s8[4194304]{0:T(1024)(128)(4,1)S(1)}, s32[]{:S(2)}) async-start(s8[8388608]{0:T(1024)(128)(4,1)} %bitcast.17), calls=%async_computation.5 | async-start | bytes 8388608
  42.6 22.3 %slice-start.1 = ((s8[8388608]{0:T(1024)(128)(4,1)}), s8[4194304]{0:T(1024)(128)(4,1)S(1)}, s32[]{:S(2)}) async-start(s8[8388608]{0:T(1024)(128)(4,1)} %bitcast.17), calls=%async_computation.6 | async-start | bytes 8388608
  55.8 5.7 %collective-permute-start.4 = (f32[72,512]{1,0:T(8,128)S(1)}, f32[72,512]{1,0:T(8,128)S(1)}, u32[]{:S(2)}, u32[]{:S(2)}) collective-permute-start(f32[72,512]{1,0:T(8,128)S(1)} %shard_map.100.own_ref), channel_id=1, source_target_pairs={{0,16},{16,0},{32,48},{48,32},{64,80},{80,64},{96,112},{112,96},{1... | collective-permute-start | bytes 442376 | tf_op jit(solution)/shard_map/ppermute | solution.py:287
  61.6 5.5 %collective-permute-start.7 = (bf16[72,512]{1,0:T(8,128)(2,1)S(1)}, bf16[72,512]{1,0:T(8,128)(2,1)S(1)}, u32[]{:S(2)}, u32[]{:S(2)}) collective-permute-start(bf16[72,512]{1,0:T(8,128)(2,1)S(1)} %shard_map.101.p0_ref), channel_id=1, source_target_pairs={{0,96},{16,112},{32,64},{48,80},{64,32},{80,48},{96,0},{112,16},{1... | collective-permute-start | bytes 221192 | tf_op jit(solution)/shard_map/ppermute | solution.py:287
  62.6 4.8 %collective-permute-start.6 = (bf16[72,512]{1,0:T(8,128)(2,1)S(1)}, bf16[72,512]{1,0:T(8,128)(2,1)S(1)}, u32[]{:S(2)}, u32[]{:S(2)}) collective-permute-start(bf16[72,512]{1,0:T(8,128)(2,1)S(1)} %shard_map.101.p0_ref), channel_id=1, source_target_pairs={{0,64},{16,80},{32,96},{48,112},{64,0},{80,16},{96,32},{112,48},{1... | collective-permute-start | bytes 221192 | tf_op jit(solution)/shard_map/ppermute | solution.py:287
  63.1 5.0 %collective-permute-start.5 = (bf16[72,512]{1,0:T(8,128)(2,1)S(1)}, bf16[72,512]{1,0:T(8,128)(2,1)S(1)}, u32[]{:S(2)}, u32[]{:S(2)}) collective-permute-start(bf16[72,512]{1,0:T(8,128)(2,1)S(1)} %shard_map.101.p0_ref), channel_id=1, source_target_pairs={{0,32},{16,48},{32,0},{48,16},{64,96},{80,112},{96,64},{112,80},{1... | collective-permute-start | bytes 221192 | tf_op jit(solution)/shard_map/ppermute | solution.py:287
  70.7 31.1 %copy-start.2 = (f32[8,512]{1,0:T(8,128)S(1)}, f32[8,512]{1,0:T(8,128)}, u32[]{:S(2)}) copy-start(f32[8,512]{1,0:T(8,128)} %res_ref.1) | copy-start | bytes 49156
  84.0 8.3 %collective-permute-start.8 = (bf16[4,8,1024]{2,1,0:T(8,128)(2,1)S(1)}, bf16[4,8,1024]{2,1,0:T(8,128)(2,1)S(1)}, u32[]{:S(2)}, u32[]{:S(2)}) collective-permute-start(bf16[4,8,1024]{2,1,0:T(8,128)(2,1)S(1)} %get-tuple-element.80), channel_id=1, source_target_pairs={{0,16},{16,0},{32,48},{48,32},{64,80},{80,64},{96,112},{112,96},{1... | collective-permute-start | bytes 196616 | tf_op jit(solution)/shard_map/ppermute | solution.py:287
  87.0 9.3 %collective-permute-start.12 = (bf16[8,1024]{1,0:T(8,128)(2,1)S(1)}, bf16[8,1024]{1,0:T(8,128)(2,1)S(1)}, u32[]{:S(2)}, u32[]{:S(2)}) collective-permute-start(bf16[8,1024]{1,0:T(8,128)(2,1)S(1)} %get-tuple-element.70.even_ref), channel_id=1, source_target_pairs={{0,1},{1,0},{2,3},{3,2},{4,5},{5,4},{6,7},{7,6},{8,9},{9,8},{10,11... | collective-permute-start | bytes 49160 | tf_op jit(solution)/shard_map/ppermute | solution.py:375
  87.3 14.5 %all-to-all-start.4 = ((f32[128,1,128]{2,1,0:T(1,128)}), f32[128,1,128]{2,1,0:T(1,128)S(1)}, u32[]{:S(2)}, u32[]{:S(2)}) async-start(f32[128,1,128]{2,1,0:T(1,128)} %get-tuple-element.72), calls=%async_computation.4 | async-start | bytes 131072 | tf_op jit(solution)/shard_map/all_to_all | solution.py:372
  92.3 9.5 %collective-permute-start.11 = (bf16[8,1024]{1,0:T(8,128)(2,1)S(1)}, bf16[8,1024]{1,0:T(8,128)(2,1)S(1)}, u32[]{:S(2)}, u32[]{:S(2)}) collective-permute-start(bf16[8,1024]{1,0:T(8,128)(2,1)S(1)} %get-tuple-element.81), channel_id=1, source_target_pairs={{0,96},{16,112},{32,64},{48,80},{64,32},{80,48},{96,0},{112,16},{1... | collective-permute-start | bytes 49160 | tf_op jit(solution)/shard_map/ppermute | solution.py:287
  95.7 6.2 %collective-permute-start.10 = (bf16[8,1024]{1,0:T(8,128)(2,1)S(1)}, bf16[8,1024]{1,0:T(8,128)(2,1)S(1)}, u32[]{:S(2)}, u32[]{:S(2)}) collective-permute-start(bf16[8,1024]{1,0:T(8,128)(2,1)S(1)} %get-tuple-element.82), channel_id=1, source_target_pairs={{0,64},{16,80},{32,96},{48,112},{64,0},{80,16},{96,32},{112,48},{1... | collective-permute-start | bytes 49160 | tf_op jit(solution)/shard_map/ppermute | solution.py:287
  95.8 6.1 %collective-permute-start.9 = (bf16[8,1024]{1,0:T(8,128)(2,1)S(1)}, bf16[8,1024]{1,0:T(8,128)(2,1)S(1)}, u32[]{:S(2)}, u32[]{:S(2)}) collective-permute-start(bf16[8,1024]{1,0:T(8,128)(2,1)S(1)} %get-tuple-element.83), channel_id=1, source_target_pairs={{0,32},{16,48},{32,0},{48,16},{64,96},{80,112},{96,64},{112,80},{1... | collective-permute-start | bytes 49160 | tf_op jit(solution)/shard_map/ppermute | solution.py:287
